TPU v7x, 256 devices: a whole 4x4x8 slice. The times are simulated.
256 devices in a mesh: rows: 64 (over x_lo, y, z), cols: 4 (over x_hi, core).
Axes of the slice: x: 4 (x_hi: 2, x_lo: 2; x = x_hi * 2 + x_lo), y: 4, z: 8, core: 2. Of those that a mesh axis runs over, the one named last changes fastest.
Arguments:
- l_blocks: bfloat16 [2048, 64, 1920], P(('rows', 'cols')), may hold values from -0.25 to 0.25
- s_blocks: bfloat16 [2048, 64, 1280], P('rows', None, 'cols'), may hold values from -6 to 6
- l_index: int32 [2048, 30], P(('rows', 'cols')), may hold values from 0 to 2047, as said below
- s_cols: int32 [2048, 20], replicated, may hold values from 0 to 2047, as said below
- c_index: int32 [2048, 24], P(('rows', 'cols')), may hold values from 0 to 2047, as said below
Outputs:
- product: bfloat16 [2048, 64, 1536], P(('rows', 'cols'))
Inputs may be any that keep to these rules, and one draw needn't show every extreme that they name: `l_index`: the 30 entries of block-row i are distinct and lie in the window of 31 block-rows starting at max(0, min(i - 15, 2017)). `s_cols`: the entries of one block-row are distinct; those in slots p * 5 to (p + 1) * 5 - 1 are congruent to p modulo 20 // 5 and lie within 7 such columns around the block-row. `c_index`: the entries of one block-row are distinct; those in slots p * 6 to (p + 1) * 6 - 1 are congruent to p modulo 24 // 6 and lie within 16 such columns around the block-row.
All inputs are finite; a program needn't handle non-finite values.
Results may differ from a plain program's by a relative error of at most 0.001.
Values may be sent and summed in bfloat16 or wider, within the bound.
No kernel may reach another device: no remote copies, remote signals or barrier semaphores. Data moves between devices by JAX's collectives and lax.ppermute only.
A program may use at most 192 MiB of HBM per device.

v0:
```python
import math

import jax
import jax.numpy as jnp
from jax import lax
from jax.sharding import PartitionSpec as P

HL = 15


def padded(block, sides, width):
    for axis, dim in sides:
        count = lax.axis_size(axis)
        forward = [(i, i + 1) for i in range(count - 1)]
        backward = [(target, source) for source, target in forward]
        low = lax.ppermute(
            lax.slice_in_dim(block, block.shape[dim] - width, None, axis=dim), axis, forward
        )
        high = lax.ppermute(lax.slice_in_dim(block, 0, width, axis=dim), axis, backward)
        block = jnp.concatenate([low, block, high], axis=dim)
    return block


def row_products(l_rows, l_ids, want_index, s_near, slot_cols, first):
    total = l_rows.shape[0]
    width = l_rows.shape[1]
    slot_total = s_near.shape[2] // width
    kept = want_index.shape[1]
    s_four = s_near.reshape(s_near.shape[0], width, slot_total, width)
    s_four = jnp.concatenate(
        [s_four, jnp.zeros((s_four.shape[0], width, 1, width), s_four.dtype)], axis=2
    )
    per_turn = math.gcd(total, max(1, 96 // kept))

    def single(left_row, left_ids, want_cols):
        slot_ids = jnp.take(slot_cols, left_ids, axis=0)
        match = slot_ids[:, None, :] == want_cols[None, :, None]
        slot_pick = jnp.sum(
            jnp.where(match, lax.iota(jnp.int32, slot_total)[None, None, :], 0),
            axis=2,
            dtype=jnp.int32,
        )
        found = jnp.any(match, axis=2)
        slot_pick = jnp.where(found, slot_pick, slot_total)
        local_ids = left_ids - first
        picked = s_four[local_ids[:, None], :, slot_pick, :]
        left_three = left_row.reshape(width, left_ids.shape[0], width)
        summed = jnp.einsum("akb,kmbc->amc", left_three, picked, preferred_element_type=jnp.float32)
        return summed.reshape(width, kept * width).astype(jnp.bfloat16)

    def one_group(group):
        return jax.vmap(single)(group[0], group[1], group[2])

    shaped = tuple(
        (
            a.reshape((total // per_turn, per_turn) + a.shape[1:])
            for a in (l_rows, l_ids, want_index)
        )
    )
    result = lax.map(one_group, shaped)
    return result.reshape((total,) + result.shape[2:])


def shards(l_blocks, s_blocks, l_index, s_cols, c_index):
    row_here = lax.axis_index("rows")
    group_size = s_blocks.shape[0]
    group_first = row_here * group_size
    whole = lax.all_gather(s_blocks, "cols", axis=2, tiled=True)
    nearby = padded(whole, (("rows", 0),), HL)
    return row_products(l_blocks, l_index, c_index, nearby, s_cols, group_first - HL)


def solution(mesh):
    return jax.shard_map(
        shards,
        mesh=mesh,
        in_specs=(
            P(("rows", "cols"), None, None),
            P("rows", None, "cols"),
            P(("rows", "cols"), None),
            P(),
            P(("rows", "cols"), None),
        ),
        out_specs=P(("rows", "cols"), None, None),
        check_vma=False,
    )
```

profile of v0, /device:TPU:3, one launch (start us, length us, event | category | flops | bytes accessed | tf_op | source)
XLA Modules:
  0.0 385.7 jit_solution(16272070342322603991)
XLA Ops:
  6.5 5.9 %copy.44 = bf16[32,64,320]{1,0,2:T(8,128)(2,1)} copy(bf16[32,64,320]{2,1,0:T(8,128)(2,1)} %param.8) | data formatting | bytes 2621440 | tf_op args[1]
  12.5 79.4 %all-gather.2.cloned.1.call-done = bf16[32,64,1280]{1,0,2:T(8,128)(2,1)} async-done(((bf16[32,64,320]{1,0,2:T(8,128)(2,1)}), bf16[32,64,1280]{1,0,2:T(8,128)(2,1)}) %all-gather.2.cloned.1.call-update) | async-done | bytes 5242896 | tf_op jit(solution)/shard_map/all_gather | solution.py:68
  91.9 9.8 %fusion.13 = (bf16[15,64,1280]{1,0,2:T(8,128)(2,1)}, bf16[15,64,1280]{1,0,2:T(8,128)(2,1)}) fusion(bf16[32,64,1280]{1,0,2:T(8,128)(2,1)} %all-gather.2.cloned.1.call-done), kind=kLoop, calls=%fused_computation.26 | loop fusion | bytes 9830400 | tf_op jit(solution)/shard_map/slice | solution.py:17
  101.7 7.1 %copy.45 = bf16[15,64,1280]{2,1,0:T(8,128)(2,1)} copy(bf16[15,64,1280]{1,0,2:T(8,128)(2,1)} %get-tuple-element.104) | data formatting | bytes 4915200 | tf_op jit(solution)/shard_map/slice | solution.py:17
  108.8 3.2 collective-permute-start
  112.0 7.1 %copy.46 = bf16[15,64,1280]{2,1,0:T(8,128)(2,1)} copy(bf16[15,64,1280]{1,0,2:T(8,128)(2,1)} %get-tuple-element.105) | data formatting | bytes 4915200 | tf_op jit(solution)/shard_map/slice | solution.py:19
  119.1 6.9 %collective-permute-start.1 = (bf16[15,64,1280]{2,1,0:T(8,128)(2,1)}, bf16[15,64,1280]{2,1,0:T(8,128)(2,1)}, u32[]{:S(2)}, u32[]{:S(2)}) collective-permute-start(bf16[15,64,1280]{2,1,0:T(8,128)(2,1)} %copy.46), channel_id=1, source_target_pairs={{4,0},{8,4},{12,8},{16,12},{20,16},{24,20},{28,24},{32,28},{36,32}... | collective-permute-start | bytes 7372808 | tf_op jit(solution)/shard_map/ppermute | solution.py:19
  126.0 1.4 copy.48
  127.4 12.7 %copy.47 = bf16[32,64,1280]{2,1,0:T(8,128)(2,1)} copy(bf16[32,64,1280]{1,0,2:T(8,128)(2,1)} %all-gather.2.cloned.1.call-done) | data formatting | bytes 10485760 | tf_op jit(solution)/shard_map/all_gather | solution.py:68
  140.0 30.5 %collective-permute-done = bf16[15,64,1280]{2,1,0:T(8,128)(2,1)S(1)} collective-permute-done((bf16[15,64,1280]{2,1,0:T(8,128)(2,1)}, bf16[15,64,1280]{2,1,0:T(8,128)(2,1)S(1)}, u32[]{:S(2)}, u32[]{:S(2)}) %collective-permute-start) | collective-permute-done | bytes 2457632 | tf_op jit(solution)/shard_map/ppermute | solution.py:16
  170.5 8.1 %collective-permute-done.1 = bf16[15,64,1280]{2,1,0:T(8,128)(2,1)} collective-permute-done((bf16[15,64,1280]{2,1,0:T(8,128)(2,1)}, bf16[15,64,1280]{2,1,0:T(8,128)(2,1)}, u32[]{:S(2)}, u32[]{:S(2)}) %collective-permute-start.1) | collective-permute-done | bytes 2457632 | tf_op jit(solution)/shard_map/ppermute | solution.py:19
  178.6 8.8 %pad_maximum_fusion = bf16[62,64,1280]{2,1,0:T(8,128)(2,1)} fusion(bf16[15,64,1280]{2,1,0:T(8,128)(2,1)} %collective-permute-done.1, bf16[32,64,1280]{2,1,0:T(8,128)(2,1)} %copy.47, bf16[15,64,1280]{2,1,0:T(8,128)(2,1)S(1)} %collective-permute-done), kind=kLoop, calls=%fused_computation.25 | loop fusion | flops 10158080 | bytes 20316160 | tf_op jit(solution)/shard_map/concatenate | solution.py:20
  187.5 29.2 %reshape.109 = bf16[62,64,20,64]{3,2,1,0:T(8,128)(2,1)} reshape(bf16[62,64,1280]{2,1,0:T(8,128)(2,1)} %pad_maximum_fusion) | data formatting | bytes 20316160 | tf_op jit(solution)/shard_map/reshape | solution.py:29
  216.6 12.8 %copy.54 = bf16[62,64,20,64]{3,1,2,0:T(8,128)(2,1)S(1)} copy(bf16[62,64,20,64]{3,2,1,0:T(8,128)(2,1)} %reshape.109) | data formatting | bytes 20316160
  229.4 11.0 %concatenate.10.clone = bf16[62,64,21,64]{3,1,2,0:T(8,128)(2,1)} pad(bf16[62,64,20,64]{3,1,2,0:T(8,128)(2,1)S(1)} %copy.54, bf16[]{:T(256)} %constant.33.clone.1), padding=0_0x0_0x0_1x0_0 | pad | bytes 20824066 | tf_op jit(solution)/shard_map/concatenate | solution.py:30
  240.4 138.4 %while.10 = (s32[]{:T(128)}, bf16[2,4,64,1536]{3,2,1,0:T(8,128)(2,1)}, bf16[2,4,64,1920]{3,2,1,0:T(8,128)(2,1)}, s32[2,4,30]{2,1,0:T(4,128)S(1)}, s32[]{:T(128)}...) while((s32[]{:T(128)}, ...), condition=%wide.region_3.4_spmd, body=%wide.region_0.3_spmd.sunk | while | flops 1510650240 | bytes 81435040 | solution.py:60
  240.5 1.9 gather_fusion
  243.3 39.2 %gather_fusion.1 = bf16[2880,64,64]{2,1,0:T(8,128)(2,1)} fusion(bf16[62,64,21,64]{3,1,2,0:T(8,128)(2,1)} %get-tuple-element.180, s32[2880]{0:T(1024)S(1)} %reshape.142), kind=kCustom, calls=%fused_computation.1.clone.1 | custom fusion | bytes 47208960 | tf_op jit(solution)/shard_map/while/body/eval_jaxpr/vmap()/gather | solution.py:46
  282.5 1.3 constant_dynamic-slice_fusion.2
  283.8 2.1 reshape.143
  285.9 19.4 %bitcast_convert_fusion.2 = bf16[4,64,24,64]{3,1,2,0:T(8,128)(2,1)} fusion(bf16[4,30,24,64,64]{4,3,2,1,0:T(8,128)(2,1)} %bitcast.48, bf16[4,64,30,64,1]{3,2,1,0,4:T(8,128)(2,1)S(1)} %bitcast.49), kind=kOutput, calls=%fused_computation.4.clone.1 | convolution fusion | flops 1510342656 | bytes 25362432 | tf_op jit(solution)/shard_map/while/body/eval_jaxpr/vmap(akb,kmbc->amc)/dot_general | solution.py:48
  305.3 2.4 copy.74
  307.7 1.0 convert_element_type.17
  308.7 0.9 constant_dynamic-update-slice_fusion.2
  309.7 1.9 gather_fusion
  312.5 39.2 %gather_fusion.1 = bf16[2880,64,64]{2,1,0:T(8,128)(2,1)} fusion(bf16[62,64,21,64]{3,1,2,0:T(8,128)(2,1)} %get-tuple-element.180, s32[2880]{0:T(1024)S(1)} %reshape.142), kind=kCustom, calls=%fused_computation.1.clone.1 | custom fusion | bytes 47208960 | tf_op jit(solution)/shard_map/while/body/eval_jaxpr/vmap()/gather | solution.py:46
  351.7 1.3 constant_dynamic-slice_fusion.2
  353.0 2.1 reshape.143
  355.1 19.4 %bitcast_convert_fusion.2 = bf16[4,64,24,64]{3,1,2,0:T(8,128)(2,1)} fusion(bf16[4,30,24,64,64]{4,3,2,1,0:T(8,128)(2,1)} %bitcast.48, bf16[4,64,30,64,1]{3,2,1,0,4:T(8,128)(2,1)S(1)} %bitcast.49), kind=kOutput, calls=%fused_computation.4.clone.1 | convolution fusion | flops 1510342656 | bytes 25362432 | tf_op jit(solution)/shard_map/while/body/eval_jaxpr/vmap(akb,kmbc->amc)/dot_general | solution.py:48
  374.5 2.4 copy.74
  376.9 1.0 convert_element_type.17
  377.9 0.9 constant_dynamic-update-slice_fusion.2
  (39 shorter events, 1.9 us)
Async XLA Ops:
  6.5 85.3 %all-gather.2.cloned.1.call-start = ((), (), s32[]{:S(2)}) async-start(), calls=%async_computation | async-start | bytes 13107200 | tf_op jit(solution)/shard_map/all_gather | solution.py:68
  108.8 61.8 %collective-permute-start = (bf16[15,64,1280]{2,1,0:T(8,128)(2,1)}, bf16[15,64,1280]{2,1,0:T(8,128)(2,1)S(1)}, u32[]{:S(2)}, u32[]{:S(2)}) collective-permute-start(bf16[15,64,1280]{2,1,0:T(8,128)(2,1)} %copy.45), channel_id=1, source_target_pairs={{0,4},{4,8},{8,12},{12,16},{16,20},{20,24},{24,28},{28,32},{32,36}... | collective-permute-start | bytes 7372808 | tf_op jit(solution)/shard_map/ppermute | solution.py:16
  111.9 14.1 %copy-start.1 = (s32[2048,20]{0,1:T(8,128)S(1)}, s32[2048,20]{0,1:T(8,128)}, u32[]{:S(2)}) copy-start(s32[2048,20]{0,1:T(8,128)} %param.10) | copy-start | bytes 491524
  119.1 59.5 %collective-permute-start.1 = (bf16[15,64,1280]{2,1,0:T(8,128)(2,1)}, bf16[15,64,1280]{2,1,0:T(8,128)(2,1)}, u32[]{:S(2)}, u32[]{:S(2)}) collective-permute-start(bf16[15,64,1280]{2,1,0:T(8,128)(2,1)} %copy.46), channel_id=1, source_target_pairs={{4,0},{8,4},{12,8},{16,12},{20,16},{24,20},{28,24},{32,28},{36,32}... | collective-permute-start | bytes 7372808 | tf_op jit(solution)/shard_map/ppermute | solution.py:19
  229.4 11.0 %copy-start = (s32[8,30]{1,0:T(8,128)S(1)}, s32[8,30]{1,0:T(8,128)}, u32[]{:S(2)}) copy-start(s32[8,30]{1,0:T(8,128)} %param.9) | copy-start | bytes 2884
  229.4 11.0 %copy-start.2 = (s32[8,24]{1,0:T(8,128)S(1)}, s32[8,24]{1,0:T(8,128)}, u32[]{:S(2)}) copy-start(s32[8,24]{1,0:T(8,128)} %param.11) | copy-start | bytes 2308
Sparse Core Ops, SparseCore 0:
  12.6 79.2 all-gather.1
where the time goes:
time: 388 us; the launch traced here: 386 us
  local copies, waits for them, and re-layouts  195 us (50%)
  waiting for transfers between devices  118 us (30%)
  matrix products  38.7 us (10%)
  between operations  13.5 us (3%)
  starting transfers between devices  10.1 us (3%)
  other arithmetic  9.79 us (3%)
    all_gather x1, waiting for transfers between devices, shards(): whole = lax.all_gather(s_blocks, 'cols', axis=2, tiled=True)  79.4 us
    gather x2, local copies, waits for them, and re-layouts, single(): picked = s_four[local_ids[:, None], :, slot_pick, :]  78.4 us
    dot_general x2, matrix products, single(): jnp.einsum('akb,kmbc->amc', left_three, picked, preferred_element_type=jn...  38.7 us
    ppermute x1, waiting for transfers between devices, padded(): lax.ppermute(lax.slice_in_dim(block, block.shape[dim] - width, None, axis...  30.5 us
    reshape x1, local copies, waits for them, and re-layouts, row_products(): s_four = s_near.reshape(s_near.shape[0], width, slot_total, width)  29.2 us
    unnamed x8, local copies, waits for them, and re-layouts  18.7 us
    slice x2, local copies, waits for them, and re-layouts, padded(): lax.slice_in_dim(block, block.shape[dim] - width, None, axis=dim)  16.9 us
    all_gather x1, local copies, waits for them, and re-layouts, shards(): whole = lax.all_gather(s_blocks, 'cols', axis=2, tiled=True)  12.7 us
  transfers between devices with their start and end apart: 3, of which 3 were waited for; matrix products, arithmetic and copies ran while one was open for 5% of the time, Pallas kernels for 0%

commit v1 on v0

v1 whole, which is shorter than its diff:
```python
import functools

import jax
import jax.numpy as jnp
from jax import lax
from jax.experimental import pallas as pl
from jax.experimental.pallas import tpu as pltpu
from jax.sharding import PartitionSpec as P

HALF = 16
TILES = 40
ZERO = 6 * TILES


def pack_body(start_ref, s_ref, first_ref, second_ref):
    def one(out_ref, base):
        def row(j, carry):
            for t in range(2):
                out_ref[2 * j + t] = s_ref[base + j, :, 128 * t : 128 * t + 128]
            return carry

        lax.fori_loop(0, HALF, row, 0, unroll=4)

        def pair(j, carry):
            out_ref[32 + j] = jnp.concatenate(
                [s_ref[base + 2 * j, :, 256:320], s_ref[base + 2 * j + 1, :, 256:320]], axis=1
            )
            return carry

        lax.fori_loop(0, HALF // 2, pair, 0, unroll=4)

    h = start_ref[0]
    one(first_ref, HALF * h)
    one(second_ref, HALF * (1 - h))


def pack(h, s_blocks):
    piece = jax.ShapeDtypeStruct((TILES, 64, 128), jnp.bfloat16)
    return pl.pallas_call(
        pack_body,
        out_shape=(piece, piece),
        in_specs=[
            pl.BlockSpec(memory_space=pltpu.SMEM),
            pl.BlockSpec(memory_space=pltpu.VMEM),
        ],
        out_specs=(
            pl.BlockSpec(memory_space=pltpu.VMEM),
            pl.BlockSpec(memory_space=pltpu.VMEM),
        ),
        compiler_params=pltpu.CompilerParams(vmem_limit_bytes=16 << 20),
        cost_estimate=pl.CostEstimate(flops=0, bytes_accessed=3 << 20, transcendentals=0),
    )(h, s_blocks)


def product_body(tab_ref, part_ref, l_ref, a_ref, b_ref, c_ref, *rest):
    o_ref, sd_ref, pk_ref = rest[-3:]
    i = pl.program_id(0)

    @pl.when(i == 0)
    def _():
        for n, piece in enumerate((a_ref, b_ref, c_ref)):

            def spread(t, carry, piece=piece, n=n):
                v = piece[t]
                lo, hi = v[:, :64], v[:, 64:]
                sd_ref[2 * TILES * n + 2 * t] = jnp.concatenate([lo, lo], axis=1)
                sd_ref[2 * TILES * n + 2 * t + 1] = jnp.concatenate([hi, hi], axis=1)
                return carry

            lax.fori_loop(0, TILES, spread, 0, unroll=4)
        sd_ref[ZERO] = jnp.zeros((64, 128), jnp.bfloat16)

    base = part_ref[0] * 6
    low = lax.broadcasted_iota(jnp.int32, (64, 128), 1) < 64

    def lay(k, carry):
        row = i * 30 + k
        for m in range(3):
            x = sd_ref[tab_ref[row, base + 2 * m]]
            y = sd_ref[tab_ref[row, base + 2 * m + 1]]
            pk_ref[pl.ds(k * 64, 64), 128 * m : 128 * m + 128] = jnp.where(low, x, y)
        return carry

    lax.fori_loop(0, 30, lay, 0, unroll=6)
    o_ref[0] = jnp.dot(
        l_ref[0], pk_ref[...], preferred_element_type=jnp.float32
    ).astype(o_ref.dtype)


def product(tab, part, l_blocks, pieces, prev):
    rows = l_blocks.shape[0]
    whole = pl.BlockSpec((TILES, 64, 128), lambda i, t, p: (0, 0, 0), pipeline_mode=pl.Buffered(1))
    in_specs = [pl.BlockSpec((1, 64, 1920), lambda i, t, p: (i, 0, 0)), whole, whole, whole]
    args = [tab, part, l_blocks, *pieces]
    aliases = {}
    if prev is not None:
        in_specs.append(pl.BlockSpec(memory_space=pl.ANY))
        aliases = {len(args): 0}
        args.append(prev)
    return pl.pallas_call(
        product_body,
        out_shape=jax.ShapeDtypeStruct((rows, 64, 1536), jnp.bfloat16),
        grid_spec=pltpu.PrefetchScalarGridSpec(
            num_scalar_prefetch=2,
            grid=(rows,),
            in_specs=in_specs,
            out_specs=pl.BlockSpec((1, 64, 384), lambda i, t, p: (i, 0, p[0])),
            scratch_shapes=[
                pltpu.VMEM((ZERO + 1, 64, 128), jnp.bfloat16),
                pltpu.VMEM((1920, 384), jnp.bfloat16),
            ],
        ),
        input_output_aliases=aliases,
        compiler_params=pltpu.CompilerParams(vmem_limit_bytes=24 << 20),
        cost_estimate=pl.CostEstimate(flops=755_000_000, bytes_accessed=4 << 20, transcendentals=0),
    )(*args)


def table(h, r, l_index, s_cols, c_index):
    total = s_cols.shape[0]
    rows, terms = l_index.shape
    kept = c_index.shape[1]
    near = 4 * HALF
    w0 = jnp.clip(32 * r - HALF, 0, total - near)
    window = lax.dynamic_slice_in_dim(s_cols, w0, near, axis=0).astype(jnp.float32)
    lane = lax.broadcasted_iota(jnp.int32, (20, 5 * kept), 1)
    source = (lane % kept) // 6 * 5 + lane // kept
    spread = (source == lax.broadcasted_iota(jnp.int32, (20, 5 * kept), 0)).astype(jnp.float32)
    slots = jnp.dot(window, spread, precision=lax.Precision.HIGHEST)
    flat = l_index.reshape(rows * terms, 1)
    hot = (flat - w0 == lax.broadcasted_iota(jnp.int32, (rows * terms, near), 1)).astype(jnp.float32)
    cols = jnp.dot(hot, slots, precision=lax.Precision.HIGHEST)
    want = jnp.broadcast_to(c_index[:, None, :], (rows, terms, kept)).reshape(rows * terms, kept)
    want = want.astype(jnp.float32)
    d = flat - 32 * r
    part = lax.broadcasted_iota(jnp.int32, (rows * terms, kept), 1) // 6
    remote = (part // 2 != h).astype(jnp.int32)
    inside = (d >= 0) & (d < 32)
    piece = jnp.where(inside, (d // HALF) ^ h ^ remote, 2)
    j = d & (HALF - 1)
    where = jnp.full((rows * terms, kept), ZERO, jnp.int32)
    for s in range(5):
        place = piece * (2 * TILES) + (4 * j + s if s < 4 else 64 + j)
        where = jnp.where(cols[:, s * kept : (s + 1) * kept] == want, place, where)
    return where


def shards(l_blocks, s_blocks, l_index, s_cols, c_index):
    r, c = lax.axis_index("rows"), lax.axis_index("cols")
    groups = lax.axis_size("rows")
    h = c // 2
    across = functools.partial(lax.ppermute, axis_name="cols", perm=[(k, k ^ 2) for k in range(4)])
    beside = functools.partial(lax.ppermute, axis_name="cols", perm=[(k, k ^ 1) for k in range(4)])
    up = [(4 * g + k, 4 * g + 4 + k) for g in range(groups - 1) for k in (0, 1)]
    down = [(4 * g + k, 4 * g - 4 + k) for g in range(1, groups) for k in (2, 3)]
    along = functools.partial(lax.ppermute, axis_name=("rows", "cols"), perm=up + down)

    first, second = pack(h.reshape(1), s_blocks)
    far_first = across(first)
    halo = along(second)
    far_second = across(second)
    mate_first, mate_second = beside(first), beside(second)
    far_halo = along(far_first)
    mate_halo = beside(halo)
    cross_first = beside(far_first)
    cross_second = beside(far_second)
    cross_halo = beside(far_halo)

    tab = table(h, r, l_index, s_cols, c_index)
    out = None
    for flip, pieces in (
        (0, (first, second, halo)),
        (1, (mate_first, mate_second, mate_halo)),
        (2, (far_first, far_second, far_halo)),
        (3, (cross_first, cross_second, cross_halo)),
    ):
        out = product(tab, (c ^ flip).reshape(1), l_blocks, pieces, out)
    return out


def solution(mesh):
    return jax.shard_map(
        shards,
        mesh=mesh,
        in_specs=(
            P(("rows", "cols"), None, None),
            P("rows", None, "cols"),
            P(("rows", "cols"), None),
            P(),
            P(("rows", "cols"), None),
        ),
        out_specs=P(("rows", "cols"), None, None),
        check_vma=False,
    )
```

time: 388 us -> 138 us (0.36)
  the two profiles are of different devices: /device:TPU:3 before, /device:TPU:11 now
where the time goes in v1:
time: 138 us; the launch traced here: 137 us
  Pallas kernels  62.5 us (45%)
  waiting for transfers between devices  51 us (37%)
  starting transfers between devices  17.6 us (13%)
  other arithmetic  2.94 us (2%)
  local copies, waits for them, and re-layouts  1.95 us (1%)
    pallas_call x4, Pallas kernels, product(): pl.pallas_call(product_body, out_shape=jax.ShapeDtypeStruct((rows, 64, 15...  60.9 us
    ppermute x1, waiting for transfers between devices, shards(): far_halo = along(far_first)  28.5 us
    ppermute x1, waiting for transfers between devices, shards(): far_first = across(first)  13.7 us
    ppermute x1, waiting for transfers between devices, shards(): far_second = across(second)  8.78 us
    ppermute x1, starting transfers between devices, shards(): far_first = across(first)  5.67 us
    ppermute x1, starting transfers between devices, shards(): halo = along(second)  3.53 us
  transfers between devices with their start and end apart: 10, of which 3 were waited for; matrix products, arithmetic and copies ran while one was open for 3% of the time, Pallas kernels for 34%

profile of v1, /device:TPU:11, one launch (start us, length us, event | category | flops | bytes accessed | tf_op | source)
XLA Modules:
  0.0 137.4 jit_solution(14648017385258657942)
XLA Ops:
  0.0 1.4 %copy-done.1 = bf16[32,64,320]{2,1,0:T(8,128)(2,1)S(1)} copy-done((bf16[32,64,320]{2,1,0:T(8,128)(2,1)S(1)}, bf16[32,64,320]{2,1,0:T(8,128)(2,1)}, u32[]{:S(2)}) %copy-start.1) | copy-done | bytes 1310744
  1.4 1.5 %shard_map.55 = (bf16[40,64,128]{2,1,0:T(8,128)(2,1)}, bf16[40,64,128]{2,1,0:T(8,128)(2,1)}) custom-call(s32[1]{0:T(128)} %bitcast.1.start_ref, bf16[32,64,320]{2,1,0:T(8,128)(2,1)S(1)} %copy-done.1), custom_call_target="tpu_custom_call" | custom-call | bytes 3145728 | tf_op jit(solution)/shard_map/pallas_call | solution.py:39
  3.0 3.5 %collective-permute-start.8 = (bf16[40,64,128]{2,1,0:T(8,128)(2,1)}, bf16[40,64,128]{2,1,0:T(8,128)(2,1)}, u32[]{:S(2)}, u32[]{:S(2)}) collective-permute-start(bf16[40,64,128]{2,1,0:T(8,128)(2,1)} %get-tuple-element.8.b_ref), channel_id=1, source_target_pairs={{0,4},{1,5},{4,8},{5,9},{8,12},{9,13},{12,16},{13,17},{16,20},{17,... | collective-permute-start | bytes 1966088 | tf_op jit(solution)/shard_map/ppermute | solution.py:160
  6.5 1.0 collective-permute-start.7
  7.6 0.1 collective-permute-start.6
  7.7 5.7 %collective-permute-start = (bf16[40,64,128]{2,1,0:T(8,128)(2,1)}, bf16[40,64,128]{2,1,0:T(8,128)(2,1)S(1)}, u32[]{:S(2)}, u32[]{:S(2)}) collective-permute-start(bf16[40,64,128]{2,1,0:T(8,128)(2,1)} %get-tuple-element.7.a_ref), channel_id=1, source_target_pairs={{0,2},{1,3},{2,0},{3,1},{4,6},{5,7},{6,4},{7,5},{8,10},{9,11},{10,... | collective-permute-start | bytes 1966088 | tf_op jit(solution)/shard_map/ppermute | solution.py:159
  13.3 0.0 collective-permute-start.2
  13.4 0.1 sub.89
  13.5 0.1 sub.84
  13.6 1.0 fusion.13
  14.6 13.7 %collective-permute-done.a_ref = bf16[40,64,128]{2,1,0:T(8,128)(2,1)S(1)} collective-permute-done((bf16[40,64,128]{2,1,0:T(8,128)(2,1)}, bf16[40,64,128]{2,1,0:T(8,128)(2,1)S(1)}, u32[]{:S(2)}, u32[]{:S(2)}) %collective-permute-start) | collective-permute-done | bytes 655392 | tf_op jit(solution)/shard_map/ppermute | solution.py:159
  28.3 1.9 %collective-permute-start.4 = (bf16[40,64,128]{2,1,0:T(8,128)(2,1)S(1)}, bf16[40,64,128]{2,1,0:T(8,128)(2,1)}, u32[]{:S(2)}, u32[]{:S(2)}) collective-permute-start(bf16[40,64,128]{2,1,0:T(8,128)(2,1)S(1)} %collective-permute-done.a_ref), channel_id=1, source_target_pairs={{0,4},{1,5},{4,8},{5,9},{8,12},{9,13},{12,16},{13,17},{16,20},{17,... | collective-permute-start | bytes 1966088 | tf_op jit(solution)/shard_map/ppermute | solution.py:163
  30.2 0.6 fusion.30
  30.8 0.3 fusion.6
  31.1 1.5 %collective-permute-start.9 = (bf16[40,64,128]{2,1,0:T(8,128)(2,1)}, bf16[40,64,128]{2,1,0:T(8,128)(2,1)}, u32[]{:S(2)}, u32[]{:S(2)}) collective-permute-start(bf16[40,64,128]{2,1,0:T(8,128)(2,1)} %collective-permute-done.8.c_ref), channel_id=1, source_target_pairs={{0,1},{1,0},{2,3},{3,2},{4,5},{5,4},{6,7},{7,6},{8,9},{9,8},{10,11... | collective-permute-start | bytes 1966088 | tf_op jit(solution)/shard_map/ppermute | solution.py:164
  32.6 0.5 compare_and_fusion
  33.2 0.1 copy.15
  33.3 0.1 broadcast_in_dim.19
  33.3 0.1 convert_element_type.17
  33.4 0.1 copy.16
  33.6 0.1 collective-permute-start.1
  33.7 8.8 %collective-permute-done.2.b_ref = bf16[40,64,128]{2,1,0:T(8,128)(2,1)} collective-permute-done((bf16[40,64,128]{2,1,0:T(8,128)(2,1)}, bf16[40,64,128]{2,1,0:T(8,128)(2,1)}, u32[]{:S(2)}, u32[]{:S(2)}) %collective-permute-start.2) | collective-permute-done | bytes 655392 | tf_op jit(solution)/shard_map/ppermute | solution.py:161
  42.4 0.9 collective-permute-start.3
  43.4 28.5 %collective-permute-done.4.c_ref = bf16[40,64,128]{2,1,0:T(8,128)(2,1)} collective-permute-done((bf16[40,64,128]{2,1,0:T(8,128)(2,1)S(1)}, bf16[40,64,128]{2,1,0:T(8,128)(2,1)}, u32[]{:S(2)}, u32[]{:S(2)}) %collective-permute-start.4) | collective-permute-done | bytes 655392 | tf_op jit(solution)/shard_map/ppermute | solution.py:163
  71.9 2.7 %collective-permute-start.5 = (bf16[40,64,128]{2,1,0:T(8,128)(2,1)}, bf16[40,64,128]{2,1,0:T(8,128)(2,1)S(1)}, u32[]{:S(2)}, u32[]{:S(2)}) collective-permute-start(bf16[40,64,128]{2,1,0:T(8,128)(2,1)} %collective-permute-done.4.c_ref), channel_id=1, source_target_pairs={{0,1},{1,0},{2,3},{3,2},{4,5},{5,4},{6,7},{7,6},{8,9},{9,8},{10,11... | collective-permute-start | bytes 1966088 | tf_op jit(solution)/shard_map/ppermute | solution.py:167
  74.6 0.7 compare_and_fusion.1
  75.3 1.1 select_select_fusion.1.tab_ref
  76.4 15.7 %shard_map.56.rest_0_ = bf16[8,64,1536]{2,1,0:T(8,128)(2,1)} custom-call(s32[240,24]{1,0:T(8,128)S(1)} %select_select_fusion.1.tab_ref, s32[1]{0:T(128)} %bitcast.4.part_ref, bf16[8,64,1920]{2,1,0:T(8,128)(2,1)S(1)} %copy-done, bf16[40,64,128]{2,1,0:T(8,128)(2,1)} %get-tuple-element.7.a_ref, bf16[40,64,128]{2,1,0:T(8,128)(2,1)} %get-tuple-element.8.b_ref, ...), custom_call_target="tpu_custom_call" | custom-call | flops 755000000 | bytes 4194304 | tf_op jit(solution)/shard_map/pallas_call | solution.py:100
  92.1 15.5 %shard_map.57.rest_0_ = bf16[8,64,1536]{2,1,0:T(8,128)(2,1)} custom-call(s32[240,24]{1,0:T(8,128)S(1)} %select_select_fusion.1.tab_ref, s32[1]{0:T(128)} %bitcast.3.part_ref, bf16[8,64,1920]{2,1,0:T(8,128)(2,1)S(1)} %copy-done, bf16[40,64,128]{2,1,0:T(8,128)(2,1)} %collective-permute-done.6.a_ref, ...), custom_call_target="tpu_custom_call", output_to_operand_aliasing={{}: (6, {})} | custom-call | flops 755000000 | bytes 4194304 | tf_op jit(solution)/shard_map/pallas_call | solution.py:100
  107.6 15.5 %shard_map.58.rest_0_ = bf16[8,64,1536]{2,1,0:T(8,128)(2,1)} custom-call(s32[240,24]{1,0:T(8,128)S(1)} %select_select_fusion.1.tab_ref, s32[1]{0:T(128)} %bitcast.2.part_ref, bf16[8,64,1920]{2,1,0:T(8,128)(2,1)S(1)} %copy-done, bf16[40,64,128]{2,1,0:T(8,128)(2,1)S(1)} %collective-permute-done.a_ref, ...), custom_call_target="tpu_custom_call", output_to_operand_aliasing={{}: (6, {})} | custom-call | flops 755000000 | bytes 4194304 | tf_op jit(solution)/shard_map/pallas_call | solution.py:100
  123.2 0.0 collective-permute-done.5.c_ref
  123.2 14.2 %shard_map.59 = bf16[8,64,1536]{2,1,0:T(8,128)(2,1)} custom-call(s32[240,24]{1,0:T(8,128)S(1)} %select_select_fusion.1.tab_ref, s32[1]{0:T(128)} %bitcast.part_ref, bf16[8,64,1920]{2,1,0:T(8,128)(2,1)S(1)} %copy-done, bf16[40,64,128]{2,1,0:T(8,128)(2,1)S(1)} %collective-permute-done.1.a_ref, ...), custom_call_target="tpu_custom_call", output_to_operand_aliasing={{}: (6, {})} | custom-call | flops 755000000 | bytes 4194304 | tf_op jit(solution)/shard_map/pallas_call | solution.py:100
  (21 shorter events, 0.1 us)
Async XLA Ops:
  0.0 13.4 %copy-start.3 = (s32[8,30]{1,0:T(8,128)S(1)}, s32[8,30]{1,0:T(8,128)}, u32[]{:S(2)}) copy-start(s32[8,30]{1,0:T(8,128)} %param.7) | copy-start | bytes 2884
  0.0 33.2 %copy-start.4 = (s32[8,24]{1,0:T(8,128)S(1)}, s32[8,24]{1,0:T(8,128)}, u32[]{:S(2)}) copy-start(s32[8,24]{1,0:T(8,128)} %param.9) | copy-start | bytes 2308
  0.0 1.4 %copy-start.1 = (bf16[32,64,320]{2,1,0:T(8,128)(2,1)S(1)}, bf16[32,64,320]{2,1,0:T(8,128)(2,1)}, u32[]{:S(2)}) copy-start(bf16[32,64,320]{2,1,0:T(8,128)(2,1)} %s_ref.1) | copy-start | bytes 3932164
  1.4 74.9 %copy-start = (bf16[8,64,1920]{2,1,0:T(8,128)(2,1)S(1)}, bf16[8,64,1920]{2,1,0:T(8,128)(2,1)}, u32[]{:S(2)}) copy-start(bf16[8,64,1920]{2,1,0:T(8,128)(2,1)} %l_ref.7) | copy-start | bytes 5898244
  3.0 28.1 %collective-permute-start.8 = (bf16[40,64,128]{2,1,0:T(8,128)(2,1)}, bf16[40,64,128]{2,1,0:T(8,128)(2,1)}, u32[]{:S(2)}, u32[]{:S(2)}) collective-permute-start(bf16[40,64,128]{2,1,0:T(8,128)(2,1)} %get-tuple-element.8.b_ref), channel_id=1, source_target_pairs={{0,4},{1,5},{4,8},{5,9},{8,12},{9,13},{12,16},{13,17},{16,20},{17,... | collective-permute-start | bytes 1966088 | tf_op jit(solution)/shard_map/ppermute | solution.py:160
  6.5 85.6 %collective-permute-start.7 = (bf16[40,64,128]{2,1,0:T(8,128)(2,1)}, bf16[40,64,128]{2,1,0:T(8,128)(2,1)S(1)}, u32[]{:S(2)}, u32[]{:S(2)}) collective-permute-start(bf16[40,64,128]{2,1,0:T(8,128)(2,1)} %get-tuple-element.8.b_ref), channel_id=1, source_target_pairs={{0,1},{1,0},{2,3},{3,2},{4,5},{5,4},{6,7},{7,6},{8,9},{9,8},{10,11... | collective-permute-start | bytes 1966088 | tf_op jit(solution)/shard_map/ppermute | solution.py:162
  7.6 26.0 %collective-permute-start.6 = (bf16[40,64,128]{2,1,0:T(8,128)(2,1)}, bf16[40,64,128]{2,1,0:T(8,128)(2,1)}, u32[]{:S(2)}, u32[]{:S(2)}) collective-permute-start(bf16[40,64,128]{2,1,0:T(8,128)(2,1)} %get-tuple-element.7.a_ref), channel_id=1, source_target_pairs={{0,1},{1,0},{2,3},{3,2},{4,5},{5,4},{6,7},{7,6},{8,9},{9,8},{10,11... | collective-permute-start | bytes 1966088 | tf_op jit(solution)/shard_map/ppermute | solution.py:162
  7.7 20.6 %collective-permute-start = (bf16[40,64,128]{2,1,0:T(8,128)(2,1)}, bf16[40,64,128]{2,1,0:T(8,128)(2,1)S(1)}, u32[]{:S(2)}, u32[]{:S(2)}) collective-permute-start(bf16[40,64,128]{2,1,0:T(8,128)(2,1)} %get-tuple-element.7.a_ref), channel_id=1, source_target_pairs={{0,2},{1,3},{2,0},{3,1},{4,6},{5,7},{6,4},{7,5},{8,10},{9,11},{10,... | collective-permute-start | bytes 1966088 | tf_op jit(solution)/shard_map/ppermute | solution.py:159
  13.3 29.1 %collective-permute-start.2 = (bf16[40,64,128]{2,1,0:T(8,128)(2,1)}, bf16[40,64,128]{2,1,0:T(8,128)(2,1)}, u32[]{:S(2)}, u32[]{:S(2)}) collective-permute-start(bf16[40,64,128]{2,1,0:T(8,128)(2,1)} %get-tuple-element.8.b_ref), channel_id=1, source_target_pairs={{0,2},{1,3},{2,0},{3,1},{4,6},{5,7},{6,4},{7,5},{8,10},{9,11},{10,... | collective-permute-start | bytes 1966088 | tf_op jit(solution)/shard_map/ppermute | solution.py:161
  13.5 16.8 %copy-start.2 = (s32[240]{0:T(256)}, s32[240]{0:T(256)S(1)}, u32[]{:S(2)}) copy-start(s32[240]{0:T(256)S(1)} %sub.89) | copy-start | bytes 2884
  28.3 43.6 %collective-permute-start.4 = (bf16[40,64,128]{2,1,0:T(8,128)(2,1)S(1)}, bf16[40,64,128]{2,1,0:T(8,128)(2,1)}, u32[]{:S(2)}, u32[]{:S(2)}) collective-permute-start(bf16[40,64,128]{2,1,0:T(8,128)(2,1)S(1)} %collective-permute-done.a_ref), channel_id=1, source_target_pairs={{0,4},{1,5},{4,8},{5,9},{8,12},{9,13},{12,16},{13,17},{16,20},{17,... | collective-permute-start | bytes 1966088 | tf_op jit(solution)/shard_map/ppermute | solution.py:163
  31.1 61.0 %collective-permute-start.9 = (bf16[40,64,128]{2,1,0:T(8,128)(2,1)}, bf16[40,64,128]{2,1,0:T(8,128)(2,1)}, u32[]{:S(2)}, u32[]{:S(2)}) collective-permute-start(bf16[40,64,128]{2,1,0:T(8,128)(2,1)} %collective-permute-done.8.c_ref), channel_id=1, source_target_pairs={{0,1},{1,0},{2,3},{3,2},{4,5},{5,4},{6,7},{7,6},{8,9},{9,8},{10,11... | collective-permute-start | bytes 1966088 | tf_op jit(solution)/shard_map/ppermute | solution.py:164
  33.6 89.6 %collective-permute-start.1 = (bf16[40,64,128]{2,1,0:T(8,128)(2,1)S(1)}, bf16[40,64,128]{2,1,0:T(8,128)(2,1)S(1)}, u32[]{:S(2)}, u32[]{:S(2)}) collective-permute-start(bf16[40,64,128]{2,1,0:T(8,128)(2,1)S(1)} %collective-permute-done.a_ref), channel_id=1, source_target_pairs={{0,1},{1,0},{2,3},{3,2},{4,5},{5,4},{6,7},{7,6},{8,9},{9,8},{10,11... | collective-permute-start | bytes 1966088 | tf_op jit(solution)/shard_map/ppermute | solution.py:165
  42.4 80.7 %collective-permute-start.3 = (bf16[40,64,128]{2,1,0:T(8,128)(2,1)}, bf16[40,64,128]{2,1,0:T(8,128)(2,1)S(1)}, u32[]{:S(2)}, u32[]{:S(2)}) collective-permute-start(bf16[40,64,128]{2,1,0:T(8,128)(2,1)} %collective-permute-done.2.b_ref), channel_id=1, source_target_pairs={{0,1},{1,0},{2,3},{3,2},{4,5},{5,4},{6,7},{7,6},{8,9},{9,8},{10,11... | collective-permute-start | bytes 1966088 | tf_op jit(solution)/shard_map/ppermute | solution.py:166
  71.9 51.3 %collective-permute-start.5 = (bf16[40,64,128]{2,1,0:T(8,128)(2,1)}, bf16[40,64,128]{2,1,0:T(8,128)(2,1)S(1)}, u32[]{:S(2)}, u32[]{:S(2)}) collective-permute-start(bf16[40,64,128]{2,1,0:T(8,128)(2,1)} %collective-permute-done.4.c_ref), channel_id=1, source_target_pairs={{0,1},{1,0},{2,3},{3,2},{4,5},{5,4},{6,7},{7,6},{8,9},{9,8},{10,11... | collective-permute-start | bytes 1966088 | tf_op jit(solution)/shard_map/ppermute | solution.py:167

commit v2 on v1

v2 whole, which is shorter than its diff:
```python
import functools

import jax
import jax.numpy as jnp
from jax import lax
from jax.experimental import pallas as pl
from jax.experimental.pallas import tpu as pltpu
from jax.sharding import PartitionSpec as P

HALF = 16
TILES = 40
ZERO = 6 * TILES


def pack_body(start_ref, s_ref, first_ref, second_ref, both_ref):
    def row(j, carry):
        for out_ref, base in places:
            for t in range(2):
                out_ref[2 * j + t] = s_ref[base + j, :, 128 * t : 128 * t + 128]
        return carry

    def pair(j, carry):
        for out_ref, base in places:
            out_ref[32 + j] = jnp.concatenate(
                [s_ref[base + 2 * j, :, 256:320], s_ref[base + 2 * j + 1, :, 256:320]], axis=1
            )
        return carry

    places = ((first_ref, HALF * start_ref[0]), (second_ref, HALF * (1 - start_ref[0])))
    lax.fori_loop(0, HALF, row, 0, unroll=4)
    lax.fori_loop(0, HALF // 2, pair, 0, unroll=4)
    both_ref[:TILES] = first_ref[...]
    both_ref[TILES:] = second_ref[...]


def pack(start, s_blocks):
    piece = jax.ShapeDtypeStruct((TILES, 64, 128), jnp.bfloat16)
    both = jax.ShapeDtypeStruct((2 * TILES, 64, 128), jnp.bfloat16)
    vmem = pl.BlockSpec(memory_space=pltpu.VMEM)
    return pl.pallas_call(
        pack_body,
        out_shape=(piece, piece, both),
        in_specs=[pl.BlockSpec(memory_space=pltpu.SMEM), vmem],
        out_specs=(vmem,) * 3,
        compiler_params=pltpu.CompilerParams(vmem_limit_bytes=16 << 20),
        cost_estimate=pl.CostEstimate(flops=0, bytes_accessed=3 << 20, transcendentals=0),
    )(start, s_blocks)


def product_body(count, tab_ref, part_ref, l_ref, *rest):
    o_ref, sd_ref, ob_ref, sem = rest[-4:]
    rows = l_ref.shape[0]
    base = 0
    for piece in rest[:count]:

        def spread(t, carry, piece=piece, base=base):
            v = piece[t]
            sd_ref[base + 2 * t] = v
            sd_ref[base + 2 * t + 1] = jnp.concatenate([v[:, 64:], v[:, :64]], axis=1)
            return carry

        lax.fori_loop(0, piece.shape[0], spread, 0, unroll=8)
        base += 2 * piece.shape[0]
    for zero in (ZERO, ZERO + 1):
        sd_ref[zero] = jnp.zeros((64, 128), jnp.bfloat16)
    part = part_ref[0]
    low = lax.broadcasted_iota(jnp.int32, (64, 128), 1) < 64

    def out(i):
        lanes = pl.ds(pl.multiple_of(part * 384, 128), 384)
        return pltpu.make_async_copy(ob_ref.at[i], o_ref.at[i, :, lanes], sem.at[i])

    def row(i, carry):
        def pick(k, m):
            at = (i * 30 + k) * 24 + part * 6 + 2 * m
            return jnp.where(low, sd_ref[tab_ref[at]], sd_ref[tab_ref[at + 1]])

        total = jnp.zeros((64, 384), jnp.float32)
        for k0 in range(0, 30, 4):
            ks = range(k0, min(k0 + 4, 30))
            picked = jnp.concatenate(
                [jnp.concatenate([pick(k, m) for m in range(3)], axis=1) for k in ks], axis=0
            )
            total = total + jnp.dot(
                l_ref[i, :, 64 * k0 : 64 * (k0 + len(ks))], picked, preferred_element_type=jnp.float32
            )
        ob_ref[i] = total.astype(o_ref.dtype)
        out(i).start()
        return carry

    lax.fori_loop(0, rows, row, 0)

    def finish(i, carry):
        out(i).wait()
        return carry

    lax.fori_loop(0, rows, finish, 0)


def product(tab, part, l_blocks, pieces, prev):
    rows = l_blocks.shape[0]
    vmem, smem = pl.BlockSpec(memory_space=pltpu.VMEM), pl.BlockSpec(memory_space=pltpu.SMEM)
    in_specs = [smem, smem] + [vmem] * (1 + len(pieces))
    args = [tab, part, l_blocks, *pieces]
    aliases = {}
    if prev is not None:
        in_specs.append(pl.BlockSpec(memory_space=pl.ANY))
        aliases = {len(args): 0}
        args.append(prev)
    return pl.pallas_call(
        functools.partial(product_body, len(pieces)),
        out_shape=jax.ShapeDtypeStruct((rows, 64, 1536), jnp.bfloat16),
        in_specs=in_specs,
        out_specs=pl.BlockSpec(memory_space=pl.ANY),
        scratch_shapes=[
            pltpu.VMEM((ZERO + 2, 64, 128), jnp.bfloat16),
            pltpu.VMEM((rows, 64, 384), jnp.bfloat16),
            pltpu.SemaphoreType.DMA((rows,)),
        ],
        input_output_aliases=aliases,
        compiler_params=pltpu.CompilerParams(vmem_limit_bytes=24 << 20),
        cost_estimate=pl.CostEstimate(flops=755_000_000, bytes_accessed=20 << 20, transcendentals=0),
    )(*args)


def table(h, r, l_index, s_cols, c_index):
    total = s_cols.shape[0]
    rows, terms = l_index.shape
    kept = c_index.shape[1]
    near = 4 * HALF
    w0 = jnp.clip(32 * r - HALF, 0, total - near)
    window = lax.dynamic_slice_in_dim(s_cols, w0, near, axis=0).astype(jnp.float32)
    lane = lax.broadcasted_iota(jnp.int32, (20, 5 * kept), 1)
    source = (lane % kept) // 6 * 5 + lane // kept
    spread = (source == lax.broadcasted_iota(jnp.int32, (20, 5 * kept), 0)).astype(jnp.float32)
    slots = jnp.dot(window, spread, precision=lax.Precision.HIGHEST)
    flat = l_index.reshape(rows * terms, 1)
    hot = (flat - w0 == lax.broadcasted_iota(jnp.int32, (rows * terms, near), 1)).astype(jnp.float32)
    cols = jnp.dot(hot, slots, precision=lax.Precision.HIGHEST)
    want = jnp.broadcast_to(c_index[:, None, :], (rows, terms, kept)).reshape(rows * terms, kept)
    want = want.astype(jnp.float32)
    d = flat - 32 * r
    part = lax.broadcasted_iota(jnp.int32, (rows * terms, kept), 1) // 6
    remote = (part // 2 != h).astype(jnp.int32)
    inside = (d >= 0) & (d < 32)
    piece = jnp.where(inside, (d // HALF) ^ h ^ remote, 2)
    j = d & (HALF - 1)
    where = jnp.full((rows * terms, kept), ZERO, jnp.int32)
    odd = lax.broadcasted_iota(jnp.int32, (rows * terms, kept), 1) & 1
    for s in range(5):
        place = piece * (2 * TILES) + (4 * j + s if s < 4 else 64 + j)
        where = jnp.where(cols[:, s * kept : (s + 1) * kept] == want, place, where)
    return (where ^ odd).reshape(rows * terms * kept)


def shards(l_blocks, s_blocks, l_index, s_cols, c_index):
    r, c = lax.axis_index("rows"), lax.axis_index("cols")
    groups = lax.axis_size("rows")
    h = c // 2
    across = functools.partial(lax.ppermute, axis_name="cols", perm=[(k, k ^ 2) for k in range(4)])
    beside = functools.partial(lax.ppermute, axis_name="cols", perm=[(k, k ^ 1) for k in range(4)])
    up = [(4 * g + k, 4 * g + 4 + k) for g in range(groups - 1) for k in (0, 1)]
    down = [(4 * g + k, 4 * g - 4 + k) for g in range(1, groups) for k in (2, 3)]
    below, above = groups // 2 - 1, groups // 2
    seam = [(4 * below + 2 + k, 4 * above + k) for k in (0, 1)]
    seam += [(4 * above + k, 4 * below + 2 + k) for k in (0, 1)]
    plain = [route for route in up + down if route[1] not in {q for _, q in seam}]
    takes = ((r == above) & (h == 0)) | ((r == below) & (h == 1))

    def send(x, perm):
        return lax.ppermute(x, ("rows", "cols"), perm)

    first, second, both = pack(h.reshape(1), s_blocks)
    far_first = across(first)
    halo = send(second, up + down)
    seam_halo = send(first, seam)
    tab = table(h, r, l_index, s_cols, c_index)
    second, both, tab = lax.optimization_barrier((second, both, tab))
    far_second = across(second)
    mate = beside(both)

    far_halo = send(far_first, plain)
    cross_first = beside(far_first)
    mate_halo = beside(halo)
    tab, far_first = lax.optimization_barrier((tab, far_first))
    parts = [(c ^ flip).reshape(1) for flip in range(4)]
    out = product(tab, parts[0], l_blocks, (both, halo), None)
    out = product(tab, parts[1], l_blocks, (mate, mate_halo), out)
    out, far_second, far_halo = lax.optimization_barrier((out, far_second, far_halo))
    cross_second = beside(far_second)
    far_halo = jnp.where(takes, seam_halo, far_halo)
    cross_halo = beside(far_halo)
    out = product(tab, parts[2], l_blocks, (far_first, far_second, far_halo), out)
    return product(tab, parts[3], l_blocks, (cross_first, cross_second, cross_halo), out)


def solution(mesh):
    return jax.shard_map(
        shards,
        mesh=mesh,
        in_specs=(
            P(("rows", "cols"), None, None),
            P("rows", None, "cols"),
            P(("rows", "cols"), None),
            P(),
            P(("rows", "cols"), None),
        ),
        out_specs=P(("rows", "cols"), None, None),
        check_vma=False,
    )
```

time: 138 us -> 84.6 us (0.61)
  the two profiles are of different devices: /device:TPU:11 before, /device:TPU:3 now
where the time goes in v2:
time: 84.6 us; the launch traced here: 84.2 us
  Pallas kernels  33.7 us (40%)
  starting transfers between devices  26.4 us (31%)
  waiting for transfers between devices  17.6 us (21%)
  other arithmetic  2.84 us (3%)
  local copies, waits for them, and re-layouts  2.02 us (2%)
  matrix products  1.4 us (2%)
    pallas_call x4, Pallas kernels, product(): pl.pallas_call(functools.partial(product_body, len(pieces)), out_shape=ja...  31.8 us
    ppermute x3, waiting for transfers between devices, send(): return lax.ppermute(x, ('rows', 'cols'), perm)  17.6 us
    ppermute x3, starting transfers between devices, send(): return lax.ppermute(x, ('rows', 'cols'), perm)  12.8 us
    ppermute x1, starting transfers between devices, shards(): far_first = across(first)  8.59 us
    pallas_call x1, Pallas kernels, pack(): pl.pallas_call(pack_body, out_shape=(piece, piece, both), in_specs=[pl.Bl...  1.88 us
    ppermute x1, starting transfers between devices, shards(): cross_halo = beside(far_halo)  1.82 us
  transfers between devices with their start and end apart: 10, of which 2 were waited for; matrix products, arithmetic and copies ran while one was open for 1% of the time, Pallas kernels for 28%

profile of v2, /device:TPU:3, one launch (start us, length us, event | category | flops | bytes accessed | tf_op | source)
XLA Modules:
  0.0 84.2 jit_solution(2148907682861710374)
XLA Ops:
  0.1 0.8 broadcast_subtract_fusion
  0.9 0.1 sub.90
  1.0 0.1 sub.85
  1.1 0.7 convert_element_type.16
  1.8 0.1 copy.10
  1.9 0.1 broadcast_in_dim.19
  2.0 0.1 convert_element_type.17
  2.1 1.0 %fusion.13 = f32[64,120]{1,0:T(8,128)S(1)} fusion(s32[2048,20]{0,1:T(8,128)} %param.8, s32[]{:T(128)S(6)} %min.4, s32[120]{0:T(128)S(1)} %get-tuple-element.37, s32[120]{0:T(128)S(1)} %get-tuple-element.39, s32[120]{0:T(128)S(1)} %get-tuple-element.38, s32[120]{0:T(128)S(1)} %get-tuple-element.40, pred[120]{0:T(512)(128)(4,1)S(1)} %get-tuple-element.35, ...), kind=kOutput, calls=%fused_computation.32 | convolution fusion | flops 1875680 | bytes 45172 | tf_op jit(solution)/shard_map/dot_general | solution.py:136
  3.1 0.4 fusion
  3.5 0.1 select_xor_fusion
  3.6 0.1 copy.11
  3.7 0.1 reshape.112.tab_ref
  3.8 1.4 %copy-done.1 = bf16[32,64,320]{2,1,0:T(8,128)(2,1)S(1)} copy-done((bf16[32,64,320]{2,1,0:T(8,128)(2,1)S(1)}, bf16[32,64,320]{2,1,0:T(8,128)(2,1)}, u32[]{:S(2)}) %copy-start.1) | copy-done | bytes 1310744
  5.2 1.9 %shard_map.55 = (bf16[40,64,128]{2,1,0:T(8,128)(2,1)}, bf16[40,64,128]{2,1,0:T(8,128)(2,1)}, bf16[80,64,128]{2,1,0:T(8,128)(2,1)}) custom-call(s32[1]{0:T(128)} %bitcast.start_ref, bf16[32,64,320]{2,1,0:T(8,128)(2,1)S(1)} %copy-done.1), custom_call_target="tpu_custom_call" | custom-call | bytes 3145728 | tf_op jit(solution)/shard_map/pallas_call | solution.py:40
  7.1 0.7 collective-permute-start.2
  7.8 3.5 %collective-permute-start.3 = (bf16[40,64,128]{2,1,0:T(8,128)(2,1)}, bf16[40,64,128]{2,1,0:T(8,128)(2,1)}, u32[]{:S(2)}, u32[]{:S(2)}) collective-permute-start(bf16[40,64,128]{2,1,0:T(8,128)(2,1)} %get-tuple-element.22), channel_id=1, source_target_pairs={{0,4},{1,5},{4,8},{5,9},{8,12},{9,13},{12,16},{13,17},{16,20},{17,... | collective-permute-start | bytes 1966088 | tf_op jit(solution)/shard_map/ppermute | solution.py:171
  11.3 8.6 %collective-permute-start = (bf16[40,64,128]{2,1,0:T(8,128)(2,1)}, bf16[40,64,128]{2,1,0:T(8,128)(2,1)}, u32[]{:S(2)}, u32[]{:S(2)}) collective-permute-start(bf16[40,64,128]{2,1,0:T(8,128)(2,1)} %get-tuple-element.19), channel_id=1, source_target_pairs={{0,2},{1,3},{2,0},{3,1},{4,6},{5,7},{6,4},{7,5},{8,10},{9,11},{10,... | collective-permute-start | bytes 1966088 | tf_op jit(solution)/shard_map/ppermute | solution.py:174
  19.9 13.2 %collective-permute-done.3.rest_1_ = bf16[40,64,128]{2,1,0:T(8,128)(2,1)} collective-permute-done((bf16[40,64,128]{2,1,0:T(8,128)(2,1)}, bf16[40,64,128]{2,1,0:T(8,128)(2,1)}, u32[]{:S(2)}, u32[]{:S(2)}) %collective-permute-start.3) | collective-permute-done | bytes 655392 | tf_op jit(solution)/shard_map/ppermute | solution.py:171
  33.1 0.6 collective-permute-start.4
  33.8 1.3 %collective-permute-start.5 = (bf16[40,64,128]{2,1,0:T(8,128)(2,1)}, bf16[40,64,128]{2,1,0:T(8,128)(2,1)}, u32[]{:S(2)}, u32[]{:S(2)}) collective-permute-start(bf16[40,64,128]{2,1,0:T(8,128)(2,1)} %get-tuple-element.22), channel_id=1, source_target_pairs={{0,2},{1,3},{2,0},{3,1},{4,6},{5,7},{6,4},{7,5},{8,10},{9,11},{10,... | collective-permute-start | bytes 1966088 | tf_op jit(solution)/shard_map/ppermute | solution.py:179
  35.1 0.0 collective-permute-done.rest_0_
  35.1 2.1 %collective-permute-start.6 = (bf16[40,64,128]{2,1,0:T(8,128)(2,1)}, bf16[40,64,128]{2,1,0:T(8,128)(2,1)}, u32[]{:S(2)}, u32[]{:S(2)}) collective-permute-start(bf16[40,64,128]{2,1,0:T(8,128)(2,1)} %collective-permute-done.rest_0_), channel_id=1, source_target_pairs={{0,4},{1,5},{4,8},{5,9},{8,12},{9,13},{12,16},{13,17},{16,20},{17,... | collective-permute-start | bytes 1966088 | tf_op jit(solution)/shard_map/ppermute | solution.py:171
  37.2 7.2 %collective-permute-start.8 = (bf16[40,64,128]{2,1,0:T(8,128)(2,1)}, bf16[40,64,128]{2,1,0:T(8,128)(2,1)}, u32[]{:S(2)}, u32[]{:S(2)}) collective-permute-start(bf16[40,64,128]{2,1,0:T(8,128)(2,1)} %get-tuple-element.19), channel_id=1, source_target_pairs={{126,128},{127,129},{128,126},{129,127}} | collective-permute-start | bytes 1966088 | tf_op jit(solution)/shard_map/ppermute | solution.py:171
  44.5 8.2 %shard_map.56.rest_2_ = bf16[8,64,1536]{2,1,0:T(8,128)(2,1)} custom-call(s32[5760]{0:T(1024)S(1)} %reshape.112.tab_ref, s32[1]{0:T(128)} %bitcast.3.part_ref, bf16[8,64,1920]{2,1,0:T(8,128)(2,1)S(1)} %copy-done, bf16[80,64,128]{2,1,0:T(8,128)(2,1)} %get-tuple-element.21.rest_0_, bf16[40,64,128]{2,1,0:T(8,128)(2,1)} %collective-permute-done.3.rest_1_), custom_call_target="tpu_custom_call" | custom-call | flops 755000000 | bytes 20971520 | tf_op jit(solution)/shard_map/pallas_call | solution.py:110
  52.6 0.4 collective-permute-start.1
  53.0 7.8 %shard_map.57.rest_3_ = bf16[8,64,1536]{2,1,0:T(8,128)(2,1)} custom-call(s32[5760]{0:T(1024)S(1)} %reshape.112.tab_ref, s32[1]{0:T(128)} %bitcast.2.part_ref, bf16[8,64,1920]{2,1,0:T(8,128)(2,1)S(1)} %copy-done, bf16[80,64,128]{2,1,0:T(8,128)(2,1)S(1)} %collective-permute-done.2.rest_0_, ...), custom_call_target="tpu_custom_call", output_to_operand_aliasing={{}: (5, {})} | custom-call | flops 755000000 | bytes 20971520 | tf_op jit(solution)/shard_map/pallas_call | solution.py:110
  60.8 4.3 %collective-permute-done.8 = bf16[40,64,128]{2,1,0:T(8,128)(2,1)} collective-permute-done((bf16[40,64,128]{2,1,0:T(8,128)(2,1)}, bf16[40,64,128]{2,1,0:T(8,128)(2,1)}, u32[]{:S(2)}, u32[]{:S(2)}) %collective-permute-start.8) | collective-permute-done | bytes 655392 | tf_op jit(solution)/shard_map/ppermute | solution.py:171
  65.1 1.2 %broadcast_select_fusion.rest_2_ = bf16[40,64,128]{2,1,0:T(8,128)(2,1)S(1)} fusion(bf16[40,64,128]{2,1,0:T(8,128)(2,1)} %collective-permute-done.8, bf16[40,64,128]{2,1,0:T(8,128)(2,1)} %collective-permute-done.6, pred[]{:T(512)S(6)} %or.3), kind=kLoop, calls=%fused_computation | loop fusion | flops 327680 | bytes 1966081 | tf_op jit(solution)/shard_map/jit(_where)/select_n | solution.py:191
  66.3 1.8 %collective-permute-start.9 = (bf16[40,64,128]{2,1,0:T(8,128)(2,1)S(1)}, bf16[40,64,128]{2,1,0:T(8,128)(2,1)S(1)}, u32[]{:S(2)}, u32[]{:S(2)}) collective-permute-start(bf16[40,64,128]{2,1,0:T(8,128)(2,1)S(1)} %broadcast_select_fusion.rest_2_), channel_id=1, source_target_pairs={{0,1},{1,0},{2,3},{3,2},{4,5},{5,4},{6,7},{7,6},{8,9},{9,8},{10,11... | collective-permute-start | bytes 1966088 | tf_op jit(solution)/shard_map/ppermute | solution.py:192
  68.1 0.1 collective-permute-start.7
  68.2 8.0 %shard_map.58.rest_3_ = bf16[8,64,1536]{2,1,0:T(8,128)(2,1)} custom-call(s32[5760]{0:T(1024)S(1)} %reshape.112.tab_ref, s32[1]{0:T(128)} %bitcast.4.part_ref, bf16[8,64,1920]{2,1,0:T(8,128)(2,1)S(1)} %copy-done, bf16[40,64,128]{2,1,0:T(8,128)(2,1)} %collective-permute-done.rest_0_, ...), custom_call_target="tpu_custom_call", output_to_operand_aliasing={{}: (6, {})} | custom-call | flops 755000000 | bytes 20971520 | tf_op jit(solution)/shard_map/pallas_call | solution.py:110
  76.2 8.0 %shard_map.59 = bf16[8,64,1536]{2,1,0:T(8,128)(2,1)} custom-call(s32[5760]{0:T(1024)S(1)} %reshape.112.tab_ref, s32[1]{0:T(128)} %bitcast.1.part_ref, bf16[8,64,1920]{2,1,0:T(8,128)(2,1)S(1)} %copy-done, bf16[40,64,128]{2,1,0:T(8,128)(2,1)} %collective-permute-done.1.rest_0_, ...), custom_call_target="tpu_custom_call", output_to_operand_aliasing={{}: (6, {})} | custom-call | flops 755000000 | bytes 20971520 | tf_op jit(solution)/shard_map/pallas_call | solution.py:110
  (18 shorter events, 0.1 us)
Async XLA Ops:
  0.0 44.4 %copy-start = (bf16[8,64,1920]{2,1,0:T(8,128)(2,1)S(1)}, bf16[8,64,1920]{2,1,0:T(8,128)(2,1)}, u32[]{:S(2)}) copy-start(bf16[8,64,1920]{2,1,0:T(8,128)(2,1)} %l_ref.7) | copy-start | bytes 5898244
  3.8 1.4 %copy-start.1 = (bf16[32,64,320]{2,1,0:T(8,128)(2,1)S(1)}, bf16[32,64,320]{2,1,0:T(8,128)(2,1)}, u32[]{:S(2)}) copy-start(bf16[32,64,320]{2,1,0:T(8,128)(2,1)} %s_ref.1) | copy-start | bytes 3932164
  7.1 45.5 %collective-permute-start.2 = (bf16[80,64,128]{2,1,0:T(8,128)(2,1)}, bf16[80,64,128]{2,1,0:T(8,128)(2,1)S(1)}, u32[]{:S(2)}, u32[]{:S(2)}) collective-permute-start(bf16[80,64,128]{2,1,0:T(8,128)(2,1)} %get-tuple-element.21.rest_0_), channel_id=1, source_target_pairs={{0,1},{1,0},{2,3},{3,2},{4,5},{5,4},{6,7},{7,6},{8,9},{9,8},{10,11... | collective-permute-start | bytes 3932168 | tf_op jit(solution)/shard_map/ppermute | solution.py:180
  7.8 25.4 %collective-permute-start.3 = (bf16[40,64,128]{2,1,0:T(8,128)(2,1)}, bf16[40,64,128]{2,1,0:T(8,128)(2,1)}, u32[]{:S(2)}, u32[]{:S(2)}) collective-permute-start(bf16[40,64,128]{2,1,0:T(8,128)(2,1)} %get-tuple-element.22), channel_id=1, source_target_pairs={{0,4},{1,5},{4,8},{5,9},{8,12},{9,13},{12,16},{13,17},{16,20},{17,... | collective-permute-start | bytes 1966088 | tf_op jit(solution)/shard_map/ppermute | solution.py:171
  11.3 23.8 %collective-permute-start = (bf16[40,64,128]{2,1,0:T(8,128)(2,1)}, bf16[40,64,128]{2,1,0:T(8,128)(2,1)}, u32[]{:S(2)}, u32[]{:S(2)}) collective-permute-start(bf16[40,64,128]{2,1,0:T(8,128)(2,1)} %get-tuple-element.19), channel_id=1, source_target_pairs={{0,2},{1,3},{2,0},{3,1},{4,6},{5,7},{6,4},{7,5},{8,10},{9,11},{10,... | collective-permute-start | bytes 1966088 | tf_op jit(solution)/shard_map/ppermute | solution.py:174
  33.1 19.9 %collective-permute-start.4 = (bf16[40,64,128]{2,1,0:T(8,128)(2,1)}, bf16[40,64,128]{2,1,0:T(8,128)(2,1)}, u32[]{:S(2)}, u32[]{:S(2)}) collective-permute-start(bf16[40,64,128]{2,1,0:T(8,128)(2,1)} %collective-permute-done.3.rest_1_), channel_id=1, source_target_pairs={{0,1},{1,0},{2,3},{3,2},{4,5},{5,4},{6,7},{7,6},{8,9},{9,8},{10,11... | collective-permute-start | bytes 1966088 | tf_op jit(solution)/shard_map/ppermute | solution.py:184
  33.8 27.0 %collective-permute-start.5 = (bf16[40,64,128]{2,1,0:T(8,128)(2,1)}, bf16[40,64,128]{2,1,0:T(8,128)(2,1)}, u32[]{:S(2)}, u32[]{:S(2)}) collective-permute-start(bf16[40,64,128]{2,1,0:T(8,128)(2,1)} %get-tuple-element.22), channel_id=1, source_target_pairs={{0,2},{1,3},{2,0},{3,1},{4,6},{5,7},{6,4},{7,5},{8,10},{9,11},{10,... | collective-permute-start | bytes 1966088 | tf_op jit(solution)/shard_map/ppermute | solution.py:179
  35.1 25.7 %collective-permute-start.6 = (bf16[40,64,128]{2,1,0:T(8,128)(2,1)}, bf16[40,64,128]{2,1,0:T(8,128)(2,1)}, u32[]{:S(2)}, u32[]{:S(2)}) collective-permute-start(bf16[40,64,128]{2,1,0:T(8,128)(2,1)} %collective-permute-done.rest_0_), channel_id=1, source_target_pairs={{0,4},{1,5},{4,8},{5,9},{8,12},{9,13},{12,16},{13,17},{16,20},{17,... | collective-permute-start | bytes 1966088 | tf_op jit(solution)/shard_map/ppermute | solution.py:171
  37.2 27.9 %collective-permute-start.8 = (bf16[40,64,128]{2,1,0:T(8,128)(2,1)}, bf16[40,64,128]{2,1,0:T(8,128)(2,1)}, u32[]{:S(2)}, u32[]{:S(2)}) collective-permute-start(bf16[40,64,128]{2,1,0:T(8,128)(2,1)} %get-tuple-element.19), channel_id=1, source_target_pairs={{126,128},{127,129},{128,126},{129,127}} | collective-permute-start | bytes 1966088 | tf_op jit(solution)/shard_map/ppermute | solution.py:171
  52.6 23.6 %collective-permute-start.1 = (bf16[40,64,128]{2,1,0:T(8,128)(2,1)}, bf16[40,64,128]{2,1,0:T(8,128)(2,1)}, u32[]{:S(2)}, u32[]{:S(2)}) collective-permute-start(bf16[40,64,128]{2,1,0:T(8,128)(2,1)} %collective-permute-done.rest_0_), channel_id=1, source_target_pairs={{0,1},{1,0},{2,3},{3,2},{4,5},{5,4},{6,7},{7,6},{8,9},{9,8},{10,11... | collective-permute-start | bytes 1966088 | tf_op jit(solution)/shard_map/ppermute | solution.py:183
  66.3 9.9 %collective-permute-start.9 = (bf16[40,64,128]{2,1,0:T(8,128)(2,1)S(1)}, bf16[40,64,128]{2,1,0:T(8,128)(2,1)S(1)}, u32[]{:S(2)}, u32[]{:S(2)}) collective-permute-start(bf16[40,64,128]{2,1,0:T(8,128)(2,1)S(1)} %broadcast_select_fusion.rest_2_), channel_id=1, source_target_pairs={{0,1},{1,0},{2,3},{3,2},{4,5},{5,4},{6,7},{7,6},{8,9},{9,8},{10,11... | collective-permute-start | bytes 1966088 | tf_op jit(solution)/shard_map/ppermute | solution.py:192
  68.1 8.1 %collective-permute-start.7 = (bf16[40,64,128]{2,1,0:T(8,128)(2,1)}, bf16[40,64,128]{2,1,0:T(8,128)(2,1)}, u32[]{:S(2)}, u32[]{:S(2)}) collective-permute-start(bf16[40,64,128]{2,1,0:T(8,128)(2,1)} %collective-permute-done.5.rest_1_), channel_id=1, source_target_pairs={{0,1},{1,0},{2,3},{3,2},{4,5},{5,4},{6,7},{7,6},{8,9},{9,8},{10,11... | collective-permute-start | bytes 1966088 | tf_op jit(solution)/shard_map/ppermute | solution.py:190

commit v3 on v2

--- a/solution.py
+++ b/solution.py
@@ -9,10 +9,11 @@
 
 HALF = 16
 TILES = 40
-ZERO = 6 * TILES
-
-
-def pack_body(start_ref, s_ref, first_ref, second_ref, both_ref):
+RAW = 6 * 2 * HALF
+ZERO = RAW + 2 * TILES
+
+
+def pack_body(start_ref, s_ref, first_ref, second_ref):
     def row(j, carry):
         for out_ref, base in places:
             for t in range(2):
@@ -29,19 +30,16 @@
     places = ((first_ref, HALF * start_ref[0]), (second_ref, HALF * (1 - start_ref[0])))
     lax.fori_loop(0, HALF, row, 0, unroll=4)
     lax.fori_loop(0, HALF // 2, pair, 0, unroll=4)
-    both_ref[:TILES] = first_ref[...]
-    both_ref[TILES:] = second_ref[...]
 
 
 def pack(start, s_blocks):
     piece = jax.ShapeDtypeStruct((TILES, 64, 128), jnp.bfloat16)
-    both = jax.ShapeDtypeStruct((2 * TILES, 64, 128), jnp.bfloat16)
     vmem = pl.BlockSpec(memory_space=pltpu.VMEM)
     return pl.pallas_call(
         pack_body,
-        out_shape=(piece, piece, both),
+        out_shape=(piece, piece),
         in_specs=[pl.BlockSpec(memory_space=pltpu.SMEM), vmem],
-        out_specs=(vmem,) * 3,
+        out_specs=(vmem,) * 2,
         compiler_params=pltpu.CompilerParams(vmem_limit_bytes=16 << 20),
         cost_estimate=pl.CostEstimate(flops=0, bytes_accessed=3 << 20, transcendentals=0),
     )(start, s_blocks)
@@ -52,15 +50,23 @@
     rows = l_ref.shape[0]
     base = 0
     for piece in rest[:count]:
-
-        def spread(t, carry, piece=piece, base=base):
-            v = piece[t]
-            sd_ref[base + 2 * t] = v
-            sd_ref[base + 2 * t + 1] = jnp.concatenate([v[:, 64:], v[:, :64]], axis=1)
+        packed = piece.shape[2] == 128
+
+        def spread(t, carry, piece=piece, base=base, packed=packed):
+            for u in range(1 if packed else 2):
+                v = piece[t, :, 128 * u : 128 * u + 128]
+                at = base + 2 * t if packed else base + 6 * t + 2 * u
+                sd_ref[at] = v
+                sd_ref[at + 1] = jnp.concatenate([v[:, 64:], v[:, :64]], axis=1)
+            if not packed:
+                v = piece[t, :, 256:320]
+                v = jnp.concatenate([v, v], axis=1)
+                sd_ref[base + 6 * t + 4] = v
+                sd_ref[base + 6 * t + 5] = v
             return carry
 
-        lax.fori_loop(0, piece.shape[0], spread, 0, unroll=8)
-        base += 2 * piece.shape[0]
+        lax.fori_loop(0, piece.shape[0], spread, 0, unroll=8 if packed else 4)
+        base += 2 * TILES if packed else RAW
     for zero in (ZERO, ZERO + 1):
         sd_ref[zero] = jnp.zeros((64, 128), jnp.bfloat16)
     part = part_ref[0]
@@ -88,7 +94,7 @@
         out(i).start()
         return carry
 
-    lax.fori_loop(0, rows, row, 0)
+    lax.fori_loop(0, rows, row, 0, unroll=True)
 
     def finish(i, carry):
         out(i).wait()
@@ -141,14 +147,16 @@
     want = want.astype(jnp.float32)
     d = flat - 32 * r
     part = lax.broadcasted_iota(jnp.int32, (rows * terms, kept), 1) // 6
-    remote = (part // 2 != h).astype(jnp.int32)
+    remote = part // 2 != h
     inside = (d >= 0) & (d < 32)
-    piece = jnp.where(inside, (d // HALF) ^ h ^ remote, 2)
+    piece = jnp.where(inside, (d // HALF) ^ h ^ 1, 2) * (2 * TILES)
     j = d & (HALF - 1)
+    odd = lax.broadcasted_iota(jnp.int32, (rows * terms, kept), 1) & 1
     where = jnp.full((rows * terms, kept), ZERO, jnp.int32)
-    odd = lax.broadcasted_iota(jnp.int32, (rows * terms, kept), 1) & 1
     for s in range(5):
-        place = piece * (2 * TILES) + (4 * j + s if s < 4 else 64 + j)
+        near_place = jnp.where(inside, 6 * d + s, RAW + (4 * j + s if s < 4 else 64 + j))
+        far_place = piece + (4 * j + s if s < 4 else 64 + j)
+        place = jnp.where(remote, far_place, near_place)
         where = jnp.where(cols[:, s * kept : (s + 1) * kept] == want, place, where)
     return (where ^ odd).reshape(rows * terms * kept)
 
@@ -170,21 +178,22 @@
     def send(x, perm):
         return lax.ppermute(x, ("rows", "cols"), perm)
 
-    first, second, both = pack(h.reshape(1), s_blocks)
+    first, second = pack(h.reshape(1), s_blocks)
     far_first = across(first)
     halo = send(second, up + down)
     seam_halo = send(first, seam)
+    mate, first = lax.optimization_barrier((s_blocks, first))
+    mate = beside(mate)
     tab = table(h, r, l_index, s_cols, c_index)
-    second, both, tab = lax.optimization_barrier((second, both, tab))
+    second, tab = lax.optimization_barrier((second, tab))
     far_second = across(second)
-    mate = beside(both)
 
     far_halo = send(far_first, plain)
     cross_first = beside(far_first)
     mate_halo = beside(halo)
     tab, far_first = lax.optimization_barrier((tab, far_first))
     parts = [(c ^ flip).reshape(1) for flip in range(4)]
-    out = product(tab, parts[0], l_blocks, (both, halo), None)
+    out = product(tab, parts[0], l_blocks, (s_blocks, halo), None)
     out = product(tab, parts[1], l_blocks, (mate, mate_halo), out)
     out, far_second, far_halo = lax.optimization_barrier((out, far_second, far_halo))
     cross_second = beside(far_second)

time: 84.6 us -> 85.2 us (level)
  starting transfers between devices: 26.4 us -> 18.4 us
  other arithmetic: 2.84 us -> 7.97 us
  local copies, waits for them, and re-layouts: 2.02 us -> 6.98 us
  Pallas kernels: 33.7 us -> 31.4 us
  matrix products: 1.4 us -> 2.77 us
  waiting for transfers between devices: 17.6 us -> 16.7 us
    ppermute x1, starting transfers between devices: 8.59 us -> 1.84 us  [shards(): far_first = across(first)]
    pallas_call x4, Pallas kernels: 31.8 us -> 28.4 us  [product(): pl.pallas_call(functools.partial(product_body, len(pieces)), out_shape=ja...]
    reshape x1, local copies, waits for them, and re-layouts: 0.11 us -> 1.61 us  [table(): return (where ^ odd).reshape(rows * terms * kept)]
    convert_element_type x2, local copies, waits for them, and re-layouts: 0.17 us -> 1.66 us  [table(): want = want.astype(jnp.float32)]
    xor x1, local copies, waits for them, and re-layouts: 0.1 us -> 1.48 us  [table(): return (where ^ odd).reshape(rows * terms * kept)]
    xor x1, other arithmetic: 0.1 us -> 1.45 us  [table(): return (where ^ odd).reshape(rows * terms * kept)]
    ppermute x1, starting transfers between devices: 1.34 us -> 0.01 us  [shards(): far_second = across(second)]
    ppermute x3, starting transfers between devices: 12.8 us -> 11.7 us  [send(): return lax.ppermute(x, ('rows', 'cols'), perm)]
  transfers between devices with their start and end apart: 10 -> 10, of which waited for: 2 -> 2; matrix products, arithmetic and copies ran while one was open for 1% -> 20% of each run, Pallas kernels for 28% -> 25%
where the time goes in v3:
time: 85.2 us; the launch traced here: 84.5 us
  Pallas kernels  31.4 us (37%)
  starting transfers between devices  18.4 us (22%)
  waiting for transfers between devices  16.7 us (20%)
  other arithmetic  7.97 us (9%)
  local copies, waits for them, and re-layouts  6.98 us (8%)
  matrix products  2.77 us (3%)
    pallas_call x4, Pallas kernels, product(): pl.pallas_call(functools.partial(product_body, len(pieces)), out_shape=ja...  28.4 us
    ppermute x3, waiting for transfers between devices, send(): return lax.ppermute(x, ('rows', 'cols'), perm)  16.6 us
    ppermute x3, starting transfers between devices, send(): return lax.ppermute(x, ('rows', 'cols'), perm)  11.7 us
    pallas_call x1, Pallas kernels, pack(): pl.pallas_call(pack_body, out_shape=(piece, piece), in_specs=[pl.BlockSpe...  3.05 us
    ppermute x1, starting transfers between devices, shards(): far_first = across(first)  1.84 us
  transfers between devices with their start and end apart: 10, of which 2 were waited for; matrix products, arithmetic and copies ran while one was open for 20% of the time, Pallas kernels for 25%

profile of v3, /device:TPU:3, one launch (start us, length us, event | category | flops | bytes accessed | tf_op | source)
XLA Modules:
  0.0 84.5 jit_solution(5455607272393171660)
XLA Ops:
  0.0 3.0 %shard_map.55 = (bf16[40,64,128]{2,1,0:T(8,128)(2,1)}, bf16[40,64,128]{2,1,0:T(8,128)(2,1)}) custom-call(s32[1]{0:T(128)} %bitcast.start_ref, bf16[32,64,320]{2,1,0:T(8,128)(2,1)} %rest_0_.1), custom_call_target="tpu_custom_call" | custom-call | bytes 3145728 | tf_op jit(solution)/shard_map/pallas_call | solution.py:38
  3.1 1.8 %collective-permute-start = (bf16[40,64,128]{2,1,0:T(8,128)(2,1)}, bf16[40,64,128]{2,1,0:T(8,128)(2,1)}, u32[]{:S(2)}, u32[]{:S(2)}) collective-permute-start(bf16[40,64,128]{2,1,0:T(8,128)(2,1)} %get-tuple-element.17), channel_id=1, source_target_pairs={{0,2},{1,3},{2,0},{3,1},{4,6},{5,7},{6,4},{7,5},{8,10},{9,11},{10,... | collective-permute-start | bytes 1966088 | tf_op jit(solution)/shard_map/ppermute | solution.py:182
  4.9 3.5 %collective-permute-start.3 = (bf16[40,64,128]{2,1,0:T(8,128)(2,1)}, bf16[40,64,128]{2,1,0:T(8,128)(2,1)}, u32[]{:S(2)}, u32[]{:S(2)}) collective-permute-start(bf16[40,64,128]{2,1,0:T(8,128)(2,1)} %get-tuple-element.20), channel_id=1, source_target_pairs={{0,4},{1,5},{4,8},{5,9},{8,12},{9,13},{12,16},{13,17},{16,20},{17,... | collective-permute-start | bytes 1966088 | tf_op jit(solution)/shard_map/ppermute | solution.py:179
  8.4 1.3 %collective-permute-start.2 = (bf16[32,64,320]{2,1,0:T(8,128)(2,1)}, bf16[32,64,320]{2,1,0:T(8,128)(2,1)S(1)}, u32[]{:S(2)}, u32[]{:S(2)}) collective-permute-start(bf16[32,64,320]{2,1,0:T(8,128)(2,1)} %rest_0_.1), channel_id=1, source_target_pairs={{0,1},{1,0},{2,3},{3,2},{4,5},{5,4},{6,7},{7,6},{8,9},{9,8},{10,11... | collective-permute-start | bytes 3932168 | tf_op jit(solution)/shard_map/ppermute | solution.py:186
  9.8 0.5 compare_and_fusion.2
  10.3 0.6 iota_divide_fusion.1
  11.4 0.6 iota_divide_fusion
  12.1 0.6 add_add_fusion.3
  12.7 1.7 %fusion.13 = f32[64,120]{1,0:T(8,128)} fusion(s32[2048,20]{0,1:T(8,128)} %param.8, s32[]{:T(128)S(6)} %min.4, s32[120]{0:T(128)} %get-tuple-element.44, s32[120]{0:T(128)} %get-tuple-element.46, s32[120]{0:T(128)} %get-tuple-element.45, s32[120]{0:T(128)} %get-tuple-element.47, pred[120]{0:T(512)(128)(4,1)S(1)} %get-tuple-element.42, ...), kind=kOutput, calls=%fused_computation.32 | convolution fusion | flops 1875680 | bytes 45692 | tf_op jit(solution)/shard_map/dot_general | solution.py:142
  14.9 0.6 compare_and_fusion.1
  15.5 0.7 sub.94
  16.2 0.7 convert_element_type.13
  16.9 0.7 broadcast_in_dim.69
  17.7 1.6 %convert_element_type.14 = f32[240,24]{0,1:T(8,128)} reshape(f32[8,30,24]{1,0,2:T(8,128)} %broadcast_in_dim.69) | data formatting | bytes 46080 | tf_op jit(solution)/shard_map/convert_element_type | solution.py:147
  19.3 0.7 add_select_fusion.6
  19.9 1.1 %fusion = f32[240,120]{0,1:T(8,128)S(1)} fusion(f32[64,120]{1,0:T(8,128)} %fusion.13, s32[240]{0:T(256)} %sub.94), kind=kOutput, calls=%fused_computation.2 | convolution fusion | flops 22133760 | bytes 146880 | tf_op jit(solution)/shard_map/dot_general | solution.py:145
  21.1 9.1 %collective-permute-done.3.rest_1_ = bf16[40,64,128]{2,1,0:T(8,128)(2,1)} collective-permute-done((bf16[40,64,128]{2,1,0:T(8,128)(2,1)}, bf16[40,64,128]{2,1,0:T(8,128)(2,1)}, u32[]{:S(2)}, u32[]{:S(2)}) %collective-permute-start.3) | collective-permute-done | bytes 655392 | tf_op jit(solution)/shard_map/ppermute | solution.py:179
  30.2 1.6 %collective-permute-start.4 = (bf16[40,64,128]{2,1,0:T(8,128)(2,1)}, bf16[40,64,128]{2,1,0:T(8,128)(2,1)}, u32[]{:S(2)}, u32[]{:S(2)}) collective-permute-start(bf16[40,64,128]{2,1,0:T(8,128)(2,1)} %collective-permute-done.3.rest_1_), channel_id=1, source_target_pairs={{0,1},{1,0},{2,3},{3,2},{4,5},{5,4},{6,7},{7,6},{8,9},{9,8},{10,11... | collective-permute-start | bytes 1966088 | tf_op jit(solution)/shard_map/ppermute | solution.py:193
  31.8 1.5 %select_xor_fusion = s32[240,24]{0,1:T(8,128)} fusion(f32[240,24]{0,1:T(8,128)} %convert_element_type.14, f32[240,120]{0,1:T(8,128)S(1)} %fusion, s32[24]{0:T(128)} %get-tuple-element.49, s32[240]{0:T(256)S(1)} %get-tuple-element.36, s32[240]{0:T(256)S(1)} %get-tuple-element.37, s32[240]{0:T(256)S(1)} %get-tuple-element.35, s32[240]{0:T(256)S(1)} %get-tuple-element.39, ...), kind=kLoop, calls=%fused_computation.21 | loop fusion | flops 190080 | bytes 171196 | tf_op jit(solution)/shard_map/xor | solution.py:161
  33.2 1.5 %copy.11 = s32[240,24]{1,0:T(8,128)} copy(s32[240,24]{0,1:T(8,128)} %select_xor_fusion) | data formatting | bytes 46080 | tf_op jit(solution)/shard_map/xor | solution.py:161
  34.7 1.6 %reshape.167.tab_ref = s32[5760]{0:T(1024)} reshape(s32[240,24]{1,0:T(8,128)} %copy.11) | data formatting | bytes 46080 | tf_op jit(solution)/shard_map/reshape | solution.py:161
  36.3 2.1 %collective-permute-start.6 = (bf16[40,64,128]{2,1,0:T(8,128)(2,1)}, bf16[40,64,128]{2,1,0:T(8,128)(2,1)}, u32[]{:S(2)}, u32[]{:S(2)}) collective-permute-start(bf16[40,64,128]{2,1,0:T(8,128)(2,1)} %collective-permute-done.rest_0_), channel_id=1, source_target_pairs={{0,4},{1,5},{4,8},{5,9},{8,12},{9,13},{12,16},{13,17},{16,20},{17,... | collective-permute-start | bytes 1966088 | tf_op jit(solution)/shard_map/ppermute | solution.py:179
  38.5 6.0 %collective-permute-start.8 = (bf16[40,64,128]{2,1,0:T(8,128)(2,1)}, bf16[40,64,128]{2,1,0:T(8,128)(2,1)}, u32[]{:S(2)}, u32[]{:S(2)}) collective-permute-start(bf16[40,64,128]{2,1,0:T(8,128)(2,1)} %get-tuple-element.17), channel_id=1, source_target_pairs={{126,128},{127,129},{128,126},{129,127}} | collective-permute-start | bytes 1966088 | tf_op jit(solution)/shard_map/ppermute | solution.py:179
  44.5 0.7 copy-done.1
  45.3 7.3 %shard_map.56.rest_2_ = bf16[8,64,1536]{2,1,0:T(8,128)(2,1)} custom-call(s32[5760]{0:T(1024)S(1)} %copy-done.1, s32[1]{0:T(128)} %bitcast.3.part_ref, bf16[8,64,1920]{2,1,0:T(8,128)(2,1)S(1)} %copy-done, bf16[32,64,320]{2,1,0:T(8,128)(2,1)} %rest_0_.1, bf16[40,64,128]{2,1,0:T(8,128)(2,1)} %collective-permute-done.3.rest_1_), custom_call_target="tpu_custom_call" | custom-call | flops 755000000 | bytes 20971520 | tf_op jit(solution)/shard_map/pallas_call | solution.py:116
  52.6 0.7 collective-permute-start.1
  53.3 6.9 %shard_map.57.rest_3_ = bf16[8,64,1536]{2,1,0:T(8,128)(2,1)} custom-call(s32[5760]{0:T(1024)S(1)} %copy-done.1, s32[1]{0:T(128)} %bitcast.2.part_ref, bf16[8,64,1920]{2,1,0:T(8,128)(2,1)S(1)} %copy-done, bf16[32,64,320]{2,1,0:T(8,128)(2,1)S(1)} %collective-permute-done.2.rest_0_, ...), custom_call_target="tpu_custom_call", output_to_operand_aliasing={{}: (5, {})} | custom-call | flops 755000000 | bytes 20971520 | tf_op jit(solution)/shard_map/pallas_call | solution.py:116
  60.2 7.5 %collective-permute-done.8 = bf16[40,64,128]{2,1,0:T(8,128)(2,1)} collective-permute-done((bf16[40,64,128]{2,1,0:T(8,128)(2,1)}, bf16[40,64,128]{2,1,0:T(8,128)(2,1)}, u32[]{:S(2)}, u32[]{:S(2)}) %collective-permute-start.8) | collective-permute-done | bytes 655392 | tf_op jit(solution)/shard_map/ppermute | solution.py:179
  67.7 1.2 %broadcast_select_fusion.rest_2_ = bf16[40,64,128]{2,1,0:T(8,128)(2,1)S(1)} fusion(bf16[40,64,128]{2,1,0:T(8,128)(2,1)} %collective-permute-done.8, bf16[40,64,128]{2,1,0:T(8,128)(2,1)} %collective-permute-done.6, pred[]{:T(512)S(6)} %or.3), kind=kLoop, calls=%fused_computation | loop fusion | flops 327680 | bytes 1966081 | tf_op jit(solution)/shard_map/jit(_where)/select_n | solution.py:200
  68.9 0.9 %collective-permute-start.9 = (bf16[40,64,128]{2,1,0:T(8,128)(2,1)S(1)}, bf16[40,64,128]{2,1,0:T(8,128)(2,1)S(1)}, u32[]{:S(2)}, u32[]{:S(2)}) collective-permute-start(bf16[40,64,128]{2,1,0:T(8,128)(2,1)S(1)} %broadcast_select_fusion.rest_2_), channel_id=1, source_target_pairs={{0,1},{1,0},{2,3},{3,2},{4,5},{5,4},{6,7},{7,6},{8,9},{9,8},{10,11... | collective-permute-start | bytes 1966088 | tf_op jit(solution)/shard_map/ppermute | solution.py:201
  70.1 7.1 %shard_map.58.rest_3_ = bf16[8,64,1536]{2,1,0:T(8,128)(2,1)} custom-call(s32[5760]{0:T(1024)S(1)} %copy-done.2, s32[1]{0:T(128)} %bitcast.4.part_ref, bf16[8,64,1920]{2,1,0:T(8,128)(2,1)S(1)} %copy-done, bf16[40,64,128]{2,1,0:T(8,128)(2,1)} %collective-permute-done.rest_0_, ...), custom_call_target="tpu_custom_call", output_to_operand_aliasing={{}: (6, {})} | custom-call | flops 755000000 | bytes 20971520 | tf_op jit(solution)/shard_map/pallas_call | solution.py:116
  77.2 7.1 %shard_map.59 = bf16[8,64,1536]{2,1,0:T(8,128)(2,1)} custom-call(s32[5760]{0:T(1024)S(1)} %copy-done.2, s32[1]{0:T(128)} %bitcast.1.part_ref, bf16[8,64,1920]{2,1,0:T(8,128)(2,1)S(1)} %copy-done, bf16[40,64,128]{2,1,0:T(8,128)(2,1)} %collective-permute-done.1.rest_0_, ...), custom_call_target="tpu_custom_call", output_to_operand_aliasing={{}: (6, {})} | custom-call | flops 755000000 | bytes 20971520 | tf_op jit(solution)/shard_map/pallas_call | solution.py:116
  (24 shorter events, 1.5 us)
Async XLA Ops:
  0.0 12.0 %copy-start.4 = (s32[8,30]{1,0:T(8,128)S(1)}, s32[8,30]{1,0:T(8,128)}, u32[]{:S(2)}) copy-start(s32[8,30]{1,0:T(8,128)} %param.7) | copy-start | bytes 2884
  0.0 44.5 %copy-start = (bf16[8,64,1920]{2,1,0:T(8,128)(2,1)S(1)}, bf16[8,64,1920]{2,1,0:T(8,128)(2,1)}, u32[]{:S(2)}) copy-start(bf16[8,64,1920]{2,1,0:T(8,128)(2,1)} %l_ref.7) | copy-start | bytes 5898244
  3.1 33.3 %collective-permute-start = (bf16[40,64,128]{2,1,0:T(8,128)(2,1)}, bf16[40,64,128]{2,1,0:T(8,128)(2,1)}, u32[]{:S(2)}, u32[]{:S(2)}) collective-permute-start(bf16[40,64,128]{2,1,0:T(8,128)(2,1)} %get-tuple-element.17), channel_id=1, source_target_pairs={{0,2},{1,3},{2,0},{3,1},{4,6},{5,7},{6,4},{7,5},{8,10},{9,11},{10,... | collective-permute-start | bytes 1966088 | tf_op jit(solution)/shard_map/ppermute | solution.py:182
  4.9 25.3 %collective-permute-start.3 = (bf16[40,64,128]{2,1,0:T(8,128)(2,1)}, bf16[40,64,128]{2,1,0:T(8,128)(2,1)}, u32[]{:S(2)}, u32[]{:S(2)}) collective-permute-start(bf16[40,64,128]{2,1,0:T(8,128)(2,1)} %get-tuple-element.20), channel_id=1, source_target_pairs={{0,4},{1,5},{4,8},{5,9},{8,12},{9,13},{12,16},{13,17},{16,20},{17,... | collective-permute-start | bytes 1966088 | tf_op jit(solution)/shard_map/ppermute | solution.py:179
  8.4 44.2 %collective-permute-start.2 = (bf16[32,64,320]{2,1,0:T(8,128)(2,1)}, bf16[32,64,320]{2,1,0:T(8,128)(2,1)S(1)}, u32[]{:S(2)}, u32[]{:S(2)}) collective-permute-start(bf16[32,64,320]{2,1,0:T(8,128)(2,1)} %rest_0_.1), channel_id=1, source_target_pairs={{0,1},{1,0},{2,3},{3,2},{4,5},{5,4},{6,7},{7,6},{8,9},{9,8},{10,11... | collective-permute-start | bytes 3932168 | tf_op jit(solution)/shard_map/ppermute | solution.py:186
  12.1 4.1 %copy-start.3 = (s32[240]{0:T(256)}, s32[240]{0:T(256)S(1)}, u32[]{:S(2)}) copy-start(s32[240]{0:T(256)S(1)} %sub.101) | copy-start | bytes 2884
  30.2 23.1 %collective-permute-start.4 = (bf16[40,64,128]{2,1,0:T(8,128)(2,1)}, bf16[40,64,128]{2,1,0:T(8,128)(2,1)}, u32[]{:S(2)}, u32[]{:S(2)}) collective-permute-start(bf16[40,64,128]{2,1,0:T(8,128)(2,1)} %collective-permute-done.3.rest_1_), channel_id=1, source_target_pairs={{0,1},{1,0},{2,3},{3,2},{4,5},{5,4},{6,7},{7,6},{8,9},{9,8},{10,11... | collective-permute-start | bytes 1966088 | tf_op jit(solution)/shard_map/ppermute | solution.py:193
  36.3 23.8 %collective-permute-start.5 = (bf16[40,64,128]{2,1,0:T(8,128)(2,1)}, bf16[40,64,128]{2,1,0:T(8,128)(2,1)}, u32[]{:S(2)}, u32[]{:S(2)}) collective-permute-start(bf16[40,64,128]{2,1,0:T(8,128)(2,1)} %get-tuple-element.20), channel_id=1, source_target_pairs={{0,2},{1,3},{2,0},{3,1},{4,6},{5,7},{6,4},{7,5},{8,10},{9,11},{10,... | collective-permute-start | bytes 1966088 | tf_op jit(solution)/shard_map/ppermute | solution.py:189
  36.3 23.8 %collective-permute-start.6 = (bf16[40,64,128]{2,1,0:T(8,128)(2,1)}, bf16[40,64,128]{2,1,0:T(8,128)(2,1)}, u32[]{:S(2)}, u32[]{:S(2)}) collective-permute-start(bf16[40,64,128]{2,1,0:T(8,128)(2,1)} %collective-permute-done.rest_0_), channel_id=1, source_target_pairs={{0,4},{1,5},{4,8},{5,9},{8,12},{9,13},{12,16},{13,17},{16,20},{17,... | collective-permute-start | bytes 1966088 | tf_op jit(solution)/shard_map/ppermute | solution.py:179
  38.5 29.2 %collective-permute-start.8 = (bf16[40,64,128]{2,1,0:T(8,128)(2,1)}, bf16[40,64,128]{2,1,0:T(8,128)(2,1)}, u32[]{:S(2)}, u32[]{:S(2)}) collective-permute-start(bf16[40,64,128]{2,1,0:T(8,128)(2,1)} %get-tuple-element.17), channel_id=1, source_target_pairs={{126,128},{127,129},{128,126},{129,127}} | collective-permute-start | bytes 1966088 | tf_op jit(solution)/shard_map/ppermute | solution.py:179
  44.5 0.7 copy-start.1
  52.6 24.6 %collective-permute-start.1 = (bf16[40,64,128]{2,1,0:T(8,128)(2,1)}, bf16[40,64,128]{2,1,0:T(8,128)(2,1)}, u32[]{:S(2)}, u32[]{:S(2)}) collective-permute-start(bf16[40,64,128]{2,1,0:T(8,128)(2,1)} %collective-permute-done.rest_0_), channel_id=1, source_target_pairs={{0,1},{1,0},{2,3},{3,2},{4,5},{5,4},{6,7},{7,6},{8,9},{9,8},{10,11... | collective-permute-start | bytes 1966088 | tf_op jit(solution)/shard_map/ppermute | solution.py:192
  60.2 9.9 %copy-start.2 = (s32[5760]{0:T(1024)S(1)}, s32[5760]{0:T(1024)}, u32[]{:S(2)}) copy-start(s32[5760]{0:T(1024)} %reshape.167.tab_ref) | copy-start | bytes 69124
  68.9 8.3 %collective-permute-start.9 = (bf16[40,64,128]{2,1,0:T(8,128)(2,1)S(1)}, bf16[40,64,128]{2,1,0:T(8,128)(2,1)S(1)}, u32[]{:S(2)}, u32[]{:S(2)}) collective-permute-start(bf16[40,64,128]{2,1,0:T(8,128)(2,1)S(1)} %broadcast_select_fusion.rest_2_), channel_id=1, source_target_pairs={{0,1},{1,0},{2,3},{3,2},{4,5},{5,4},{6,7},{7,6},{8,9},{9,8},{10,11... | collective-permute-start | bytes 1966088 | tf_op jit(solution)/shard_map/ppermute | solution.py:201
  69.8 7.4 %collective-permute-start.7 = (bf16[40,64,128]{2,1,0:T(8,128)(2,1)}, bf16[40,64,128]{2,1,0:T(8,128)(2,1)}, u32[]{:S(2)}, u32[]{:S(2)}) collective-permute-start(bf16[40,64,128]{2,1,0:T(8,128)(2,1)} %collective-permute-done.5.rest_1_), channel_id=1, source_target_pairs={{0,1},{1,0},{2,3},{3,2},{4,5},{5,4},{6,7},{7,6},{8,9},{9,8},{10,11... | collective-permute-start | bytes 1966088 | tf_op jit(solution)/shard_map/ppermute | solution.py:199

commit v4 on v3

--- a/solution.py
+++ b/solution.py
@@ -78,7 +78,7 @@
 
     def row(i, carry):
         def pick(k, m):
-            at = (i * 30 + k) * 24 + part * 6 + 2 * m
+            at = (k // 5 * 8 + i) * 128 + k % 5 * 24 + part * 6 + 2 * m
             return jnp.where(low, sd_ref[tab_ref[at]], sd_ref[tab_ref[at + 1]])
 
         total = jnp.zeros((64, 384), jnp.float32)
@@ -129,36 +129,76 @@
     )(*args)
 
 
+def split(v):
+    return [x.astype(jnp.float32).astype(jnp.bfloat16) for x in (v >> 6, v & 63)]
+
+
+def exact(a, b, dims):
+    return lax.dot_general(a, b, (dims, ((), ())), preferred_element_type=jnp.float32)
+
+
+def table_body(at_ref, near_ref, l_ref, c_ref, tab_ref):
+    start, first, h = at_ref[0], at_ref[1], at_ref[2]
+
+    def places(shape, dim):
+        lane = lax.broadcasted_iota(jnp.int32, shape, dim)
+        k = sum((lane >= 24 * t).astype(jnp.int32) for t in range(1, 5))
+        m = lane - 24 * k
+        return k, m, sum((m >= 6 * t).astype(jnp.int32) for t in range(1, 4))
+
+    k_of, m_of, part = places((48, 128), 1)
+    _, m_wide, _ = places((24, 128), 1)
+    tile = (lax.broadcasted_iota(jnp.int32, (24, 128), 0) == m_wide).astype(jnp.float32).astype(jnp.bfloat16)
+    want = [exact(x, tile, ((1,), (0,))) for x in split(c_ref[...])]
+    want = jnp.concatenate([want[0] * 64.0 + want[1]] * 6, axis=0)
+
+    _, _, part_tall = places((128, 20), 0)
+    column = lax.broadcasted_iota(jnp.int32, (128, 20), 1)
+    slots = []
+    for x in split(near_ref[...]):
+        for s in range(5):
+            pick = (column == 5 * part_tall + s).astype(jnp.float32).astype(jnp.bfloat16)
+            slots.append(exact(pick, x, ((1,), (0,))).astype(jnp.bfloat16))
+    slots = jnp.concatenate(slots, axis=0)
+
+    cols = jnp.zeros((48, 1280), jnp.float32)
+    d = jnp.zeros((48, 128), jnp.int32)
+    wide = jnp.concatenate([k_of] * 10, axis=1)
+    for t in range(5):
+        ids = jnp.concatenate([l_ref[:, 5 * g + t : 5 * g + t + 1] for g in range(6)], axis=0)
+        hot = ids - start == lax.broadcasted_iota(jnp.int32, (48, near_ref.shape[1]), 1)
+        hot = hot.astype(jnp.float32).astype(jnp.bfloat16)
+        cols = jnp.where(wide == t, exact(hot, slots, ((1,), (1,))), cols)
+        d = jnp.where(k_of == t, ids - first, d)
+
+    remote = (part >> 1) != h
+    inside = (d >= 0) & (d < 2 * HALF)
+    piece = jnp.where(inside, (d >> 4) ^ h ^ 1, 2) * (2 * TILES)
+    j = d & (HALF - 1)
+    where = jnp.full((48, 128), ZERO, jnp.int32)
+    for s in range(5):
+        packed = 4 * j + s if s < 4 else 2 * TILES - HALF + j
+        place = jnp.where(remote, piece + packed, jnp.where(inside, 6 * d + s, RAW + packed))
+        got = cols[:, 128 * s : 128 * s + 128] * 64.0 + cols[:, 640 + 128 * s : 768 + 128 * s]
+        where = jnp.where(got == want, place, where)
+    tab_ref[...] = where ^ (m_of & 1)
+
+
 def table(h, r, l_index, s_cols, c_index):
     total = s_cols.shape[0]
-    rows, terms = l_index.shape
-    kept = c_index.shape[1]
-    near = 4 * HALF
-    w0 = jnp.clip(32 * r - HALF, 0, total - near)
-    window = lax.dynamic_slice_in_dim(s_cols, w0, near, axis=0).astype(jnp.float32)
-    lane = lax.broadcasted_iota(jnp.int32, (20, 5 * kept), 1)
-    source = (lane % kept) // 6 * 5 + lane // kept
-    spread = (source == lax.broadcasted_iota(jnp.int32, (20, 5 * kept), 0)).astype(jnp.float32)
-    slots = jnp.dot(window, spread, precision=lax.Precision.HIGHEST)
-    flat = l_index.reshape(rows * terms, 1)
-    hot = (flat - w0 == lax.broadcasted_iota(jnp.int32, (rows * terms, near), 1)).astype(jnp.float32)
-    cols = jnp.dot(hot, slots, precision=lax.Precision.HIGHEST)
-    want = jnp.broadcast_to(c_index[:, None, :], (rows, terms, kept)).reshape(rows * terms, kept)
-    want = want.astype(jnp.float32)
-    d = flat - 32 * r
-    part = lax.broadcasted_iota(jnp.int32, (rows * terms, kept), 1) // 6
-    remote = part // 2 != h
-    inside = (d >= 0) & (d < 32)
-    piece = jnp.where(inside, (d // HALF) ^ h ^ 1, 2) * (2 * TILES)
-    j = d & (HALF - 1)
-    odd = lax.broadcasted_iota(jnp.int32, (rows * terms, kept), 1) & 1
-    where = jnp.full((rows * terms, kept), ZERO, jnp.int32)
-    for s in range(5):
-        near_place = jnp.where(inside, 6 * d + s, RAW + (4 * j + s if s < 4 else 64 + j))
-        far_place = piece + (4 * j + s if s < 4 else 64 + j)
-        place = jnp.where(remote, far_place, near_place)
-        where = jnp.where(cols[:, s * kept : (s + 1) * kept] == want, place, where)
-    return (where ^ odd).reshape(rows * terms * kept)
+    first = 2 * HALF * r
+    start = jnp.clip(first - HALF, 0, total - 4 * HALF)
+    near = lax.dynamic_slice_in_dim(s_cols, start, 4 * HALF, axis=0).T
+    vmem = pl.BlockSpec(memory_space=pltpu.VMEM)
+    out = pl.pallas_call(
+        table_body,
+        out_shape=jax.ShapeDtypeStruct((48, 128), jnp.int32),
+        in_specs=[pl.BlockSpec(memory_space=pltpu.SMEM), vmem, vmem, vmem],
+        out_specs=vmem,
+        compiler_params=pltpu.CompilerParams(vmem_limit_bytes=8 << 20),
+        cost_estimate=pl.CostEstimate(flops=1 << 28, bytes_accessed=8 << 20, transcendentals=0),
+    )(jnp.stack([start, first, h]), near, l_index, c_index)
+    return out.reshape(48 * 128)
 
 
 def shards(l_blocks, s_blocks, l_index, s_cols, c_index):
@@ -185,13 +225,13 @@
     mate, first = lax.optimization_barrier((s_blocks, first))
     mate = beside(mate)
     tab = table(h, r, l_index, s_cols, c_index)
-    second, tab = lax.optimization_barrier((second, tab))
+    second, halo, tab = lax.optimization_barrier((second, halo, tab))
     far_second = across(second)
 
     far_halo = send(far_first, plain)
     cross_first = beside(far_first)
     mate_halo = beside(halo)
-    tab, far_first = lax.optimization_barrier((tab, far_first))
+    tab, far_first, seam_halo = lax.optimization_barrier((tab, far_first, seam_halo))
     parts = [(c ^ flip).reshape(1) for flip in range(4)]
     out = product(tab, parts[0], l_blocks, (s_blocks, halo), None)
     out = product(tab, parts[1], l_blocks, (mate, mate_halo), out)

time: 85.2 us -> 80.4 us (0.944)
  starting transfers between devices: 18.4 us -> 26.9 us
  local copies, waits for them, and re-layouts: 6.98 us -> 0.1 us
  other arithmetic: 7.97 us -> 1.24 us
  matrix products: 2.77 us -> 0 us
  waiting for transfers between devices: 16.7 us -> 18.7 us
  Pallas kernels: 31.4 us -> 32.9 us
    ppermute x1, starting transfers between devices: 1.84 us -> 8.52 us  [shards(): far_first = across(first)]
    ppermute x1, starting transfers between devices: 0.01 us -> 4.89 us  [shards(): far_second = across(second)]
    ppermute x3, starting transfers between devices: 11.7 us -> 7.59 us  [send(): return lax.ppermute(x, ('rows', 'cols'), perm)]
    dot_general x2 -> x0, matrix products: 2.77 us -> none  [the longest x1 1.66 us: table(): slots = jnp.dot(window, spread, precision=lax.Precision.HIGHEST)]
    ppermute x3, waiting for transfers between devices: 16.6 us -> 18.7 us  [send(): return lax.ppermute(x, ('rows', 'cols'), perm)]
    convert_element_type x2 -> x0, local copies, waits for them, and re-layouts: 1.66 us -> none  [table(): want = want.astype(jnp.float32)]
    reshape x1 -> x0, local copies, waits for them, and re-layouts: 1.61 us -> none  [table(): return (where ^ odd).reshape(rows * terms * kept)]
    xor x1 -> x0, local copies, waits for them, and re-layouts: 1.48 us -> none  [table(): return (where ^ odd).reshape(rows * terms * kept)]
  transfers between devices with their start and end apart: 10 -> 10, of which waited for: 2 -> 2; matrix products, arithmetic and copies ran while one was open for 20% -> 2% of each run, Pallas kernels for 25% -> 28%
where the time goes in v4:
time: 80.4 us; the launch traced here: 80.1 us
  Pallas kernels  32.9 us (41%)
  starting transfers between devices  26.9 us (33%)
  waiting for transfers between devices  18.7 us (23%)
  other arithmetic  1.24 us (2%)
    pallas_call x4, Pallas kernels, product(): pl.pallas_call(functools.partial(product_body, len(pieces)), out_shape=ja...  28.6 us
    ppermute x3, waiting for transfers between devices, send(): return lax.ppermute(x, ('rows', 'cols'), perm)  18.7 us
    ppermute x1, starting transfers between devices, shards(): far_first = across(first)  8.52 us
    ppermute x3, starting transfers between devices, send(): return lax.ppermute(x, ('rows', 'cols'), perm)  7.59 us
    ppermute x1, starting transfers between devices, shards(): far_second = across(second)  4.89 us
    pallas_call x1, Pallas kernels, pack(): pl.pallas_call(pack_body, out_shape=(piece, piece), in_specs=[pl.BlockSpe...  3.02 us
    ppermute x1, starting transfers between devices, shards(): mate_halo = beside(halo)  2.21 us
    ppermute x1, starting transfers between devices, shards(): cross_first = beside(far_first)  2.02 us
  transfers between devices with their start and end apart: 10, of which 2 were waited for; matrix products, arithmetic and copies ran while one was open for 2% of the time, Pallas kernels for 28%

profile of v4, /device:TPU:3, one launch (start us, length us, event | category | flops | bytes accessed | tf_op | source)
XLA Modules:
  0.0 80.1 jit_solution(1419332384100435668)
XLA Ops:
  0.0 0.0 copy-start
  0.0 0.0 copy-start.1
  0.0 3.0 %shard_map.55 = (bf16[40,64,128]{2,1,0:T(8,128)(2,1)}, bf16[40,64,128]{2,1,0:T(8,128)(2,1)}) custom-call(s32[1]{0:T(128)} %bitcast.start_ref, bf16[32,64,320]{2,1,0:T(8,128)(2,1)} %rest_0_.1), custom_call_target="tpu_custom_call" | custom-call | bytes 3145728 | tf_op jit(solution)/shard_map/pallas_call | solution.py:38
  3.1 3.5 %collective-permute-start = (bf16[40,64,128]{2,1,0:T(8,128)(2,1)}, bf16[40,64,128]{2,1,0:T(8,128)(2,1)S(1)}, u32[]{:S(2)}, u32[]{:S(2)}) collective-permute-start(bf16[40,64,128]{2,1,0:T(8,128)(2,1)} %get-tuple-element.23), channel_id=1, source_target_pairs={{0,4},{1,5},{4,8},{5,9},{8,12},{9,13},{12,16},{13,17},{16,20},{17,... | collective-permute-start | bytes 1966088 | tf_op jit(solution)/shard_map/ppermute | solution.py:219
  6.6 1.0 %collective-permute-start.4 = (bf16[32,64,320]{2,1,0:T(8,128)(2,1)}, bf16[32,64,320]{2,1,0:T(8,128)(2,1)}, u32[]{:S(2)}, u32[]{:S(2)}) collective-permute-start(bf16[32,64,320]{2,1,0:T(8,128)(2,1)} %rest_0_.1), channel_id=1, source_target_pairs={{0,1},{1,0},{2,3},{3,2},{4,5},{5,4},{6,7},{7,6},{8,9},{9,8},{10,11... | collective-permute-start | bytes 3932168 | tf_op jit(solution)/shard_map/ppermute | solution.py:226
  7.6 8.5 %collective-permute-start.1 = (bf16[40,64,128]{2,1,0:T(8,128)(2,1)}, bf16[40,64,128]{2,1,0:T(8,128)(2,1)}, u32[]{:S(2)}, u32[]{:S(2)}) collective-permute-start(bf16[40,64,128]{2,1,0:T(8,128)(2,1)} %get-tuple-element.19), channel_id=1, source_target_pairs={{0,2},{1,3},{2,0},{3,1},{4,6},{5,7},{6,4},{7,5},{8,10},{9,11},{10,... | collective-permute-start | bytes 1966088 | tf_op jit(solution)/shard_map/ppermute | solution.py:222
  16.2 1.9 %collective-permute-start.2 = (bf16[40,64,128]{2,1,0:T(8,128)(2,1)}, bf16[40,64,128]{2,1,0:T(8,128)(2,1)}, u32[]{:S(2)}, u32[]{:S(2)}) collective-permute-start(bf16[40,64,128]{2,1,0:T(8,128)(2,1)} %get-tuple-element.19), channel_id=1, source_target_pairs={{126,128},{127,129},{128,126},{129,127}} | collective-permute-start | bytes 1966088 | tf_op jit(solution)/shard_map/ppermute | solution.py:219
  18.1 0.0 copy-done
  18.1 0.1 dynamic-slice_bitcast_fusion.near_ref
  18.2 0.1 pad_add_fusion.at_ref
  18.3 1.3 %shard_map.56 = s32[48,128]{1,0:T(8,128)S(1)} custom-call(s32[3]{0:T(128)S(1)} %pad_add_fusion.at_ref, s32[20,64]{1,0:T(8,128)S(1)} %dynamic-slice_bitcast_fusion.near_ref, s32[8,30]{1,0:T(8,128)S(1)} %copy-done.2, s32[8,24]{1,0:T(8,128)S(1)} %copy-done.3), custom_call_target="tpu_custom_call" | custom-call | flops 268435456 | bytes 8388608 | tf_op jit(solution)/shard_map/pallas_call | solution.py:193
  19.6 10.1 %collective-permute-done.rest_1_ = bf16[40,64,128]{2,1,0:T(8,128)(2,1)S(1)} collective-permute-done((bf16[40,64,128]{2,1,0:T(8,128)(2,1)}, bf16[40,64,128]{2,1,0:T(8,128)(2,1)S(1)}, u32[]{:S(2)}, u32[]{:S(2)}) %collective-permute-start) | collective-permute-done | bytes 655392 | tf_op jit(solution)/shard_map/ppermute | solution.py:219
  29.7 2.2 %collective-permute-start.5 = (bf16[40,64,128]{2,1,0:T(8,128)(2,1)S(1)}, bf16[40,64,128]{2,1,0:T(8,128)(2,1)S(1)}, u32[]{:S(2)}, u32[]{:S(2)}) collective-permute-start(bf16[40,64,128]{2,1,0:T(8,128)(2,1)S(1)} %collective-permute-done.rest_1_), channel_id=1, source_target_pairs={{0,1},{1,0},{2,3},{3,2},{4,5},{5,4},{6,7},{7,6},{8,9},{9,8},{10,11... | collective-permute-start | bytes 1966088 | tf_op jit(solution)/shard_map/ppermute | solution.py:233
  31.9 4.9 %collective-permute-start.6 = (bf16[40,64,128]{2,1,0:T(8,128)(2,1)}, bf16[40,64,128]{2,1,0:T(8,128)(2,1)}, u32[]{:S(2)}, u32[]{:S(2)}) collective-permute-start(bf16[40,64,128]{2,1,0:T(8,128)(2,1)} %get-tuple-element.23), channel_id=1, source_target_pairs={{0,2},{1,3},{2,0},{3,1},{4,6},{5,7},{6,4},{7,5},{8,10},{9,11},{10,... | collective-permute-start | bytes 1966088 | tf_op jit(solution)/shard_map/ppermute | solution.py:229
  36.8 0.0 collective-permute-done.1.rest_0_
  36.8 2.1 %collective-permute-start.7 = (bf16[40,64,128]{2,1,0:T(8,128)(2,1)}, bf16[40,64,128]{2,1,0:T(8,128)(2,1)}, u32[]{:S(2)}, u32[]{:S(2)}) collective-permute-start(bf16[40,64,128]{2,1,0:T(8,128)(2,1)} %collective-permute-done.1.rest_0_), channel_id=1, source_target_pairs={{0,4},{1,5},{4,8},{5,9},{8,12},{9,13},{12,16},{13,17},{16,20},{17,... | collective-permute-start | bytes 1966088 | tf_op jit(solution)/shard_map/ppermute | solution.py:219
  38.9 8.6 %collective-permute-done.2 = bf16[40,64,128]{2,1,0:T(8,128)(2,1)} collective-permute-done((bf16[40,64,128]{2,1,0:T(8,128)(2,1)}, bf16[40,64,128]{2,1,0:T(8,128)(2,1)}, u32[]{:S(2)}, u32[]{:S(2)}) %collective-permute-start.2) | collective-permute-done | bytes 655392 | tf_op jit(solution)/shard_map/ppermute | solution.py:219
  47.5 2.0 %collective-permute-start.3 = (bf16[40,64,128]{2,1,0:T(8,128)(2,1)}, bf16[40,64,128]{2,1,0:T(8,128)(2,1)}, u32[]{:S(2)}, u32[]{:S(2)}) collective-permute-start(bf16[40,64,128]{2,1,0:T(8,128)(2,1)} %collective-permute-done.1.rest_0_), channel_id=1, source_target_pairs={{0,1},{1,0},{2,3},{3,2},{4,5},{5,4},{6,7},{7,6},{8,9},{9,8},{10,11... | collective-permute-start | bytes 1966088 | tf_op jit(solution)/shard_map/ppermute | solution.py:232
  49.5 7.2 %shard_map.57.rest_2_ = bf16[8,64,1536]{2,1,0:T(8,128)(2,1)} custom-call(s32[6144]{0:T(1024)S(1)} %bitcast.10, s32[1]{0:T(128)} %bitcast.7.part_ref, bf16[8,64,1920]{2,1,0:T(8,128)(2,1)S(1)} %copy-done.1, bf16[32,64,320]{2,1,0:T(8,128)(2,1)} %rest_0_.1, bf16[40,64,128]{2,1,0:T(8,128)(2,1)S(1)} %collective-permute-done.rest_1_), custom_call_target="tpu_custom_call" | custom-call | flops 755000000 | bytes 20971520 | tf_op jit(solution)/shard_map/pallas_call | solution.py:116
  56.7 0.0 collective-permute-done.4.rest_0_
  56.7 0.0 collective-permute-done.5.rest_1_
  56.7 7.2 %shard_map.58.rest_3_ = bf16[8,64,1536]{2,1,0:T(8,128)(2,1)} custom-call(s32[6144]{0:T(1024)S(1)} %bitcast.11, s32[1]{0:T(128)} %bitcast.6.part_ref, bf16[8,64,1920]{2,1,0:T(8,128)(2,1)S(1)} %copy-done.1, bf16[32,64,320]{2,1,0:T(8,128)(2,1)} %collective-permute-done.4.rest_0_, ...), custom_call_target="tpu_custom_call", output_to_operand_aliasing={{}: (5, {})} | custom-call | flops 755000000 | bytes 20971520 | tf_op jit(solution)/shard_map/pallas_call | solution.py:116
  63.9 0.0 collective-permute-done.6.rest_1_
  63.9 0.0 collective-permute-done.7
  63.9 1.2 %broadcast_select_fusion.rest_2_ = bf16[40,64,128]{2,1,0:T(8,128)(2,1)S(1)} fusion(bf16[40,64,128]{2,1,0:T(8,128)(2,1)} %collective-permute-done.2, bf16[40,64,128]{2,1,0:T(8,128)(2,1)} %collective-permute-done.7, pred[]{:T(512)S(6)} %or.3), kind=kLoop, calls=%fused_computation | loop fusion | flops 327680 | bytes 1966081 | tf_op jit(solution)/shard_map/jit(_where)/select_n | solution.py:240
  65.1 0.1 collective-permute-start.9
  65.2 0.5 collective-permute-start.8
  65.7 7.1 %shard_map.59.rest_3_ = bf16[8,64,1536]{2,1,0:T(8,128)(2,1)} custom-call(s32[6144]{0:T(1024)S(1)} %bitcast.12, s32[1]{0:T(128)} %bitcast.8.part_ref, bf16[8,64,1920]{2,1,0:T(8,128)(2,1)S(1)} %copy-done.1, bf16[40,64,128]{2,1,0:T(8,128)(2,1)} %collective-permute-done.1.rest_0_, ...), custom_call_target="tpu_custom_call", output_to_operand_aliasing={{}: (6, {})} | custom-call | flops 755000000 | bytes 20971520 | tf_op jit(solution)/shard_map/pallas_call | solution.py:116
  72.8 0.0 collective-permute-done.3.rest_0_
  72.8 0.0 collective-permute-done.9.rest_2_
  72.8 0.0 collective-permute-done.8.rest_1_
  72.9 7.1 %shard_map.60 = bf16[8,64,1536]{2,1,0:T(8,128)(2,1)} custom-call(s32[6144]{0:T(1024)S(1)} %bitcast.13, s32[1]{0:T(128)} %bitcast.5.part_ref, bf16[8,64,1920]{2,1,0:T(8,128)(2,1)S(1)} %copy-done.1, bf16[40,64,128]{2,1,0:T(8,128)(2,1)} %collective-permute-done.3.rest_0_, ...), custom_call_target="tpu_custom_call", output_to_operand_aliasing={{}: (6, {})} | custom-call | flops 755000000 | bytes 20971520 | tf_op jit(solution)/shard_map/pallas_call | solution.py:116
  (5 shorter events, 0.0 us)
Async XLA Ops:
  0.0 18.1 %copy-start = (s32[2048,20]{0,1:T(8,128)S(1)}, s32[2048,20]{0,1:T(8,128)}, u32[]{:S(2)}) copy-start(s32[2048,20]{0,1:T(8,128)} %param.8) | copy-start | bytes 491524
  0.0 18.3 %copy-start.2 = (s32[8,30]{1,0:T(8,128)S(1)}, s32[8,30]{1,0:T(8,128)}, u32[]{:S(2)}) copy-start(s32[8,30]{1,0:T(8,128)} %l_ref.5) | copy-start | bytes 2884
  0.0 18.3 %copy-start.3 = (s32[8,24]{1,0:T(8,128)S(1)}, s32[8,24]{1,0:T(8,128)}, u32[]{:S(2)}) copy-start(s32[8,24]{1,0:T(8,128)} %c_ref.1) | copy-start | bytes 2308
  0.0 49.5 %copy-start.1 = (bf16[8,64,1920]{2,1,0:T(8,128)(2,1)S(1)}, bf16[8,64,1920]{2,1,0:T(8,128)(2,1)}, u32[]{:S(2)}) copy-start(bf16[8,64,1920]{2,1,0:T(8,128)(2,1)} %l_ref.9) | copy-start | bytes 5898244
  3.1 26.6 %collective-permute-start = (bf16[40,64,128]{2,1,0:T(8,128)(2,1)}, bf16[40,64,128]{2,1,0:T(8,128)(2,1)S(1)}, u32[]{:S(2)}, u32[]{:S(2)}) collective-permute-start(bf16[40,64,128]{2,1,0:T(8,128)(2,1)} %get-tuple-element.23), channel_id=1, source_target_pairs={{0,4},{1,5},{4,8},{5,9},{8,12},{9,13},{12,16},{13,17},{16,20},{17,... | collective-permute-start | bytes 1966088 | tf_op jit(solution)/shard_map/ppermute | solution.py:219
  6.6 50.1 %collective-permute-start.4 = (bf16[32,64,320]{2,1,0:T(8,128)(2,1)}, bf16[32,64,320]{2,1,0:T(8,128)(2,1)}, u32[]{:S(2)}, u32[]{:S(2)}) collective-permute-start(bf16[32,64,320]{2,1,0:T(8,128)(2,1)} %rest_0_.1), channel_id=1, source_target_pairs={{0,1},{1,0},{2,3},{3,2},{4,5},{5,4},{6,7},{7,6},{8,9},{9,8},{10,11... | collective-permute-start | bytes 3932168 | tf_op jit(solution)/shard_map/ppermute | solution.py:226
  7.6 29.1 %collective-permute-start.1 = (bf16[40,64,128]{2,1,0:T(8,128)(2,1)}, bf16[40,64,128]{2,1,0:T(8,128)(2,1)}, u32[]{:S(2)}, u32[]{:S(2)}) collective-permute-start(bf16[40,64,128]{2,1,0:T(8,128)(2,1)} %get-tuple-element.19), channel_id=1, source_target_pairs={{0,2},{1,3},{2,0},{3,1},{4,6},{5,7},{6,4},{7,5},{8,10},{9,11},{10,... | collective-permute-start | bytes 1966088 | tf_op jit(solution)/shard_map/ppermute | solution.py:222
  16.2 31.3 %collective-permute-start.2 = (bf16[40,64,128]{2,1,0:T(8,128)(2,1)}, bf16[40,64,128]{2,1,0:T(8,128)(2,1)}, u32[]{:S(2)}, u32[]{:S(2)}) collective-permute-start(bf16[40,64,128]{2,1,0:T(8,128)(2,1)} %get-tuple-element.19), channel_id=1, source_target_pairs={{126,128},{127,129},{128,126},{129,127}} | collective-permute-start | bytes 1966088 | tf_op jit(solution)/shard_map/ppermute | solution.py:219
  29.7 27.1 %collective-permute-start.5 = (bf16[40,64,128]{2,1,0:T(8,128)(2,1)S(1)}, bf16[40,64,128]{2,1,0:T(8,128)(2,1)S(1)}, u32[]{:S(2)}, u32[]{:S(2)}) collective-permute-start(bf16[40,64,128]{2,1,0:T(8,128)(2,1)S(1)} %collective-permute-done.rest_1_), channel_id=1, source_target_pairs={{0,1},{1,0},{2,3},{3,2},{4,5},{5,4},{6,7},{7,6},{8,9},{9,8},{10,11... | collective-permute-start | bytes 1966088 | tf_op jit(solution)/shard_map/ppermute | solution.py:233
  31.9 32.1 %collective-permute-start.6 = (bf16[40,64,128]{2,1,0:T(8,128)(2,1)}, bf16[40,64,128]{2,1,0:T(8,128)(2,1)}, u32[]{:S(2)}, u32[]{:S(2)}) collective-permute-start(bf16[40,64,128]{2,1,0:T(8,128)(2,1)} %get-tuple-element.23), channel_id=1, source_target_pairs={{0,2},{1,3},{2,0},{3,1},{4,6},{5,7},{6,4},{7,5},{8,10},{9,11},{10,... | collective-permute-start | bytes 1966088 | tf_op jit(solution)/shard_map/ppermute | solution.py:229
  36.8 27.2 %collective-permute-start.7 = (bf16[40,64,128]{2,1,0:T(8,128)(2,1)}, bf16[40,64,128]{2,1,0:T(8,128)(2,1)}, u32[]{:S(2)}, u32[]{:S(2)}) collective-permute-start(bf16[40,64,128]{2,1,0:T(8,128)(2,1)} %collective-permute-done.1.rest_0_), channel_id=1, source_target_pairs={{0,4},{1,5},{4,8},{5,9},{8,12},{9,13},{12,16},{13,17},{16,20},{17,... | collective-permute-start | bytes 1966088 | tf_op jit(solution)/shard_map/ppermute | solution.py:219
  47.5 25.3 %collective-permute-start.3 = (bf16[40,64,128]{2,1,0:T(8,128)(2,1)}, bf16[40,64,128]{2,1,0:T(8,128)(2,1)}, u32[]{:S(2)}, u32[]{:S(2)}) collective-permute-start(bf16[40,64,128]{2,1,0:T(8,128)(2,1)} %collective-permute-done.1.rest_0_), channel_id=1, source_target_pairs={{0,1},{1,0},{2,3},{3,2},{4,5},{5,4},{6,7},{7,6},{8,9},{9,8},{10,11... | collective-permute-start | bytes 1966088 | tf_op jit(solution)/shard_map/ppermute | solution.py:232
  65.1 7.7 %collective-permute-start.9 = (bf16[40,64,128]{2,1,0:T(8,128)(2,1)S(1)}, bf16[40,64,128]{2,1,0:T(8,128)(2,1)S(1)}, u32[]{:S(2)}, u32[]{:S(2)}) collective-permute-start(bf16[40,64,128]{2,1,0:T(8,128)(2,1)S(1)} %broadcast_select_fusion.rest_2_), channel_id=1, source_target_pairs={{0,1},{1,0},{2,3},{3,2},{4,5},{5,4},{6,7},{7,6},{8,9},{9,8},{10,11... | collective-permute-start | bytes 1966088 | tf_op jit(solution)/shard_map/ppermute | solution.py:241
  65.2 7.6 %collective-permute-start.8 = (bf16[40,64,128]{2,1,0:T(8,128)(2,1)}, bf16[40,64,128]{2,1,0:T(8,128)(2,1)}, u32[]{:S(2)}, u32[]{:S(2)}) collective-permute-start(bf16[40,64,128]{2,1,0:T(8,128)(2,1)} %collective-permute-done.6.rest_1_), channel_id=1, source_target_pairs={{0,1},{1,0},{2,3},{3,2},{4,5},{5,4},{6,7},{7,6},{8,9},{9,8},{10,11... | collective-permute-start | bytes 1966088 | tf_op jit(solution)/shard_map/ppermute | solution.py:239

commit v5 on v4

--- a/solution.py
+++ b/solution.py
@@ -225,15 +225,15 @@
     mate, first = lax.optimization_barrier((s_blocks, first))
     mate = beside(mate)
     tab = table(h, r, l_index, s_cols, c_index)
-    second, halo, tab = lax.optimization_barrier((second, halo, tab))
+    second, far_first, tab = lax.optimization_barrier((second, far_first, tab))
     far_second = across(second)
-
     far_halo = send(far_first, plain)
     cross_first = beside(far_first)
+    halo, far_first = lax.optimization_barrier((halo, far_first))
     mate_halo = beside(halo)
-    tab, far_first, seam_halo = lax.optimization_barrier((tab, far_first, seam_halo))
     parts = [(c ^ flip).reshape(1) for flip in range(4)]
     out = product(tab, parts[0], l_blocks, (s_blocks, halo), None)
+    out, mate, seam_halo = lax.optimization_barrier((out, mate, seam_halo))
     out = product(tab, parts[1], l_blocks, (mate, mate_halo), out)
     out, far_second, far_halo = lax.optimization_barrier((out, far_second, far_halo))
     cross_second = beside(far_second)

time: 80.4 us -> 79.7 us (level)
  the two profiles are of different devices: /device:TPU:3 before, /device:TPU:7 now
where the time goes in v5:
time: 79.7 us; the launch traced here: 79.5 us
  Pallas kernels  32.9 us (41%)
  starting transfers between devices  28.4 us (36%)
  waiting for transfers between devices  16.5 us (21%)
  other arithmetic  1.23 us (2%)
    pallas_call x4, Pallas kernels, product(): pl.pallas_call(functools.partial(product_body, len(pieces)), out_shape=ja...  28.6 us
    ppermute x3, waiting for transfers between devices, send(): return lax.ppermute(x, ('rows', 'cols'), perm)  13.7 us
    ppermute x3, starting transfers between devices, send(): return lax.ppermute(x, ('rows', 'cols'), perm)  12.1 us
    ppermute x1, starting transfers between devices, shards(): far_second = across(second)  8.81 us
    ppermute x1, starting transfers between devices, shards(): mate_halo = beside(halo)  3.27 us
    pallas_call x1, Pallas kernels, pack(): pl.pallas_call(pack_body, out_shape=(piece, piece), in_specs=[pl.BlockSpe...  3.05 us
    ppermute x1, waiting for transfers between devices, shards(): far_first = across(first)  2.73 us
  transfers between devices with their start and end apart: 10, of which 3 were waited for; matrix products, arithmetic and copies ran while one was open for 2% of the time, Pallas kernels for 29%

profile of v5, /device:TPU:7, one launch (start us, length us, event | category | flops | bytes accessed | tf_op | source)
XLA Modules:
  0.0 79.5 jit_solution(12266259015951145329)
XLA Ops:
  0.0 0.0 copy-start
  0.0 0.0 copy-start.1
  0.0 3.1 %shard_map.55 = (bf16[40,64,128]{2,1,0:T(8,128)(2,1)}, bf16[40,64,128]{2,1,0:T(8,128)(2,1)}) custom-call(s32[1]{0:T(128)} %bitcast.start_ref, bf16[32,64,320]{2,1,0:T(8,128)(2,1)} %rest_0_.1), custom_call_target="tpu_custom_call" | custom-call | bytes 3145728 | tf_op jit(solution)/shard_map/pallas_call | solution.py:38
  3.1 1.1 %collective-permute-start = (bf16[40,64,128]{2,1,0:T(8,128)(2,1)}, bf16[40,64,128]{2,1,0:T(8,128)(2,1)}, u32[]{:S(2)}, u32[]{:S(2)}) collective-permute-start(bf16[40,64,128]{2,1,0:T(8,128)(2,1)} %get-tuple-element.20), channel_id=1, source_target_pairs={{0,2},{1,3},{2,0},{3,1},{4,6},{5,7},{6,4},{7,5},{8,10},{9,11},{10,... | collective-permute-start | bytes 1966088 | tf_op jit(solution)/shard_map/ppermute | solution.py:222
  4.2 9.3 %collective-permute-start.2 = (bf16[40,64,128]{2,1,0:T(8,128)(2,1)}, bf16[40,64,128]{2,1,0:T(8,128)(2,1)S(1)}, u32[]{:S(2)}, u32[]{:S(2)}) collective-permute-start(bf16[40,64,128]{2,1,0:T(8,128)(2,1)} %get-tuple-element.27), channel_id=1, source_target_pairs={{0,4},{1,5},{4,8},{5,9},{8,12},{9,13},{12,16},{13,17},{16,20},{17,... | collective-permute-start | bytes 1966088 | tf_op jit(solution)/shard_map/ppermute | solution.py:219
  13.5 1.3 %collective-permute-start.3 = (bf16[32,64,320]{2,1,0:T(8,128)(2,1)}, bf16[32,64,320]{2,1,0:T(8,128)(2,1)}, u32[]{:S(2)}, u32[]{:S(2)}) collective-permute-start(bf16[32,64,320]{2,1,0:T(8,128)(2,1)} %rest_0_.1), channel_id=1, source_target_pairs={{0,1},{1,0},{2,3},{3,2},{4,5},{5,4},{6,7},{7,6},{8,9},{9,8},{10,11... | collective-permute-start | bytes 3932168 | tf_op jit(solution)/shard_map/ppermute | solution.py:226
  14.8 1.5 %collective-permute-start.4 = (bf16[40,64,128]{2,1,0:T(8,128)(2,1)}, bf16[40,64,128]{2,1,0:T(8,128)(2,1)}, u32[]{:S(2)}, u32[]{:S(2)}) collective-permute-start(bf16[40,64,128]{2,1,0:T(8,128)(2,1)} %get-tuple-element.20), channel_id=1, source_target_pairs={{126,128},{127,129},{128,126},{129,127}} | collective-permute-start | bytes 1966088 | tf_op jit(solution)/shard_map/ppermute | solution.py:219
  16.3 0.1 pad_add_fusion.at_ref
  16.4 0.1 dynamic-slice_bitcast_fusion.near_ref
  16.5 0.0 copy-done.2
  16.5 1.3 %shard_map.56 = s32[48,128]{1,0:T(8,128)S(1)} custom-call(s32[3]{0:T(128)S(1)} %pad_add_fusion.at_ref, s32[20,64]{1,0:T(8,128)S(1)} %dynamic-slice_bitcast_fusion.near_ref, s32[8,30]{1,0:T(8,128)S(1)} %copy-done.2, s32[8,24]{1,0:T(8,128)S(1)} %copy-done.3), custom_call_target="tpu_custom_call" | custom-call | flops 268435456 | bytes 8388608 | tf_op jit(solution)/shard_map/pallas_call | solution.py:193
  17.8 2.7 %collective-permute-done.rest_0_ = bf16[40,64,128]{2,1,0:T(8,128)(2,1)} collective-permute-done((bf16[40,64,128]{2,1,0:T(8,128)(2,1)}, bf16[40,64,128]{2,1,0:T(8,128)(2,1)}, u32[]{:S(2)}, u32[]{:S(2)}) %collective-permute-start) | collective-permute-done | bytes 655392 | tf_op jit(solution)/shard_map/ppermute | solution.py:222
  20.5 11.6 %collective-permute-done.2.rest_1_ = bf16[40,64,128]{2,1,0:T(8,128)(2,1)S(1)} collective-permute-done((bf16[40,64,128]{2,1,0:T(8,128)(2,1)}, bf16[40,64,128]{2,1,0:T(8,128)(2,1)S(1)}, u32[]{:S(2)}, u32[]{:S(2)}) %collective-permute-start.2) | collective-permute-done | bytes 655392 | tf_op jit(solution)/shard_map/ppermute | solution.py:219
  32.1 3.3 %collective-permute-start.5 = (bf16[40,64,128]{2,1,0:T(8,128)(2,1)S(1)}, bf16[40,64,128]{2,1,0:T(8,128)(2,1)S(1)}, u32[]{:S(2)}, u32[]{:S(2)}) collective-permute-start(bf16[40,64,128]{2,1,0:T(8,128)(2,1)S(1)} %collective-permute-done.2.rest_1_), channel_id=1, source_target_pairs={{0,1},{1,0},{2,3},{3,2},{4,5},{5,4},{6,7},{7,6},{8,9},{9,8},{10,11... | collective-permute-start | bytes 1966088 | tf_op jit(solution)/shard_map/ppermute | solution.py:233
  35.4 8.8 %collective-permute-start.6 = (bf16[40,64,128]{2,1,0:T(8,128)(2,1)}, bf16[40,64,128]{2,1,0:T(8,128)(2,1)}, u32[]{:S(2)}, u32[]{:S(2)}) collective-permute-start(bf16[40,64,128]{2,1,0:T(8,128)(2,1)} %get-tuple-element.27), channel_id=1, source_target_pairs={{0,2},{1,3},{2,0},{3,1},{4,6},{5,7},{6,4},{7,5},{8,10},{9,11},{10,... | collective-permute-start | bytes 1966088 | tf_op jit(solution)/shard_map/ppermute | solution.py:229
  44.2 1.3 %collective-permute-start.7 = (bf16[40,64,128]{2,1,0:T(8,128)(2,1)}, bf16[40,64,128]{2,1,0:T(8,128)(2,1)}, u32[]{:S(2)}, u32[]{:S(2)}) collective-permute-start(bf16[40,64,128]{2,1,0:T(8,128)(2,1)} %collective-permute-done.rest_0_), channel_id=1, source_target_pairs={{0,4},{1,5},{4,8},{5,9},{8,12},{9,13},{12,16},{13,17},{16,20},{17,... | collective-permute-start | bytes 1966088 | tf_op jit(solution)/shard_map/ppermute | solution.py:219
  45.5 7.2 %shard_map.57.rest_2_ = bf16[8,64,1536]{2,1,0:T(8,128)(2,1)} custom-call(s32[6144]{0:T(1024)S(1)} %bitcast.10, s32[1]{0:T(128)} %bitcast.7.part_ref, bf16[8,64,1920]{2,1,0:T(8,128)(2,1)S(1)} %copy-done.1, bf16[32,64,320]{2,1,0:T(8,128)(2,1)} %rest_0_.1, bf16[40,64,128]{2,1,0:T(8,128)(2,1)S(1)} %collective-permute-done.2.rest_1_), custom_call_target="tpu_custom_call" | custom-call | flops 755000000 | bytes 20971520 | tf_op jit(solution)/shard_map/pallas_call | solution.py:116
  52.7 0.0 collective-permute-done.4
  52.7 0.4 collective-permute-start.1
  53.0 0.0 collective-permute-done.3.rest_0_
  53.0 0.0 collective-permute-done.5.rest_1_
  53.1 7.2 %shard_map.58.rest_3_ = bf16[8,64,1536]{2,1,0:T(8,128)(2,1)} custom-call(s32[6144]{0:T(1024)S(1)} %bitcast.11, s32[1]{0:T(128)} %bitcast.6.part_ref, bf16[8,64,1920]{2,1,0:T(8,128)(2,1)S(1)} %copy-done.1, bf16[32,64,320]{2,1,0:T(8,128)(2,1)} %collective-permute-done.3.rest_0_, ...), custom_call_target="tpu_custom_call", output_to_operand_aliasing={{}: (5, {})} | custom-call | flops 755000000 | bytes 20971520 | tf_op jit(solution)/shard_map/pallas_call | solution.py:116
  60.2 0.0 collective-permute-done.6.rest_1_
  60.2 2.2 %collective-permute-done.7 = bf16[40,64,128]{2,1,0:T(8,128)(2,1)} collective-permute-done((bf16[40,64,128]{2,1,0:T(8,128)(2,1)}, bf16[40,64,128]{2,1,0:T(8,128)(2,1)}, u32[]{:S(2)}, u32[]{:S(2)}) %collective-permute-start.7) | collective-permute-done | bytes 655392 | tf_op jit(solution)/shard_map/ppermute | solution.py:219
  62.4 1.2 %broadcast_select_fusion.rest_2_ = bf16[40,64,128]{2,1,0:T(8,128)(2,1)S(1)} fusion(bf16[40,64,128]{2,1,0:T(8,128)(2,1)} %collective-permute-done.4, bf16[40,64,128]{2,1,0:T(8,128)(2,1)} %collective-permute-done.7, pred[]{:T(512)S(6)} %or.3), kind=kLoop, calls=%fused_computation | loop fusion | flops 327680 | bytes 1966081 | tf_op jit(solution)/shard_map/jit(_where)/select_n | solution.py:240
  63.6 1.2 %collective-permute-start.9 = (bf16[40,64,128]{2,1,0:T(8,128)(2,1)S(1)}, bf16[40,64,128]{2,1,0:T(8,128)(2,1)S(1)}, u32[]{:S(2)}, u32[]{:S(2)}) collective-permute-start(bf16[40,64,128]{2,1,0:T(8,128)(2,1)S(1)} %broadcast_select_fusion.rest_2_), channel_id=1, source_target_pairs={{0,1},{1,0},{2,3},{3,2},{4,5},{5,4},{6,7},{7,6},{8,9},{9,8},{10,11... | collective-permute-start | bytes 1966088 | tf_op jit(solution)/shard_map/ppermute | solution.py:241
  64.8 0.3 collective-permute-start.8
  65.0 7.1 %shard_map.59.rest_3_ = bf16[8,64,1536]{2,1,0:T(8,128)(2,1)} custom-call(s32[6144]{0:T(1024)S(1)} %bitcast.12, s32[1]{0:T(128)} %bitcast.8.part_ref, bf16[8,64,1920]{2,1,0:T(8,128)(2,1)S(1)} %copy-done.1, bf16[40,64,128]{2,1,0:T(8,128)(2,1)} %collective-permute-done.rest_0_, ...), custom_call_target="tpu_custom_call", output_to_operand_aliasing={{}: (6, {})} | custom-call | flops 755000000 | bytes 20971520 | tf_op jit(solution)/shard_map/pallas_call | solution.py:116
  72.2 0.0 collective-permute-done.1.rest_0_
  72.2 0.0 collective-permute-done.9.rest_2_
  72.2 0.0 collective-permute-done.8.rest_1_
  72.2 7.1 %shard_map.60 = bf16[8,64,1536]{2,1,0:T(8,128)(2,1)} custom-call(s32[6144]{0:T(1024)S(1)} %bitcast.13, s32[1]{0:T(128)} %bitcast.5.part_ref, bf16[8,64,1920]{2,1,0:T(8,128)(2,1)S(1)} %copy-done.1, bf16[40,64,128]{2,1,0:T(8,128)(2,1)} %collective-permute-done.1.rest_0_, ...), custom_call_target="tpu_custom_call", output_to_operand_aliasing={{}: (6, {})} | custom-call | flops 755000000 | bytes 20971520 | tf_op jit(solution)/shard_map/pallas_call | solution.py:116
  (5 shorter events, 0.0 us)
Async XLA Ops:
  0.0 16.4 %copy-start = (s32[2048,20]{0,1:T(8,128)S(1)}, s32[2048,20]{0,1:T(8,128)}, u32[]{:S(2)}) copy-start(s32[2048,20]{0,1:T(8,128)} %param.8) | copy-start | bytes 491524
  0.0 16.5 %copy-start.2 = (s32[8,30]{1,0:T(8,128)S(1)}, s32[8,30]{1,0:T(8,128)}, u32[]{:S(2)}) copy-start(s32[8,30]{1,0:T(8,128)} %l_ref.5) | copy-start | bytes 2884
  0.0 16.5 %copy-start.3 = (s32[8,24]{1,0:T(8,128)S(1)}, s32[8,24]{1,0:T(8,128)}, u32[]{:S(2)}) copy-start(s32[8,24]{1,0:T(8,128)} %c_ref.1) | copy-start | bytes 2308
  0.0 45.5 %copy-start.1 = (bf16[8,64,1920]{2,1,0:T(8,128)(2,1)S(1)}, bf16[8,64,1920]{2,1,0:T(8,128)(2,1)}, u32[]{:S(2)}) copy-start(bf16[8,64,1920]{2,1,0:T(8,128)(2,1)} %l_ref.9) | copy-start | bytes 5898244
  3.1 17.4 %collective-permute-start = (bf16[40,64,128]{2,1,0:T(8,128)(2,1)}, bf16[40,64,128]{2,1,0:T(8,128)(2,1)}, u32[]{:S(2)}, u32[]{:S(2)}) collective-permute-start(bf16[40,64,128]{2,1,0:T(8,128)(2,1)} %get-tuple-element.20), channel_id=1, source_target_pairs={{0,2},{1,3},{2,0},{3,1},{4,6},{5,7},{6,4},{7,5},{8,10},{9,11},{10,... | collective-permute-start | bytes 1966088 | tf_op jit(solution)/shard_map/ppermute | solution.py:222
  4.2 27.9 %collective-permute-start.2 = (bf16[40,64,128]{2,1,0:T(8,128)(2,1)}, bf16[40,64,128]{2,1,0:T(8,128)(2,1)S(1)}, u32[]{:S(2)}, u32[]{:S(2)}) collective-permute-start(bf16[40,64,128]{2,1,0:T(8,128)(2,1)} %get-tuple-element.27), channel_id=1, source_target_pairs={{0,4},{1,5},{4,8},{5,9},{8,12},{9,13},{12,16},{13,17},{16,20},{17,... | collective-permute-start | bytes 1966088 | tf_op jit(solution)/shard_map/ppermute | solution.py:219
  13.5 39.5 %collective-permute-start.3 = (bf16[32,64,320]{2,1,0:T(8,128)(2,1)}, bf16[32,64,320]{2,1,0:T(8,128)(2,1)}, u32[]{:S(2)}, u32[]{:S(2)}) collective-permute-start(bf16[32,64,320]{2,1,0:T(8,128)(2,1)} %rest_0_.1), channel_id=1, source_target_pairs={{0,1},{1,0},{2,3},{3,2},{4,5},{5,4},{6,7},{7,6},{8,9},{9,8},{10,11... | collective-permute-start | bytes 3932168 | tf_op jit(solution)/shard_map/ppermute | solution.py:226
  14.8 37.8 %collective-permute-start.4 = (bf16[40,64,128]{2,1,0:T(8,128)(2,1)}, bf16[40,64,128]{2,1,0:T(8,128)(2,1)}, u32[]{:S(2)}, u32[]{:S(2)}) collective-permute-start(bf16[40,64,128]{2,1,0:T(8,128)(2,1)} %get-tuple-element.20), channel_id=1, source_target_pairs={{126,128},{127,129},{128,126},{129,127}} | collective-permute-start | bytes 1966088 | tf_op jit(solution)/shard_map/ppermute | solution.py:219
  32.1 21.0 %collective-permute-start.5 = (bf16[40,64,128]{2,1,0:T(8,128)(2,1)S(1)}, bf16[40,64,128]{2,1,0:T(8,128)(2,1)S(1)}, u32[]{:S(2)}, u32[]{:S(2)}) collective-permute-start(bf16[40,64,128]{2,1,0:T(8,128)(2,1)S(1)} %collective-permute-done.2.rest_1_), channel_id=1, source_target_pairs={{0,1},{1,0},{2,3},{3,2},{4,5},{5,4},{6,7},{7,6},{8,9},{9,8},{10,11... | collective-permute-start | bytes 1966088 | tf_op jit(solution)/shard_map/ppermute | solution.py:233
  35.4 24.9 %collective-permute-start.6 = (bf16[40,64,128]{2,1,0:T(8,128)(2,1)}, bf16[40,64,128]{2,1,0:T(8,128)(2,1)}, u32[]{:S(2)}, u32[]{:S(2)}) collective-permute-start(bf16[40,64,128]{2,1,0:T(8,128)(2,1)} %get-tuple-element.27), channel_id=1, source_target_pairs={{0,2},{1,3},{2,0},{3,1},{4,6},{5,7},{6,4},{7,5},{8,10},{9,11},{10,... | collective-permute-start | bytes 1966088 | tf_op jit(solution)/shard_map/ppermute | solution.py:229
  44.2 18.2 %collective-permute-start.7 = (bf16[40,64,128]{2,1,0:T(8,128)(2,1)}, bf16[40,64,128]{2,1,0:T(8,128)(2,1)}, u32[]{:S(2)}, u32[]{:S(2)}) collective-permute-start(bf16[40,64,128]{2,1,0:T(8,128)(2,1)} %collective-permute-done.rest_0_), channel_id=1, source_target_pairs={{0,4},{1,5},{4,8},{5,9},{8,12},{9,13},{12,16},{13,17},{16,20},{17,... | collective-permute-start | bytes 1966088 | tf_op jit(solution)/shard_map/ppermute | solution.py:219
  52.7 19.5 %collective-permute-start.1 = (bf16[40,64,128]{2,1,0:T(8,128)(2,1)}, bf16[40,64,128]{2,1,0:T(8,128)(2,1)}, u32[]{:S(2)}, u32[]{:S(2)}) collective-permute-start(bf16[40,64,128]{2,1,0:T(8,128)(2,1)} %collective-permute-done.rest_0_), channel_id=1, source_target_pairs={{0,1},{1,0},{2,3},{3,2},{4,5},{5,4},{6,7},{7,6},{8,9},{9,8},{10,11... | collective-permute-start | bytes 1966088 | tf_op jit(solution)/shard_map/ppermute | solution.py:231
  63.6 8.6 %collective-permute-start.9 = (bf16[40,64,128]{2,1,0:T(8,128)(2,1)S(1)}, bf16[40,64,128]{2,1,0:T(8,128)(2,1)S(1)}, u32[]{:S(2)}, u32[]{:S(2)}) collective-permute-start(bf16[40,64,128]{2,1,0:T(8,128)(2,1)S(1)} %broadcast_select_fusion.rest_2_), channel_id=1, source_target_pairs={{0,1},{1,0},{2,3},{3,2},{4,5},{5,4},{6,7},{7,6},{8,9},{9,8},{10,11... | collective-permute-start | bytes 1966088 | tf_op jit(solution)/shard_map/ppermute | solution.py:241
  64.8 7.4 %collective-permute-start.8 = (bf16[40,64,128]{2,1,0:T(8,128)(2,1)}, bf16[40,64,128]{2,1,0:T(8,128)(2,1)}, u32[]{:S(2)}, u32[]{:S(2)}) collective-permute-start(bf16[40,64,128]{2,1,0:T(8,128)(2,1)} %collective-permute-done.6.rest_1_), channel_id=1, source_target_pairs={{0,1},{1,0},{2,3},{3,2},{4,5},{5,4},{6,7},{7,6},{8,9},{9,8},{10,11... | collective-permute-start | bytes 1966088 | tf_op jit(solution)/shard_map/ppermute | solution.py:239

commit v6 on v5

--- a/solution.py
+++ b/solution.py
@@ -209,10 +209,14 @@
     beside = functools.partial(lax.ppermute, axis_name="cols", perm=[(k, k ^ 1) for k in range(4)])
     up = [(4 * g + k, 4 * g + 4 + k) for g in range(groups - 1) for k in (0, 1)]
     down = [(4 * g + k, 4 * g - 4 + k) for g in range(1, groups) for k in (2, 3)]
-    below, above = groups // 2 - 1, groups // 2
+    below, above, last = groups // 2 - 1, groups // 2, groups - 1
     seam = [(4 * below + 2 + k, 4 * above + k) for k in (0, 1)]
     seam += [(4 * above + k, 4 * below + 2 + k) for k in (0, 1)]
     plain = [route for route in up + down if route[1] not in {q for _, q in seam}]
+    direct = [(4 * below + k, 4 * above + k) for k in (0, 1)]
+    direct += [(4 * above + 2 + k, 4 * below + 2 + k) for k in (0, 1)]
+    relay = [(4 * below + k, 4 * last + k) for k in (0, 1)] + [(4 * above + 2 + k, 2 + k) for k in (0, 1)]
+    onward = [(4 * last + k, 4 * above + k) for k in (0, 1)] + [(2 + k, 4 * below + 2 + k) for k in (0, 1)]
     takes = ((r == above) & (h == 0)) | ((r == below) & (h == 1))
 
     def send(x, perm):
@@ -220,16 +224,21 @@
 
     first, second = pack(h.reshape(1), s_blocks)
     far_first = across(first)
-    halo = send(second, up + down)
+    halo = send(second, plain)
+    relayed = send(second[TILES // 2 :], relay)
+    seam_first = send(second[: TILES // 2], direct)
     seam_halo = send(first, seam)
     mate, first = lax.optimization_barrier((s_blocks, first))
     mate = beside(mate)
+    c_index, relayed = lax.optimization_barrier((c_index, relayed))
+    seam_second = send(relayed, onward)
     tab = table(h, r, l_index, s_cols, c_index)
     second, far_first, tab = lax.optimization_barrier((second, far_first, tab))
     far_second = across(second)
     far_halo = send(far_first, plain)
     cross_first = beside(far_first)
     halo, far_first = lax.optimization_barrier((halo, far_first))
+    halo = jnp.where(takes, jnp.concatenate([seam_first, seam_second]), halo)
     mate_halo = beside(halo)
     parts = [(c ^ flip).reshape(1) for flip in range(4)]
     out = product(tab, parts[0], l_blocks, (s_blocks, halo), None)

time: 79.7 us -> 91.1 us (1.14)
  the two profiles are of different devices: /device:TPU:7 before, /device:TPU:3 now
where the time goes in v6:
time: 91.1 us; the launch traced here: 90.7 us
  Pallas kernels  32.8 us (36%)
  starting transfers between devices  29.4 us (32%)
  waiting for transfers between devices  24.5 us (27%)
  other arithmetic  2.4 us (3%)
  local copies, waits for them, and re-layouts  1.21 us (1%)
    pallas_call x4, Pallas kernels, product(): pl.pallas_call(functools.partial(product_body, len(pieces)), out_shape=ja...  28.6 us
    ppermute x6, starting transfers between devices, send(): return lax.ppermute(x, ('rows', 'cols'), perm)  20.7 us
    ppermute x6, waiting for transfers between devices, send(): return lax.ppermute(x, ('rows', 'cols'), perm)  16.9 us
    ppermute x1, starting transfers between devices, shards(): mate_halo = beside(halo)  4.36 us
    ppermute x1, waiting for transfers between devices, shards(): far_first = across(first)  4.01 us
    ppermute x1, waiting for transfers between devices, shards(): far_second = across(second)  3.65 us
    pallas_call x1, Pallas kernels, pack(): pl.pallas_call(pack_body, out_shape=(piece, piece), in_specs=[pl.BlockSpe...  2.92 us
    ppermute x1, starting transfers between devices, shards(): far_first = across(first)  1.84 us
  transfers between devices with their start and end apart: 13, of which 3 were waited for; matrix products, arithmetic and copies ran while one was open for 4% of the time, Pallas kernels for 25%

profile of v6, /device:TPU:3, one launch (start us, length us, event | category | flops | bytes accessed | tf_op | source)
XLA Modules:
  0.0 90.7 jit_solution(14629814671743502885)
XLA Ops:
  0.0 2.9 %shard_map.55 = (bf16[40,64,128]{2,1,0:T(8,128)(2,1)}, bf16[40,64,128]{2,1,0:T(8,128)(2,1)}) custom-call(s32[1]{0:T(128)} %bitcast.start_ref, bf16[32,64,320]{2,1,0:T(8,128)(2,1)} %rest_0_.1), custom_call_target="tpu_custom_call" | custom-call | bytes 3145728 | tf_op jit(solution)/shard_map/pallas_call | solution.py:38
  2.9 1.8 %collective-permute-start = (bf16[40,64,128]{2,1,0:T(8,128)(2,1)}, bf16[40,64,128]{2,1,0:T(8,128)(2,1)}, u32[]{:S(2)}, u32[]{:S(2)}) collective-permute-start(bf16[40,64,128]{2,1,0:T(8,128)(2,1)} %get-tuple-element.22), channel_id=1, source_target_pairs={{0,2},{1,3},{2,0},{3,1},{4,6},{5,7},{6,4},{7,5},{8,10},{9,11},{10,... | collective-permute-start | bytes 1966088 | tf_op jit(solution)/shard_map/ppermute | solution.py:226
  4.8 3.6 %collective-permute-start.5 = (bf16[40,64,128]{2,1,0:T(8,128)(2,1)}, bf16[40,64,128]{2,1,0:T(8,128)(2,1)S(1)}, u32[]{:S(2)}, u32[]{:S(2)}) collective-permute-start(bf16[40,64,128]{2,1,0:T(8,128)(2,1)} %get-tuple-element.31), channel_id=1, source_target_pairs={{0,4},{1,5},{4,8},{5,9},{8,12},{9,13},{12,16},{13,17},{16,20},{17,... | collective-permute-start | bytes 1966088 | tf_op jit(solution)/shard_map/ppermute | solution.py:223
  8.4 1.1 %fusion = (bf16[20,64,128]{2,1,0:T(8,128)(2,1)S(1)}, bf16[20,64,128]{2,1,0:T(8,128)(2,1)S(1)}) fusion(bf16[40,64,128]{2,1,0:T(8,128)(2,1)} %get-tuple-element.31), kind=kLoop, calls=%fused_computation.4 | loop fusion | bytes 1310720 | tf_op jit(solution)/shard_map/slice | solution.py:229
  9.5 0.0 copy-start.1
  9.5 1.6 %collective-permute-start.1 = (bf16[20,64,128]{2,1,0:T(8,128)(2,1)S(1)}, bf16[20,64,128]{2,1,0:T(8,128)(2,1)}, u32[]{:S(2)}, u32[]{:S(2)}) collective-permute-start(bf16[20,64,128]{2,1,0:T(8,128)(2,1)S(1)} %get-tuple-element.38), channel_id=1, source_target_pairs={{124,252},{125,253},{130,2},{131,3}} | collective-permute-start | bytes 983048 | tf_op jit(solution)/shard_map/ppermute | solution.py:223
  11.1 1.2 %collective-permute-start.6 = (bf16[32,64,320]{2,1,0:T(8,128)(2,1)}, bf16[32,64,320]{2,1,0:T(8,128)(2,1)}, u32[]{:S(2)}, u32[]{:S(2)}) collective-permute-start(bf16[32,64,320]{2,1,0:T(8,128)(2,1)} %rest_0_.1), channel_id=1, source_target_pairs={{0,1},{1,0},{2,3},{3,2},{4,5},{5,4},{6,7},{7,6},{8,9},{9,8},{10,11... | collective-permute-start | bytes 3932168 | tf_op jit(solution)/shard_map/ppermute | solution.py:232
  12.3 1.3 %collective-permute-start.3 = (bf16[20,64,128]{2,1,0:T(8,128)(2,1)S(1)}, bf16[20,64,128]{2,1,0:T(8,128)(2,1)}, u32[]{:S(2)}, u32[]{:S(2)}) collective-permute-start(bf16[20,64,128]{2,1,0:T(8,128)(2,1)S(1)} %get-tuple-element.37), channel_id=1, source_target_pairs={{124,128},{125,129},{130,126},{131,127}} | collective-permute-start | bytes 983048 | tf_op jit(solution)/shard_map/ppermute | solution.py:223
  13.6 0.0 collective-permute-done.1
  13.6 1.3 %collective-permute-start.4 = (bf16[20,64,128]{2,1,0:T(8,128)(2,1)}, bf16[20,64,128]{2,1,0:T(8,128)(2,1)}, u32[]{:S(2)}, u32[]{:S(2)}) collective-permute-start(bf16[20,64,128]{2,1,0:T(8,128)(2,1)} %collective-permute-done.1), channel_id=1, source_target_pairs={{252,128},{253,129},{2,126},{3,127}} | collective-permute-start | bytes 983048 | tf_op jit(solution)/shard_map/ppermute | solution.py:223
  14.9 0.1 pad_add_fusion.at_ref
  15.0 0.1 dynamic-slice_bitcast_fusion.near_ref
  15.1 1.3 %shard_map.56 = s32[48,128]{1,0:T(8,128)S(1)} custom-call(s32[3]{0:T(128)S(1)} %pad_add_fusion.at_ref, s32[20,64]{1,0:T(8,128)S(1)} %dynamic-slice_bitcast_fusion.near_ref, s32[8,30]{1,0:T(8,128)S(1)} %copy-done.2, s32[8,24]{1,0:T(8,128)S(1)} %copy-done.3), custom_call_target="tpu_custom_call" | custom-call | flops 268435456 | bytes 8388608 | tf_op jit(solution)/shard_map/pallas_call | solution.py:193
  16.4 4.0 %collective-permute-done.rest_0_ = bf16[40,64,128]{2,1,0:T(8,128)(2,1)} collective-permute-done((bf16[40,64,128]{2,1,0:T(8,128)(2,1)}, bf16[40,64,128]{2,1,0:T(8,128)(2,1)}, u32[]{:S(2)}, u32[]{:S(2)}) %collective-permute-start) | collective-permute-done | bytes 655392 | tf_op jit(solution)/shard_map/ppermute | solution.py:226
  20.4 10.9 %collective-permute-start.7 = (bf16[40,64,128]{2,1,0:T(8,128)(2,1)}, bf16[40,64,128]{2,1,0:T(8,128)(2,1)}, u32[]{:S(2)}, u32[]{:S(2)}) collective-permute-start(bf16[40,64,128]{2,1,0:T(8,128)(2,1)} %get-tuple-element.22), channel_id=1, source_target_pairs={{126,128},{127,129},{128,126},{129,127}} | collective-permute-start | bytes 1966088 | tf_op jit(solution)/shard_map/ppermute | solution.py:223
  31.2 0.0 collective-permute-done.3
  31.2 16.8 %collective-permute-done.4 = bf16[20,64,128]{2,1,0:T(8,128)(2,1)} collective-permute-done((bf16[20,64,128]{2,1,0:T(8,128)(2,1)}, bf16[20,64,128]{2,1,0:T(8,128)(2,1)}, u32[]{:S(2)}, u32[]{:S(2)}) %collective-permute-start.4) | collective-permute-done | bytes 327712 | tf_op jit(solution)/shard_map/ppermute | solution.py:223
  48.1 1.2 %maximum_select_fusion.rest_1_ = bf16[40,64,128]{2,1,0:T(8,128)(2,1)S(1)} fusion(bf16[40,64,128]{2,1,0:T(8,128)(2,1)S(1)} %collective-permute-done.5, bf16[20,64,128]{2,1,0:T(8,128)(2,1)} %collective-permute-done.4, bf16[20,64,128]{2,1,0:T(8,128)(2,1)} %collective-permute-done.3, pred[]{:T(512)S(6)} %or.3), kind=kLoop, calls=%fused_computation | loop fusion | flops 655360 | bytes 1966081 | tf_op jit(solution)/shard_map/jit(_where)/select_n | solution.py:241
  49.2 4.4 %collective-permute-start.8 = (bf16[40,64,128]{2,1,0:T(8,128)(2,1)S(1)}, bf16[40,64,128]{2,1,0:T(8,128)(2,1)S(1)}, u32[]{:S(2)}, u32[]{:S(2)}) collective-permute-start(bf16[40,64,128]{2,1,0:T(8,128)(2,1)S(1)} %maximum_select_fusion.rest_1_), channel_id=1, source_target_pairs={{0,1},{1,0},{2,3},{3,2},{4,5},{5,4},{6,7},{7,6},{8,9},{9,8},{10,11... | collective-permute-start | bytes 1966088 | tf_op jit(solution)/shard_map/ppermute | solution.py:242
  53.6 2.2 %collective-permute-start.10 = (bf16[40,64,128]{2,1,0:T(8,128)(2,1)}, bf16[40,64,128]{2,1,0:T(8,128)(2,1)}, u32[]{:S(2)}, u32[]{:S(2)}) collective-permute-start(bf16[40,64,128]{2,1,0:T(8,128)(2,1)} %collective-permute-done.rest_0_), channel_id=1, source_target_pairs={{0,4},{1,5},{4,8},{5,9},{8,12},{9,13},{12,16},{13,17},{16,20},{17,... | collective-permute-start | bytes 1966088 | tf_op jit(solution)/shard_map/ppermute | solution.py:223
  55.8 7.2 %shard_map.57.rest_2_ = bf16[8,64,1536]{2,1,0:T(8,128)(2,1)} custom-call(s32[6144]{0:T(1024)S(1)} %bitcast.10, s32[1]{0:T(128)} %bitcast.7.part_ref, bf16[8,64,1920]{2,1,0:T(8,128)(2,1)S(1)} %copy-done.1, bf16[32,64,320]{2,1,0:T(8,128)(2,1)} %rest_0_.1, bf16[40,64,128]{2,1,0:T(8,128)(2,1)S(1)} %maximum_select_fusion.rest_1_), custom_call_target="tpu_custom_call" | custom-call | flops 755000000 | bytes 20971520 | tf_op jit(solution)/shard_map/pallas_call | solution.py:116
  63.0 0.0 collective-permute-done.7
  63.0 0.1 collective-permute-start.2
  63.1 0.0 collective-permute-done.6.rest_0_
  63.1 0.0 collective-permute-done.8.rest_1_
  63.1 7.2 %shard_map.58.rest_3_ = bf16[8,64,1536]{2,1,0:T(8,128)(2,1)} custom-call(s32[6144]{0:T(1024)S(1)} %bitcast.11, s32[1]{0:T(128)} %bitcast.6.part_ref, bf16[8,64,1920]{2,1,0:T(8,128)(2,1)S(1)} %copy-done.1, bf16[32,64,320]{2,1,0:T(8,128)(2,1)} %collective-permute-done.6.rest_0_, ...), custom_call_target="tpu_custom_call", output_to_operand_aliasing={{}: (5, {})} | custom-call | flops 755000000 | bytes 20971520 | tf_op jit(solution)/shard_map/pallas_call | solution.py:116
  70.3 3.6 %collective-permute-done.9.rest_1_ = bf16[40,64,128]{2,1,0:T(8,128)(2,1)} collective-permute-done((bf16[40,64,128]{2,1,0:T(8,128)(2,1)}, bf16[40,64,128]{2,1,0:T(8,128)(2,1)}, u32[]{:S(2)}, u32[]{:S(2)}) %collective-permute-start.9) | collective-permute-done | bytes 655392 | tf_op jit(solution)/shard_map/ppermute | solution.py:237
  73.9 1.2 %broadcast_select_fusion.rest_2_ = bf16[40,64,128]{2,1,0:T(8,128)(2,1)S(1)} fusion(bf16[40,64,128]{2,1,0:T(8,128)(2,1)} %collective-permute-done.7, bf16[40,64,128]{2,1,0:T(8,128)(2,1)} %collective-permute-done.10, pred[]{:T(512)S(6)} %or.3), kind=kLoop, calls=%fused_computation.1 | loop fusion | flops 327680 | bytes 1966081 | tf_op jit(solution)/shard_map/jit(_where)/select_n | solution.py:249
  75.1 0.9 collective-permute-start.12
  76.0 0.3 collective-permute-start.11
  76.3 7.1 %shard_map.59.rest_3_ = bf16[8,64,1536]{2,1,0:T(8,128)(2,1)} custom-call(s32[6144]{0:T(1024)S(1)} %bitcast.12, s32[1]{0:T(128)} %bitcast.8.part_ref, bf16[8,64,1920]{2,1,0:T(8,128)(2,1)S(1)} %copy-done.1, bf16[40,64,128]{2,1,0:T(8,128)(2,1)} %collective-permute-done.rest_0_, ...), custom_call_target="tpu_custom_call", output_to_operand_aliasing={{}: (6, {})} | custom-call | flops 755000000 | bytes 20971520 | tf_op jit(solution)/shard_map/pallas_call | solution.py:116
  83.4 7.1 %shard_map.60 = bf16[8,64,1536]{2,1,0:T(8,128)(2,1)} custom-call(s32[6144]{0:T(1024)S(1)} %bitcast.13, s32[1]{0:T(128)} %bitcast.5.part_ref, bf16[8,64,1920]{2,1,0:T(8,128)(2,1)S(1)} %copy-done.1, bf16[40,64,128]{2,1,0:T(8,128)(2,1)} %collective-permute-done.2.rest_0_, ...), custom_call_target="tpu_custom_call", output_to_operand_aliasing={{}: (6, {})} | custom-call | flops 755000000 | bytes 20971520 | tf_op jit(solution)/shard_map/pallas_call | solution.py:116
  (13 shorter events, 0.0 us)
Async XLA Ops:
  0.0 15.0 %copy-start = (s32[2048,20]{0,1:T(8,128)S(1)}, s32[2048,20]{0,1:T(8,128)}, u32[]{:S(2)}) copy-start(s32[2048,20]{0,1:T(8,128)} %param.8) | copy-start | bytes 491524
  0.0 15.1 %copy-start.3 = (s32[8,24]{1,0:T(8,128)S(1)}, s32[8,24]{1,0:T(8,128)}, u32[]{:S(2)}) copy-start(s32[8,24]{1,0:T(8,128)} %c_ref) | copy-start | bytes 2308
  0.0 15.1 %copy-start.2 = (s32[8,30]{1,0:T(8,128)S(1)}, s32[8,30]{1,0:T(8,128)}, u32[]{:S(2)}) copy-start(s32[8,30]{1,0:T(8,128)} %l_ref.5) | copy-start | bytes 2884
  2.9 17.4 %collective-permute-start = (bf16[40,64,128]{2,1,0:T(8,128)(2,1)}, bf16[40,64,128]{2,1,0:T(8,128)(2,1)}, u32[]{:S(2)}, u32[]{:S(2)}) collective-permute-start(bf16[40,64,128]{2,1,0:T(8,128)(2,1)} %get-tuple-element.22), channel_id=1, source_target_pairs={{0,2},{1,3},{2,0},{3,1},{4,6},{5,7},{6,4},{7,5},{8,10},{9,11},{10,... | collective-permute-start | bytes 1966088 | tf_op jit(solution)/shard_map/ppermute | solution.py:226
  4.8 26.4 %collective-permute-start.5 = (bf16[40,64,128]{2,1,0:T(8,128)(2,1)}, bf16[40,64,128]{2,1,0:T(8,128)(2,1)S(1)}, u32[]{:S(2)}, u32[]{:S(2)}) collective-permute-start(bf16[40,64,128]{2,1,0:T(8,128)(2,1)} %get-tuple-element.31), channel_id=1, source_target_pairs={{0,4},{1,5},{4,8},{5,9},{8,12},{9,13},{12,16},{13,17},{16,20},{17,... | collective-permute-start | bytes 1966088 | tf_op jit(solution)/shard_map/ppermute | solution.py:223
  9.5 46.3 %copy-start.1 = (bf16[8,64,1920]{2,1,0:T(8,128)(2,1)S(1)}, bf16[8,64,1920]{2,1,0:T(8,128)(2,1)}, u32[]{:S(2)}) copy-start(bf16[8,64,1920]{2,1,0:T(8,128)(2,1)} %l_ref.9) | copy-start | bytes 5898244
  9.5 4.1 %collective-permute-start.1 = (bf16[20,64,128]{2,1,0:T(8,128)(2,1)S(1)}, bf16[20,64,128]{2,1,0:T(8,128)(2,1)}, u32[]{:S(2)}, u32[]{:S(2)}) collective-permute-start(bf16[20,64,128]{2,1,0:T(8,128)(2,1)S(1)} %get-tuple-element.38), channel_id=1, source_target_pairs={{124,252},{125,253},{130,2},{131,3}} | collective-permute-start | bytes 983048 | tf_op jit(solution)/shard_map/ppermute | solution.py:223
  11.1 52.0 %collective-permute-start.6 = (bf16[32,64,320]{2,1,0:T(8,128)(2,1)}, bf16[32,64,320]{2,1,0:T(8,128)(2,1)}, u32[]{:S(2)}, u32[]{:S(2)}) collective-permute-start(bf16[32,64,320]{2,1,0:T(8,128)(2,1)} %rest_0_.1), channel_id=1, source_target_pairs={{0,1},{1,0},{2,3},{3,2},{4,5},{5,4},{6,7},{7,6},{8,9},{9,8},{10,11... | collective-permute-start | bytes 3932168 | tf_op jit(solution)/shard_map/ppermute | solution.py:232
  12.3 19.0 %collective-permute-start.3 = (bf16[20,64,128]{2,1,0:T(8,128)(2,1)S(1)}, bf16[20,64,128]{2,1,0:T(8,128)(2,1)}, u32[]{:S(2)}, u32[]{:S(2)}) collective-permute-start(bf16[20,64,128]{2,1,0:T(8,128)(2,1)S(1)} %get-tuple-element.37), channel_id=1, source_target_pairs={{124,128},{125,129},{130,126},{131,127}} | collective-permute-start | bytes 983048 | tf_op jit(solution)/shard_map/ppermute | solution.py:223
  13.6 34.5 %collective-permute-start.4 = (bf16[20,64,128]{2,1,0:T(8,128)(2,1)}, bf16[20,64,128]{2,1,0:T(8,128)(2,1)}, u32[]{:S(2)}, u32[]{:S(2)}) collective-permute-start(bf16[20,64,128]{2,1,0:T(8,128)(2,1)} %collective-permute-done.1), channel_id=1, source_target_pairs={{252,128},{253,129},{2,126},{3,127}} | collective-permute-start | bytes 983048 | tf_op jit(solution)/shard_map/ppermute | solution.py:223
  20.4 42.6 %collective-permute-start.7 = (bf16[40,64,128]{2,1,0:T(8,128)(2,1)}, bf16[40,64,128]{2,1,0:T(8,128)(2,1)}, u32[]{:S(2)}, u32[]{:S(2)}) collective-permute-start(bf16[40,64,128]{2,1,0:T(8,128)(2,1)} %get-tuple-element.22), channel_id=1, source_target_pairs={{126,128},{127,129},{128,126},{129,127}} | collective-permute-start | bytes 1966088 | tf_op jit(solution)/shard_map/ppermute | solution.py:223
  49.2 13.8 %collective-permute-start.8 = (bf16[40,64,128]{2,1,0:T(8,128)(2,1)S(1)}, bf16[40,64,128]{2,1,0:T(8,128)(2,1)S(1)}, u32[]{:S(2)}, u32[]{:S(2)}) collective-permute-start(bf16[40,64,128]{2,1,0:T(8,128)(2,1)S(1)} %maximum_select_fusion.rest_1_), channel_id=1, source_target_pairs={{0,1},{1,0},{2,3},{3,2},{4,5},{5,4},{6,7},{7,6},{8,9},{9,8},{10,11... | collective-permute-start | bytes 1966088 | tf_op jit(solution)/shard_map/ppermute | solution.py:242
  53.6 16.7 %collective-permute-start.10 = (bf16[40,64,128]{2,1,0:T(8,128)(2,1)}, bf16[40,64,128]{2,1,0:T(8,128)(2,1)}, u32[]{:S(2)}, u32[]{:S(2)}) collective-permute-start(bf16[40,64,128]{2,1,0:T(8,128)(2,1)} %collective-permute-done.rest_0_), channel_id=1, source_target_pairs={{0,4},{1,5},{4,8},{5,9},{8,12},{9,13},{12,16},{13,17},{16,20},{17,... | collective-permute-start | bytes 1966088 | tf_op jit(solution)/shard_map/ppermute | solution.py:223
  55.8 18.2 %collective-permute-start.9 = (bf16[40,64,128]{2,1,0:T(8,128)(2,1)}, bf16[40,64,128]{2,1,0:T(8,128)(2,1)}, u32[]{:S(2)}, u32[]{:S(2)}) collective-permute-start(bf16[40,64,128]{2,1,0:T(8,128)(2,1)} %get-tuple-element.31), channel_id=1, source_target_pairs={{0,2},{1,3},{2,0},{3,1},{4,6},{5,7},{6,4},{7,5},{8,10},{9,11},{10,... | collective-permute-start | bytes 1966088 | tf_op jit(solution)/shard_map/ppermute | solution.py:237
  63.0 20.4 %collective-permute-start.2 = (bf16[40,64,128]{2,1,0:T(8,128)(2,1)}, bf16[40,64,128]{2,1,0:T(8,128)(2,1)}, u32[]{:S(2)}, u32[]{:S(2)}) collective-permute-start(bf16[40,64,128]{2,1,0:T(8,128)(2,1)} %collective-permute-done.rest_0_), channel_id=1, source_target_pairs={{0,1},{1,0},{2,3},{3,2},{4,5},{5,4},{6,7},{7,6},{8,9},{9,8},{10,11... | collective-permute-start | bytes 1966088 | tf_op jit(solution)/shard_map/ppermute | solution.py:239
  75.1 8.3 %collective-permute-start.12 = (bf16[40,64,128]{2,1,0:T(8,128)(2,1)S(1)}, bf16[40,64,128]{2,1,0:T(8,128)(2,1)S(1)}, u32[]{:S(2)}, u32[]{:S(2)}) collective-permute-start(bf16[40,64,128]{2,1,0:T(8,128)(2,1)S(1)} %broadcast_select_fusion.rest_2_), channel_id=1, source_target_pairs={{0,1},{1,0},{2,3},{3,2},{4,5},{5,4},{6,7},{7,6},{8,9},{9,8},{10,11... | collective-permute-start | bytes 1966088 | tf_op jit(solution)/shard_map/ppermute | solution.py:250
  76.0 7.4 %collective-permute-start.11 = (bf16[40,64,128]{2,1,0:T(8,128)(2,1)}, bf16[40,64,128]{2,1,0:T(8,128)(2,1)}, u32[]{:S(2)}, u32[]{:S(2)}) collective-permute-start(bf16[40,64,128]{2,1,0:T(8,128)(2,1)} %collective-permute-done.9.rest_1_), channel_id=1, source_target_pairs={{0,1},{1,0},{2,3},{3,2},{4,5},{5,4},{6,7},{7,6},{8,9},{9,8},{10,11... | collective-permute-start | bytes 1966088 | tf_op jit(solution)/shard_map/ppermute | solution.py:248

commit v7 on v4

--- a/solution.py
+++ b/solution.py
@@ -45,8 +45,10 @@
     )(start, s_blocks)
 
 
-def product_body(count, tab_ref, part_ref, l_ref, *rest):
-    o_ref, sd_ref, ob_ref, sem = rest[-4:]
+def product_body(count, tab_hbm, part_ref, l_ref, *rest):
+    o_ref, sd_ref, ob_ref, tab_ref, sem, tab_sem = rest[-6:]
+    load = pltpu.make_async_copy(tab_hbm, tab_ref, tab_sem)
+    load.start()
     rows = l_ref.shape[0]
     base = 0
     for piece in rest[:count]:
@@ -69,6 +71,7 @@
         base += 2 * TILES if packed else RAW
     for zero in (ZERO, ZERO + 1):
         sd_ref[zero] = jnp.zeros((64, 128), jnp.bfloat16)
+    load.wait()
     part = part_ref[0]
     low = lax.broadcasted_iota(jnp.int32, (64, 128), 1) < 64
 
@@ -106,7 +109,7 @@
 def product(tab, part, l_blocks, pieces, prev):
     rows = l_blocks.shape[0]
     vmem, smem = pl.BlockSpec(memory_space=pltpu.VMEM), pl.BlockSpec(memory_space=pltpu.SMEM)
-    in_specs = [smem, smem] + [vmem] * (1 + len(pieces))
+    in_specs = [pl.BlockSpec(memory_space=pl.ANY), smem] + [vmem] * (1 + len(pieces))
     args = [tab, part, l_blocks, *pieces]
     aliases = {}
     if prev is not None:
@@ -121,7 +124,9 @@
         scratch_shapes=[
             pltpu.VMEM((ZERO + 2, 64, 128), jnp.bfloat16),
             pltpu.VMEM((rows, 64, 384), jnp.bfloat16),
+            pltpu.SMEM(tab.shape, jnp.int32),
             pltpu.SemaphoreType.DMA((rows,)),
+            pltpu.SemaphoreType.DMA,
         ],
         input_output_aliases=aliases,
         compiler_params=pltpu.CompilerParams(vmem_limit_bytes=24 << 20),
@@ -227,15 +232,14 @@
     tab = table(h, r, l_index, s_cols, c_index)
     second, halo, tab = lax.optimization_barrier((second, halo, tab))
     far_second = across(second)
-
+    mate_halo = beside(halo)
+    parts = [(c ^ flip).reshape(1) for flip in range(4)]
+    out = product(tab, parts[0], l_blocks, (s_blocks, halo), None)
+    out, far_first = lax.optimization_barrier((out, far_first))
     far_halo = send(far_first, plain)
     cross_first = beside(far_first)
-    mate_halo = beside(halo)
-    tab, far_first, seam_halo = lax.optimization_barrier((tab, far_first, seam_halo))
-    parts = [(c ^ flip).reshape(1) for flip in range(4)]
-    out = product(tab, parts[0], l_blocks, (s_blocks, halo), None)
     out = product(tab, parts[1], l_blocks, (mate, mate_halo), out)
-    out, far_second, far_halo = lax.optimization_barrier((out, far_second, far_halo))
+    out, far_second, far_halo, seam_halo = lax.optimization_barrier((out, far_second, far_halo, seam_halo))
     cross_second = beside(far_second)
     far_halo = jnp.where(takes, seam_halo, far_halo)
     cross_halo = beside(far_halo)

time: 80.4 us -> 80.8 us (level)
  the two profiles are of different devices: /device:TPU:3 before, /device:TPU:253 now
where the time goes in v7:
time: 80.8 us; the launch traced here: 80.5 us
  Pallas kernels  33 us (41%)
  waiting for transfers between devices  27.9 us (35%)
  starting transfers between devices  18 us (22%)
  other arithmetic  1.24 us (2%)
    pallas_call x4, Pallas kernels, product(): pl.pallas_call(functools.partial(product_body, len(pieces)), out_shape=ja...  28.6 us
    ppermute x3, waiting for transfers between devices, send(): return lax.ppermute(x, ('rows', 'cols'), perm)  23.5 us
    ppermute x3, starting transfers between devices, send(): return lax.ppermute(x, ('rows', 'cols'), perm)  12.8 us
    ppermute x1, waiting for transfers between devices, shards(): far_second = across(second)  4.36 us
    pallas_call x1, Pallas kernels, pack(): pl.pallas_call(pack_body, out_shape=(piece, piece), in_specs=[pl.BlockSpe...  3.04 us
    ppermute x1, starting transfers between devices, shards(): mate_halo = beside(halo)  2.98 us
  transfers between devices with their start and end apart: 10, of which 3 were waited for; matrix products, arithmetic and copies ran while one was open for 2% of the time, Pallas kernels for 28%

profile of v7, /device:TPU:253, one launch (start us, length us, event | category | flops | bytes accessed | tf_op | source)
XLA Modules:
  0.0 80.5 jit_solution(2031978592423115857)
XLA Ops:
  0.0 0.0 copy-start
  0.0 0.0 copy-start.1
  0.0 3.0 %shard_map.55 = (bf16[40,64,128]{2,1,0:T(8,128)(2,1)}, bf16[40,64,128]{2,1,0:T(8,128)(2,1)}) custom-call(s32[1]{0:T(128)} %bitcast.start_ref, bf16[32,64,320]{2,1,0:T(8,128)(2,1)} %rest_0_.1), custom_call_target="tpu_custom_call" | custom-call | bytes 3145728 | tf_op jit(solution)/shard_map/pallas_call | solution.py:38
  3.1 2.6 %collective-permute-start = (bf16[40,64,128]{2,1,0:T(8,128)(2,1)}, bf16[40,64,128]{2,1,0:T(8,128)(2,1)S(1)}, u32[]{:S(2)}, u32[]{:S(2)}) collective-permute-start(bf16[40,64,128]{2,1,0:T(8,128)(2,1)} %get-tuple-element.24), channel_id=1, source_target_pairs={{0,4},{1,5},{4,8},{5,9},{8,12},{9,13},{12,16},{13,17},{16,20},{17,... | collective-permute-start | bytes 1966088 | tf_op jit(solution)/shard_map/ppermute | solution.py:224
  5.7 1.0 %collective-permute-start.3 = (bf16[32,64,320]{2,1,0:T(8,128)(2,1)}, bf16[32,64,320]{2,1,0:T(8,128)(2,1)}, u32[]{:S(2)}, u32[]{:S(2)}) collective-permute-start(bf16[32,64,320]{2,1,0:T(8,128)(2,1)} %rest_0_.1), channel_id=1, source_target_pairs={{0,1},{1,0},{2,3},{3,2},{4,5},{5,4},{6,7},{7,6},{8,9},{9,8},{10,11... | collective-permute-start | bytes 3932168 | tf_op jit(solution)/shard_map/ppermute | solution.py:231
  6.8 0.0 collective-permute-start.1
  6.8 8.1 %collective-permute-start.7 = (bf16[40,64,128]{2,1,0:T(8,128)(2,1)}, bf16[40,64,128]{2,1,0:T(8,128)(2,1)}, u32[]{:S(2)}, u32[]{:S(2)}) collective-permute-start(bf16[40,64,128]{2,1,0:T(8,128)(2,1)} %get-tuple-element.20), channel_id=1, source_target_pairs={{126,128},{127,129},{128,126},{129,127}} | collective-permute-start | bytes 1966088 | tf_op jit(solution)/shard_map/ppermute | solution.py:224
  14.8 0.1 pad_add_fusion.at_ref
  14.9 0.0 copy-done
  14.9 0.1 dynamic-slice_bitcast_fusion.near_ref
  15.0 1.3 %shard_map.56 = s32[48,128]{1,0:T(8,128)S(1)} custom-call(s32[3]{0:T(128)S(1)} %pad_add_fusion.at_ref, s32[20,64]{1,0:T(8,128)S(1)} %dynamic-slice_bitcast_fusion.near_ref, s32[8,30]{1,0:T(8,128)S(1)} %copy-done.2, s32[8,24]{1,0:T(8,128)S(1)} %copy-done.3), custom_call_target="tpu_custom_call" | custom-call | flops 268435456 | bytes 8388608 | tf_op jit(solution)/shard_map/pallas_call | solution.py:198
  16.3 16.9 %collective-permute-done.rest_1_ = bf16[40,64,128]{2,1,0:T(8,128)(2,1)S(1)} collective-permute-done((bf16[40,64,128]{2,1,0:T(8,128)(2,1)}, bf16[40,64,128]{2,1,0:T(8,128)(2,1)S(1)}, u32[]{:S(2)}, u32[]{:S(2)}) %collective-permute-start) | collective-permute-done | bytes 655392 | tf_op jit(solution)/shard_map/ppermute | solution.py:224
  33.2 3.0 %collective-permute-start.4 = (bf16[40,64,128]{2,1,0:T(8,128)(2,1)S(1)}, bf16[40,64,128]{2,1,0:T(8,128)(2,1)S(1)}, u32[]{:S(2)}, u32[]{:S(2)}) collective-permute-start(bf16[40,64,128]{2,1,0:T(8,128)(2,1)S(1)} %collective-permute-done.rest_1_), channel_id=1, source_target_pairs={{0,1},{1,0},{2,3},{3,2},{4,5},{5,4},{6,7},{7,6},{8,9},{9,8},{10,11... | collective-permute-start | bytes 1966088 | tf_op jit(solution)/shard_map/ppermute | solution.py:235
  36.2 7.2 %shard_map.57.rest_2_ = bf16[8,64,1536]{2,1,0:T(8,128)(2,1)} custom-call(s32[6144]{0:T(1024)S(1)} %bitcast.10, s32[1]{0:T(128)} %bitcast.6.part_ref, bf16[8,64,1920]{2,1,0:T(8,128)(2,1)S(1)} %copy-done.1, bf16[32,64,320]{2,1,0:T(8,128)(2,1)} %rest_0_.1, bf16[40,64,128]{2,1,0:T(8,128)(2,1)S(1)} %collective-permute-done.rest_1_), custom_call_target="tpu_custom_call" | custom-call | flops 755000000 | bytes 20971520 | tf_op jit(solution)/shard_map/pallas_call | solution.py:119
  43.4 0.0 collective-permute-done.1.rest_0_
  43.4 2.1 %collective-permute-start.6 = (bf16[40,64,128]{2,1,0:T(8,128)(2,1)}, bf16[40,64,128]{2,1,0:T(8,128)(2,1)}, u32[]{:S(2)}, u32[]{:S(2)}) collective-permute-start(bf16[40,64,128]{2,1,0:T(8,128)(2,1)} %collective-permute-done.1.rest_0_), channel_id=1, source_target_pairs={{0,4},{1,5},{4,8},{5,9},{8,12},{9,13},{12,16},{13,17},{16,20},{17,... | collective-permute-start | bytes 1966088 | tf_op jit(solution)/shard_map/ppermute | solution.py:224
  45.5 0.0 collective-permute-start.5
  45.5 0.0 collective-permute-done.3.rest_0_
  45.5 0.0 collective-permute-start.2
  45.5 0.0 collective-permute-done.4.rest_1_
  45.6 7.2 %shard_map.58.rest_3_ = bf16[8,64,1536]{2,1,0:T(8,128)(2,1)} custom-call(s32[6144]{0:T(1024)S(1)} %bitcast.11, s32[1]{0:T(128)} %bitcast.7.part_ref, bf16[8,64,1920]{2,1,0:T(8,128)(2,1)S(1)} %copy-done.1, bf16[32,64,320]{2,1,0:T(8,128)(2,1)} %collective-permute-done.3.rest_0_, ...), custom_call_target="tpu_custom_call", output_to_operand_aliasing={{}: (5, {})} | custom-call | flops 755000000 | bytes 20971520 | tf_op jit(solution)/shard_map/pallas_call | solution.py:119
  52.8 0.0 collective-permute-done.7
  52.8 6.6 %collective-permute-done.6 = bf16[40,64,128]{2,1,0:T(8,128)(2,1)} collective-permute-done((bf16[40,64,128]{2,1,0:T(8,128)(2,1)}, bf16[40,64,128]{2,1,0:T(8,128)(2,1)}, u32[]{:S(2)}, u32[]{:S(2)}) %collective-permute-start.6) | collective-permute-done | bytes 655392 | tf_op jit(solution)/shard_map/ppermute | solution.py:224
  59.4 4.4 %collective-permute-done.5.rest_1_ = bf16[40,64,128]{2,1,0:T(8,128)(2,1)} collective-permute-done((bf16[40,64,128]{2,1,0:T(8,128)(2,1)}, bf16[40,64,128]{2,1,0:T(8,128)(2,1)}, u32[]{:S(2)}, u32[]{:S(2)}) %collective-permute-start.5) | collective-permute-done | bytes 655392 | tf_op jit(solution)/shard_map/ppermute | solution.py:234
  63.7 1.2 %broadcast_select_fusion.rest_2_ = bf16[40,64,128]{2,1,0:T(8,128)(2,1)S(1)} fusion(bf16[40,64,128]{2,1,0:T(8,128)(2,1)} %collective-permute-done.7, bf16[40,64,128]{2,1,0:T(8,128)(2,1)} %collective-permute-done.6, pred[]{:T(512)S(6)} %or.3), kind=kLoop, calls=%fused_computation | loop fusion | flops 327680 | bytes 1966081 | tf_op jit(solution)/shard_map/jit(_where)/select_n | solution.py:244
  64.9 0.9 %collective-permute-start.9 = (bf16[40,64,128]{2,1,0:T(8,128)(2,1)S(1)}, bf16[40,64,128]{2,1,0:T(8,128)(2,1)S(1)}, u32[]{:S(2)}, u32[]{:S(2)}) collective-permute-start(bf16[40,64,128]{2,1,0:T(8,128)(2,1)S(1)} %broadcast_select_fusion.rest_2_), channel_id=1, source_target_pairs={{0,1},{1,0},{2,3},{3,2},{4,5},{5,4},{6,7},{7,6},{8,9},{9,8},{10,11... | collective-permute-start | bytes 1966088 | tf_op jit(solution)/shard_map/ppermute | solution.py:245
  65.8 0.3 collective-permute-start.8
  66.0 7.1 %shard_map.59.rest_3_ = bf16[8,64,1536]{2,1,0:T(8,128)(2,1)} custom-call(s32[6144]{0:T(1024)S(1)} %bitcast.12, s32[1]{0:T(128)} %bitcast.8.part_ref, bf16[8,64,1920]{2,1,0:T(8,128)(2,1)S(1)} %copy-done.1, bf16[40,64,128]{2,1,0:T(8,128)(2,1)} %collective-permute-done.1.rest_0_, ...), custom_call_target="tpu_custom_call", output_to_operand_aliasing={{}: (6, {})} | custom-call | flops 755000000 | bytes 20971520 | tf_op jit(solution)/shard_map/pallas_call | solution.py:119
  73.2 0.0 collective-permute-done.2.rest_0_
  73.2 0.0 collective-permute-done.9.rest_2_
  73.2 0.0 collective-permute-done.8.rest_1_
  73.2 7.1 %shard_map.60 = bf16[8,64,1536]{2,1,0:T(8,128)(2,1)} custom-call(s32[6144]{0:T(1024)S(1)} %bitcast.13, s32[1]{0:T(128)} %bitcast.5.part_ref, bf16[8,64,1920]{2,1,0:T(8,128)(2,1)S(1)} %copy-done.1, bf16[40,64,128]{2,1,0:T(8,128)(2,1)} %collective-permute-done.2.rest_0_, ...), custom_call_target="tpu_custom_call", output_to_operand_aliasing={{}: (6, {})} | custom-call | flops 755000000 | bytes 20971520 | tf_op jit(solution)/shard_map/pallas_call | solution.py:119
  (5 shorter events, 0.0 us)
Async XLA Ops:
  0.0 14.9 %copy-start = (s32[2048,20]{0,1:T(8,128)S(1)}, s32[2048,20]{0,1:T(8,128)}, u32[]{:S(2)}) copy-start(s32[2048,20]{0,1:T(8,128)} %param.8) | copy-start | bytes 491524
  0.0 15.0 %copy-start.2 = (s32[8,30]{1,0:T(8,128)S(1)}, s32[8,30]{1,0:T(8,128)}, u32[]{:S(2)}) copy-start(s32[8,30]{1,0:T(8,128)} %l_ref.5) | copy-start | bytes 2884
  0.0 15.0 %copy-start.3 = (s32[8,24]{1,0:T(8,128)S(1)}, s32[8,24]{1,0:T(8,128)}, u32[]{:S(2)}) copy-start(s32[8,24]{1,0:T(8,128)} %c_ref.1) | copy-start | bytes 2308
  0.0 36.2 %copy-start.1 = (bf16[8,64,1920]{2,1,0:T(8,128)(2,1)S(1)}, bf16[8,64,1920]{2,1,0:T(8,128)(2,1)}, u32[]{:S(2)}) copy-start(bf16[8,64,1920]{2,1,0:T(8,128)(2,1)} %l_ref.9) | copy-start | bytes 5898244
  3.1 30.1 %collective-permute-start = (bf16[40,64,128]{2,1,0:T(8,128)(2,1)}, bf16[40,64,128]{2,1,0:T(8,128)(2,1)S(1)}, u32[]{:S(2)}, u32[]{:S(2)}) collective-permute-start(bf16[40,64,128]{2,1,0:T(8,128)(2,1)} %get-tuple-element.24), channel_id=1, source_target_pairs={{0,4},{1,5},{4,8},{5,9},{8,12},{9,13},{12,16},{13,17},{16,20},{17,... | collective-permute-start | bytes 1966088 | tf_op jit(solution)/shard_map/ppermute | solution.py:224
  5.7 39.8 %collective-permute-start.3 = (bf16[32,64,320]{2,1,0:T(8,128)(2,1)}, bf16[32,64,320]{2,1,0:T(8,128)(2,1)}, u32[]{:S(2)}, u32[]{:S(2)}) collective-permute-start(bf16[32,64,320]{2,1,0:T(8,128)(2,1)} %rest_0_.1), channel_id=1, source_target_pairs={{0,1},{1,0},{2,3},{3,2},{4,5},{5,4},{6,7},{7,6},{8,9},{9,8},{10,11... | collective-permute-start | bytes 3932168 | tf_op jit(solution)/shard_map/ppermute | solution.py:231
  6.8 36.6 %collective-permute-start.1 = (bf16[40,64,128]{2,1,0:T(8,128)(2,1)}, bf16[40,64,128]{2,1,0:T(8,128)(2,1)}, u32[]{:S(2)}, u32[]{:S(2)}) collective-permute-start(bf16[40,64,128]{2,1,0:T(8,128)(2,1)} %get-tuple-element.20), channel_id=1, source_target_pairs={{0,2},{1,3},{2,0},{3,1},{4,6},{5,7},{6,4},{7,5},{8,10},{9,11},{10,... | collective-permute-start | bytes 1966088 | tf_op jit(solution)/shard_map/ppermute | solution.py:227
  6.8 46.0 %collective-permute-start.7 = (bf16[40,64,128]{2,1,0:T(8,128)(2,1)}, bf16[40,64,128]{2,1,0:T(8,128)(2,1)}, u32[]{:S(2)}, u32[]{:S(2)}) collective-permute-start(bf16[40,64,128]{2,1,0:T(8,128)(2,1)} %get-tuple-element.20), channel_id=1, source_target_pairs={{126,128},{127,129},{128,126},{129,127}} | collective-permute-start | bytes 1966088 | tf_op jit(solution)/shard_map/ppermute | solution.py:224
  33.2 12.3 %collective-permute-start.4 = (bf16[40,64,128]{2,1,0:T(8,128)(2,1)S(1)}, bf16[40,64,128]{2,1,0:T(8,128)(2,1)S(1)}, u32[]{:S(2)}, u32[]{:S(2)}) collective-permute-start(bf16[40,64,128]{2,1,0:T(8,128)(2,1)S(1)} %collective-permute-done.rest_1_), channel_id=1, source_target_pairs={{0,1},{1,0},{2,3},{3,2},{4,5},{5,4},{6,7},{7,6},{8,9},{9,8},{10,11... | collective-permute-start | bytes 1966088 | tf_op jit(solution)/shard_map/ppermute | solution.py:235
  43.4 16.0 %collective-permute-start.6 = (bf16[40,64,128]{2,1,0:T(8,128)(2,1)}, bf16[40,64,128]{2,1,0:T(8,128)(2,1)}, u32[]{:S(2)}, u32[]{:S(2)}) collective-permute-start(bf16[40,64,128]{2,1,0:T(8,128)(2,1)} %collective-permute-done.1.rest_0_), channel_id=1, source_target_pairs={{0,4},{1,5},{4,8},{5,9},{8,12},{9,13},{12,16},{13,17},{16,20},{17,... | collective-permute-start | bytes 1966088 | tf_op jit(solution)/shard_map/ppermute | solution.py:224
  45.5 18.2 %collective-permute-start.5 = (bf16[40,64,128]{2,1,0:T(8,128)(2,1)}, bf16[40,64,128]{2,1,0:T(8,128)(2,1)}, u32[]{:S(2)}, u32[]{:S(2)}) collective-permute-start(bf16[40,64,128]{2,1,0:T(8,128)(2,1)} %get-tuple-element.24), channel_id=1, source_target_pairs={{0,2},{1,3},{2,0},{3,1},{4,6},{5,7},{6,4},{7,5},{8,10},{9,11},{10,... | collective-permute-start | bytes 1966088 | tf_op jit(solution)/shard_map/ppermute | solution.py:234
  45.5 27.6 %collective-permute-start.2 = (bf16[40,64,128]{2,1,0:T(8,128)(2,1)}, bf16[40,64,128]{2,1,0:T(8,128)(2,1)}, u32[]{:S(2)}, u32[]{:S(2)}) collective-permute-start(bf16[40,64,128]{2,1,0:T(8,128)(2,1)} %collective-permute-done.1.rest_0_), channel_id=1, source_target_pairs={{0,1},{1,0},{2,3},{3,2},{4,5},{5,4},{6,7},{7,6},{8,9},{9,8},{10,11... | collective-permute-start | bytes 1966088 | tf_op jit(solution)/shard_map/ppermute | solution.py:240
  64.9 8.3 %collective-permute-start.9 = (bf16[40,64,128]{2,1,0:T(8,128)(2,1)S(1)}, bf16[40,64,128]{2,1,0:T(8,128)(2,1)S(1)}, u32[]{:S(2)}, u32[]{:S(2)}) collective-permute-start(bf16[40,64,128]{2,1,0:T(8,128)(2,1)S(1)} %broadcast_select_fusion.rest_2_), channel_id=1, source_target_pairs={{0,1},{1,0},{2,3},{3,2},{4,5},{5,4},{6,7},{7,6},{8,9},{9,8},{10,11... | collective-permute-start | bytes 1966088 | tf_op jit(solution)/shard_map/ppermute | solution.py:245
  65.8 7.4 %collective-permute-start.8 = (bf16[40,64,128]{2,1,0:T(8,128)(2,1)}, bf16[40,64,128]{2,1,0:T(8,128)(2,1)}, u32[]{:S(2)}, u32[]{:S(2)}) collective-permute-start(bf16[40,64,128]{2,1,0:T(8,128)(2,1)} %collective-permute-done.5.rest_1_), channel_id=1, source_target_pairs={{0,1},{1,0},{2,3},{3,2},{4,5},{5,4},{6,7},{7,6},{8,9},{9,8},{10,11... | collective-permute-start | bytes 1966088 | tf_op jit(solution)/shard_map/ppermute | solution.py:243

commit v8 on v5

--- a/solution.py
+++ b/solution.py
@@ -225,15 +225,15 @@
     mate, first = lax.optimization_barrier((s_blocks, first))
     mate = beside(mate)
     tab = table(h, r, l_index, s_cols, c_index)
-    second, far_first, tab = lax.optimization_barrier((second, far_first, tab))
-    far_second = across(second)
+    far_first, tab = lax.optimization_barrier((far_first, tab))
     far_halo = send(far_first, plain)
     cross_first = beside(far_first)
     halo, far_first = lax.optimization_barrier((halo, far_first))
     mate_halo = beside(halo)
     parts = [(c ^ flip).reshape(1) for flip in range(4)]
     out = product(tab, parts[0], l_blocks, (s_blocks, halo), None)
-    out, mate, seam_halo = lax.optimization_barrier((out, mate, seam_halo))
+    out, mate, seam_halo, second = lax.optimization_barrier((out, mate, seam_halo, second))
+    far_second = across(second)
     out = product(tab, parts[1], l_blocks, (mate, mate_halo), out)
     out, far_second, far_halo = lax.optimization_barrier((out, far_second, far_halo))
     cross_second = beside(far_second)

time: 79.7 us -> 87.5 us (1.098)
  the two profiles are of different devices: /device:TPU:7 before, /device:TPU:3 now
where the time goes in v8:
time: 87.5 us; the launch traced here: 87.2 us
  Pallas kernels  32.9 us (38%)
  waiting for transfers between devices  31.1 us (36%)
  starting transfers between devices  21.6 us (25%)
  other arithmetic  1.24 us (1%)
    pallas_call x4, Pallas kernels, product(): pl.pallas_call(functools.partial(product_body, len(pieces)), out_shape=ja...  28.6 us
    ppermute x3, waiting for transfers between devices, send(): return lax.ppermute(x, ('rows', 'cols'), perm)  17.2 us
    ppermute x3, starting transfers between devices, send(): return lax.ppermute(x, ('rows', 'cols'), perm)  16.3 us
    ppermute x1, waiting for transfers between devices, shards(): far_second = across(second)  10.8 us
    pallas_call x1, Pallas kernels, pack(): pl.pallas_call(pack_body, out_shape=(piece, piece), in_specs=[pl.BlockSpe...  3.04 us
    ppermute x1, waiting for transfers between devices, shards(): far_first = across(first)  3 us
    ppermute x1, starting transfers between devices, shards(): far_first = across(first)  1.84 us
  transfers between devices with their start and end apart: 10, of which 3 were waited for; matrix products, arithmetic and copies ran while one was open for 2% of the time, Pallas kernels for 26%

profile of v8, /device:TPU:3, one launch (start us, length us, event | category | flops | bytes accessed | tf_op | source)
XLA Modules:
  0.0 87.2 jit_solution(12744805584471949905)
XLA Ops:
  0.0 0.0 copy-start
  0.0 0.0 copy-start.1
  0.0 3.0 %shard_map.55 = (bf16[40,64,128]{2,1,0:T(8,128)(2,1)}, bf16[40,64,128]{2,1,0:T(8,128)(2,1)}) custom-call(s32[1]{0:T(128)} %bitcast.start_ref, bf16[32,64,320]{2,1,0:T(8,128)(2,1)} %rest_0_.1), custom_call_target="tpu_custom_call" | custom-call | bytes 3145728 | tf_op jit(solution)/shard_map/pallas_call | solution.py:38
  3.1 0.7 collective-permute-start.3
  3.7 1.8 %collective-permute-start = (bf16[40,64,128]{2,1,0:T(8,128)(2,1)}, bf16[40,64,128]{2,1,0:T(8,128)(2,1)}, u32[]{:S(2)}, u32[]{:S(2)}) collective-permute-start(bf16[40,64,128]{2,1,0:T(8,128)(2,1)} %get-tuple-element.19), channel_id=1, source_target_pairs={{0,2},{1,3},{2,0},{3,1},{4,6},{5,7},{6,4},{7,5},{8,10},{9,11},{10,... | collective-permute-start | bytes 1966088 | tf_op jit(solution)/shard_map/ppermute | solution.py:222
  5.6 3.5 %collective-permute-start.2 = (bf16[40,64,128]{2,1,0:T(8,128)(2,1)}, bf16[40,64,128]{2,1,0:T(8,128)(2,1)S(1)}, u32[]{:S(2)}, u32[]{:S(2)}) collective-permute-start(bf16[40,64,128]{2,1,0:T(8,128)(2,1)} %get-tuple-element.27), channel_id=1, source_target_pairs={{0,4},{1,5},{4,8},{5,9},{8,12},{9,13},{12,16},{13,17},{16,20},{17,... | collective-permute-start | bytes 1966088 | tf_op jit(solution)/shard_map/ppermute | solution.py:219
  9.1 8.3 %collective-permute-start.4 = (bf16[40,64,128]{2,1,0:T(8,128)(2,1)}, bf16[40,64,128]{2,1,0:T(8,128)(2,1)}, u32[]{:S(2)}, u32[]{:S(2)}) collective-permute-start(bf16[40,64,128]{2,1,0:T(8,128)(2,1)} %get-tuple-element.19), channel_id=1, source_target_pairs={{126,128},{127,129},{128,126},{129,127}} | collective-permute-start | bytes 1966088 | tf_op jit(solution)/shard_map/ppermute | solution.py:219
  17.5 0.1 pad_add_fusion.at_ref
  17.6 0.1 dynamic-slice_bitcast_fusion.near_ref
  17.6 0.0 copy-done.2
  17.6 1.3 %shard_map.56 = s32[48,128]{1,0:T(8,128)S(1)} custom-call(s32[3]{0:T(128)S(1)} %pad_add_fusion.at_ref, s32[20,64]{1,0:T(8,128)S(1)} %dynamic-slice_bitcast_fusion.near_ref, s32[8,30]{1,0:T(8,128)S(1)} %copy-done.2, s32[8,24]{1,0:T(8,128)S(1)} %copy-done.3), custom_call_target="tpu_custom_call" | custom-call | flops 268435456 | bytes 8388608 | tf_op jit(solution)/shard_map/pallas_call | solution.py:193
  18.9 3.0 %collective-permute-done.rest_0_ = bf16[40,64,128]{2,1,0:T(8,128)(2,1)} collective-permute-done((bf16[40,64,128]{2,1,0:T(8,128)(2,1)}, bf16[40,64,128]{2,1,0:T(8,128)(2,1)}, u32[]{:S(2)}, u32[]{:S(2)}) %collective-permute-start) | collective-permute-done | bytes 655392 | tf_op jit(solution)/shard_map/ppermute | solution.py:222
  21.9 4.4 %collective-permute-start.7 = (bf16[40,64,128]{2,1,0:T(8,128)(2,1)}, bf16[40,64,128]{2,1,0:T(8,128)(2,1)}, u32[]{:S(2)}, u32[]{:S(2)}) collective-permute-start(bf16[40,64,128]{2,1,0:T(8,128)(2,1)} %collective-permute-done.rest_0_), channel_id=1, source_target_pairs={{0,4},{1,5},{4,8},{5,9},{8,12},{9,13},{12,16},{13,17},{16,20},{17,... | collective-permute-start | bytes 1966088 | tf_op jit(solution)/shard_map/ppermute | solution.py:219
  26.3 17.2 %collective-permute-done.2.rest_1_ = bf16[40,64,128]{2,1,0:T(8,128)(2,1)S(1)} collective-permute-done((bf16[40,64,128]{2,1,0:T(8,128)(2,1)}, bf16[40,64,128]{2,1,0:T(8,128)(2,1)S(1)}, u32[]{:S(2)}, u32[]{:S(2)}) %collective-permute-start.2) | collective-permute-done | bytes 655392 | tf_op jit(solution)/shard_map/ppermute | solution.py:219
  43.5 1.5 %collective-permute-start.5 = (bf16[40,64,128]{2,1,0:T(8,128)(2,1)S(1)}, bf16[40,64,128]{2,1,0:T(8,128)(2,1)S(1)}, u32[]{:S(2)}, u32[]{:S(2)}) collective-permute-start(bf16[40,64,128]{2,1,0:T(8,128)(2,1)S(1)} %collective-permute-done.2.rest_1_), channel_id=1, source_target_pairs={{0,1},{1,0},{2,3},{3,2},{4,5},{5,4},{6,7},{7,6},{8,9},{9,8},{10,11... | collective-permute-start | bytes 1966088 | tf_op jit(solution)/shard_map/ppermute | solution.py:232
  45.0 7.2 %shard_map.57.rest_2_ = bf16[8,64,1536]{2,1,0:T(8,128)(2,1)} custom-call(s32[6144]{0:T(1024)S(1)} %bitcast.10, s32[1]{0:T(128)} %bitcast.7.part_ref, bf16[8,64,1920]{2,1,0:T(8,128)(2,1)S(1)} %copy-done.1, bf16[32,64,320]{2,1,0:T(8,128)(2,1)} %rest_0_.1, bf16[40,64,128]{2,1,0:T(8,128)(2,1)S(1)} %collective-permute-done.2.rest_1_), custom_call_target="tpu_custom_call" | custom-call | flops 755000000 | bytes 20971520 | tf_op jit(solution)/shard_map/pallas_call | solution.py:116
  52.2 0.0 collective-permute-done.4
  52.2 0.0 collective-permute-done.3.rest_0_
  52.2 0.1 collective-permute-start.6
  52.3 0.1 collective-permute-start.1
  52.4 0.0 collective-permute-done.5.rest_1_
  52.4 7.2 %shard_map.58.rest_3_ = bf16[8,64,1536]{2,1,0:T(8,128)(2,1)} custom-call(s32[6144]{0:T(1024)S(1)} %bitcast.11, s32[1]{0:T(128)} %bitcast.6.part_ref, bf16[8,64,1920]{2,1,0:T(8,128)(2,1)S(1)} %copy-done.1, bf16[32,64,320]{2,1,0:T(8,128)(2,1)} %collective-permute-done.3.rest_0_, ...), custom_call_target="tpu_custom_call", output_to_operand_aliasing={{}: (5, {})} | custom-call | flops 755000000 | bytes 20971520 | tf_op jit(solution)/shard_map/pallas_call | solution.py:116
  59.6 0.0 collective-permute-done.7
  59.6 10.8 %collective-permute-done.6.rest_1_ = bf16[40,64,128]{2,1,0:T(8,128)(2,1)} collective-permute-done((bf16[40,64,128]{2,1,0:T(8,128)(2,1)}, bf16[40,64,128]{2,1,0:T(8,128)(2,1)}, u32[]{:S(2)}, u32[]{:S(2)}) %collective-permute-start.6) | collective-permute-done | bytes 655392 | tf_op jit(solution)/shard_map/ppermute | solution.py:236
  70.5 1.2 %broadcast_select_fusion.rest_2_ = bf16[40,64,128]{2,1,0:T(8,128)(2,1)S(1)} fusion(bf16[40,64,128]{2,1,0:T(8,128)(2,1)} %collective-permute-done.4, bf16[40,64,128]{2,1,0:T(8,128)(2,1)} %collective-permute-done.7, pred[]{:T(512)S(6)} %or.3), kind=kLoop, calls=%fused_computation | loop fusion | flops 327680 | bytes 1966081 | tf_op jit(solution)/shard_map/jit(_where)/select_n | solution.py:240
  71.6 0.9 %collective-permute-start.9 = (bf16[40,64,128]{2,1,0:T(8,128)(2,1)S(1)}, bf16[40,64,128]{2,1,0:T(8,128)(2,1)S(1)}, u32[]{:S(2)}, u32[]{:S(2)}) collective-permute-start(bf16[40,64,128]{2,1,0:T(8,128)(2,1)S(1)} %broadcast_select_fusion.rest_2_), channel_id=1, source_target_pairs={{0,1},{1,0},{2,3},{3,2},{4,5},{5,4},{6,7},{7,6},{8,9},{9,8},{10,11... | collective-permute-start | bytes 1966088 | tf_op jit(solution)/shard_map/ppermute | solution.py:241
  72.5 0.3 collective-permute-start.8
  72.8 7.1 %shard_map.59.rest_3_ = bf16[8,64,1536]{2,1,0:T(8,128)(2,1)} custom-call(s32[6144]{0:T(1024)S(1)} %bitcast.12, s32[1]{0:T(128)} %bitcast.8.part_ref, bf16[8,64,1920]{2,1,0:T(8,128)(2,1)S(1)} %copy-done.1, bf16[40,64,128]{2,1,0:T(8,128)(2,1)} %collective-permute-done.rest_0_, ...), custom_call_target="tpu_custom_call", output_to_operand_aliasing={{}: (6, {})} | custom-call | flops 755000000 | bytes 20971520 | tf_op jit(solution)/shard_map/pallas_call | solution.py:116
  79.9 0.0 collective-permute-done.1.rest_0_
  79.9 0.0 collective-permute-done.9.rest_2_
  79.9 0.0 collective-permute-done.8.rest_1_
  79.9 7.1 %shard_map.60 = bf16[8,64,1536]{2,1,0:T(8,128)(2,1)} custom-call(s32[6144]{0:T(1024)S(1)} %bitcast.13, s32[1]{0:T(128)} %bitcast.5.part_ref, bf16[8,64,1920]{2,1,0:T(8,128)(2,1)S(1)} %copy-done.1, bf16[40,64,128]{2,1,0:T(8,128)(2,1)} %collective-permute-done.1.rest_0_, ...), custom_call_target="tpu_custom_call", output_to_operand_aliasing={{}: (6, {})} | custom-call | flops 755000000 | bytes 20971520 | tf_op jit(solution)/shard_map/pallas_call | solution.py:116
  (5 shorter events, 0.0 us)
Async XLA Ops:
  0.0 17.6 %copy-start = (s32[2048,20]{0,1:T(8,128)S(1)}, s32[2048,20]{0,1:T(8,128)}, u32[]{:S(2)}) copy-start(s32[2048,20]{0,1:T(8,128)} %param.8) | copy-start | bytes 491524
  0.0 17.6 %copy-start.2 = (s32[8,30]{1,0:T(8,128)S(1)}, s32[8,30]{1,0:T(8,128)}, u32[]{:S(2)}) copy-start(s32[8,30]{1,0:T(8,128)} %l_ref.5) | copy-start | bytes 2884
  0.0 17.6 %copy-start.3 = (s32[8,24]{1,0:T(8,128)S(1)}, s32[8,24]{1,0:T(8,128)}, u32[]{:S(2)}) copy-start(s32[8,24]{1,0:T(8,128)} %c_ref.1) | copy-start | bytes 2308
  0.0 45.0 %copy-start.1 = (bf16[8,64,1920]{2,1,0:T(8,128)(2,1)S(1)}, bf16[8,64,1920]{2,1,0:T(8,128)(2,1)}, u32[]{:S(2)}) copy-start(bf16[8,64,1920]{2,1,0:T(8,128)(2,1)} %l_ref.9) | copy-start | bytes 5898244
  3.1 49.1 %collective-permute-start.3 = (bf16[32,64,320]{2,1,0:T(8,128)(2,1)}, bf16[32,64,320]{2,1,0:T(8,128)(2,1)}, u32[]{:S(2)}, u32[]{:S(2)}) collective-permute-start(bf16[32,64,320]{2,1,0:T(8,128)(2,1)} %rest_0_.1), channel_id=1, source_target_pairs={{0,1},{1,0},{2,3},{3,2},{4,5},{5,4},{6,7},{7,6},{8,9},{9,8},{10,11... | collective-permute-start | bytes 3932168 | tf_op jit(solution)/shard_map/ppermute | solution.py:226
  3.7 18.2 %collective-permute-start = (bf16[40,64,128]{2,1,0:T(8,128)(2,1)}, bf16[40,64,128]{2,1,0:T(8,128)(2,1)}, u32[]{:S(2)}, u32[]{:S(2)}) collective-permute-start(bf16[40,64,128]{2,1,0:T(8,128)(2,1)} %get-tuple-element.19), channel_id=1, source_target_pairs={{0,2},{1,3},{2,0},{3,1},{4,6},{5,7},{6,4},{7,5},{8,10},{9,11},{10,... | collective-permute-start | bytes 1966088 | tf_op jit(solution)/shard_map/ppermute | solution.py:222
  5.6 37.9 %collective-permute-start.2 = (bf16[40,64,128]{2,1,0:T(8,128)(2,1)}, bf16[40,64,128]{2,1,0:T(8,128)(2,1)S(1)}, u32[]{:S(2)}, u32[]{:S(2)}) collective-permute-start(bf16[40,64,128]{2,1,0:T(8,128)(2,1)} %get-tuple-element.27), channel_id=1, source_target_pairs={{0,4},{1,5},{4,8},{5,9},{8,12},{9,13},{12,16},{13,17},{16,20},{17,... | collective-permute-start | bytes 1966088 | tf_op jit(solution)/shard_map/ppermute | solution.py:219
  9.1 43.1 %collective-permute-start.4 = (bf16[40,64,128]{2,1,0:T(8,128)(2,1)}, bf16[40,64,128]{2,1,0:T(8,128)(2,1)}, u32[]{:S(2)}, u32[]{:S(2)}) collective-permute-start(bf16[40,64,128]{2,1,0:T(8,128)(2,1)} %get-tuple-element.19), channel_id=1, source_target_pairs={{126,128},{127,129},{128,126},{129,127}} | collective-permute-start | bytes 1966088 | tf_op jit(solution)/shard_map/ppermute | solution.py:219
  21.9 37.7 %collective-permute-start.7 = (bf16[40,64,128]{2,1,0:T(8,128)(2,1)}, bf16[40,64,128]{2,1,0:T(8,128)(2,1)}, u32[]{:S(2)}, u32[]{:S(2)}) collective-permute-start(bf16[40,64,128]{2,1,0:T(8,128)(2,1)} %collective-permute-done.rest_0_), channel_id=1, source_target_pairs={{0,4},{1,5},{4,8},{5,9},{8,12},{9,13},{12,16},{13,17},{16,20},{17,... | collective-permute-start | bytes 1966088 | tf_op jit(solution)/shard_map/ppermute | solution.py:219
  43.5 8.9 %collective-permute-start.5 = (bf16[40,64,128]{2,1,0:T(8,128)(2,1)S(1)}, bf16[40,64,128]{2,1,0:T(8,128)(2,1)S(1)}, u32[]{:S(2)}, u32[]{:S(2)}) collective-permute-start(bf16[40,64,128]{2,1,0:T(8,128)(2,1)S(1)} %collective-permute-done.2.rest_1_), channel_id=1, source_target_pairs={{0,1},{1,0},{2,3},{3,2},{4,5},{5,4},{6,7},{7,6},{8,9},{9,8},{10,11... | collective-permute-start | bytes 1966088 | tf_op jit(solution)/shard_map/ppermute | solution.py:232
  52.2 18.3 %collective-permute-start.6 = (bf16[40,64,128]{2,1,0:T(8,128)(2,1)}, bf16[40,64,128]{2,1,0:T(8,128)(2,1)}, u32[]{:S(2)}, u32[]{:S(2)}) collective-permute-start(bf16[40,64,128]{2,1,0:T(8,128)(2,1)} %get-tuple-element.27), channel_id=1, source_target_pairs={{0,2},{1,3},{2,0},{3,1},{4,6},{5,7},{6,4},{7,5},{8,10},{9,11},{10,... | collective-permute-start | bytes 1966088 | tf_op jit(solution)/shard_map/ppermute | solution.py:236
  52.3 27.6 %collective-permute-start.1 = (bf16[40,64,128]{2,1,0:T(8,128)(2,1)}, bf16[40,64,128]{2,1,0:T(8,128)(2,1)}, u32[]{:S(2)}, u32[]{:S(2)}) collective-permute-start(bf16[40,64,128]{2,1,0:T(8,128)(2,1)} %collective-permute-done.rest_0_), channel_id=1, source_target_pairs={{0,1},{1,0},{2,3},{3,2},{4,5},{5,4},{6,7},{7,6},{8,9},{9,8},{10,11... | collective-permute-start | bytes 1966088 | tf_op jit(solution)/shard_map/ppermute | solution.py:230
  71.6 8.3 %collective-permute-start.9 = (bf16[40,64,128]{2,1,0:T(8,128)(2,1)S(1)}, bf16[40,64,128]{2,1,0:T(8,128)(2,1)S(1)}, u32[]{:S(2)}, u32[]{:S(2)}) collective-permute-start(bf16[40,64,128]{2,1,0:T(8,128)(2,1)S(1)} %broadcast_select_fusion.rest_2_), channel_id=1, source_target_pairs={{0,1},{1,0},{2,3},{3,2},{4,5},{5,4},{6,7},{7,6},{8,9},{9,8},{10,11... | collective-permute-start | bytes 1966088 | tf_op jit(solution)/shard_map/ppermute | solution.py:241
  72.5 7.4 %collective-permute-start.8 = (bf16[40,64,128]{2,1,0:T(8,128)(2,1)}, bf16[40,64,128]{2,1,0:T(8,128)(2,1)}, u32[]{:S(2)}, u32[]{:S(2)}) collective-permute-start(bf16[40,64,128]{2,1,0:T(8,128)(2,1)} %collective-permute-done.6.rest_1_), channel_id=1, source_target_pairs={{0,1},{1,0},{2,3},{3,2},{4,5},{5,4},{6,7},{7,6},{8,9},{9,8},{10,11... | collective-permute-start | bytes 1966088 | tf_op jit(solution)/shard_map/ppermute | solution.py:239

commit v9 on v5

--- a/solution.py
+++ b/solution.py
@@ -221,7 +221,6 @@
     first, second = pack(h.reshape(1), s_blocks)
     far_first = across(first)
     halo = send(second, up + down)
-    seam_halo = send(first, seam)
     mate, first = lax.optimization_barrier((s_blocks, first))
     mate = beside(mate)
     tab = table(h, r, l_index, s_cols, c_index)
@@ -229,13 +228,14 @@
     far_second = across(second)
     far_halo = send(far_first, plain)
     cross_first = beside(far_first)
-    halo, far_first = lax.optimization_barrier((halo, far_first))
+    halo, far_first, first = lax.optimization_barrier((halo, far_first, first))
+    seam_halo = send(first, seam)
     mate_halo = beside(halo)
     parts = [(c ^ flip).reshape(1) for flip in range(4)]
     out = product(tab, parts[0], l_blocks, (s_blocks, halo), None)
-    out, mate, seam_halo = lax.optimization_barrier((out, mate, seam_halo))
+    out, mate = lax.optimization_barrier((out, mate))
     out = product(tab, parts[1], l_blocks, (mate, mate_halo), out)
-    out, far_second, far_halo = lax.optimization_barrier((out, far_second, far_halo))
+    out, far_second, far_halo, seam_halo = lax.optimization_barrier((out, far_second, far_halo, seam_halo))
     cross_second = beside(far_second)
     far_halo = jnp.where(takes, seam_halo, far_halo)
     cross_halo = beside(far_halo)

time: 79.7 us -> 81.1 us (1.018)
  the two profiles are of different devices: /device:TPU:7 before, /device:TPU:3 now
where the time goes in v9:
time: 81.1 us; the launch traced here: 80.8 us
  Pallas kernels  32.9 us (41%)
  waiting for transfers between devices  27.6 us (34%)
  starting transfers between devices  18.6 us (23%)
  other arithmetic  1.24 us (2%)
    pallas_call x4, Pallas kernels, product(): pl.pallas_call(functools.partial(product_body, len(pieces)), out_shape=ja...  28.6 us
    ppermute x3, waiting for transfers between devices, send(): return lax.ppermute(x, ('rows', 'cols'), perm)  18.4 us
    ppermute x3, starting transfers between devices, send(): return lax.ppermute(x, ('rows', 'cols'), perm)  11.7 us
    ppermute x1, waiting for transfers between devices, shards(): far_first = across(first)  9.27 us
    pallas_call x1, Pallas kernels, pack(): pl.pallas_call(pack_body, out_shape=(piece, piece), in_specs=[pl.BlockSpe...  3.04 us
    ppermute x1, starting transfers between devices, shards(): far_first = across(first)  1.84 us
  transfers between devices with their start and end apart: 10, of which 3 were waited for; matrix products, arithmetic and copies ran while one was open for 2% of the time, Pallas kernels for 28%

profile of v9, /device:TPU:3, one launch (start us, length us, event | category | flops | bytes accessed | tf_op | source)
XLA Modules:
  0.0 80.8 jit_solution(3515323665753585301)
XLA Ops:
  0.0 0.0 copy-start
  0.0 0.0 copy-start.1
  0.0 3.0 %shard_map.55 = (bf16[40,64,128]{2,1,0:T(8,128)(2,1)}, bf16[40,64,128]{2,1,0:T(8,128)(2,1)}) custom-call(s32[1]{0:T(128)} %bitcast.start_ref, bf16[32,64,320]{2,1,0:T(8,128)(2,1)} %rest_0_.1), custom_call_target="tpu_custom_call" | custom-call | bytes 3145728 | tf_op jit(solution)/shard_map/pallas_call | solution.py:38
  3.1 1.8 %collective-permute-start = (bf16[40,64,128]{2,1,0:T(8,128)(2,1)}, bf16[40,64,128]{2,1,0:T(8,128)(2,1)}, u32[]{:S(2)}, u32[]{:S(2)}) collective-permute-start(bf16[40,64,128]{2,1,0:T(8,128)(2,1)} %get-tuple-element.31), channel_id=1, source_target_pairs={{0,2},{1,3},{2,0},{3,1},{4,6},{5,7},{6,4},{7,5},{8,10},{9,11},{10,... | collective-permute-start | bytes 1966088 | tf_op jit(solution)/shard_map/ppermute | solution.py:222
  4.9 3.5 %collective-permute-start.2 = (bf16[40,64,128]{2,1,0:T(8,128)(2,1)}, bf16[40,64,128]{2,1,0:T(8,128)(2,1)S(1)}, u32[]{:S(2)}, u32[]{:S(2)}) collective-permute-start(bf16[40,64,128]{2,1,0:T(8,128)(2,1)} %get-tuple-element.30), channel_id=1, source_target_pairs={{0,4},{1,5},{4,8},{5,9},{8,12},{9,13},{12,16},{13,17},{16,20},{17,... | collective-permute-start | bytes 1966088 | tf_op jit(solution)/shard_map/ppermute | solution.py:219
  8.5 1.3 %collective-permute-start.3 = (bf16[32,64,320]{2,1,0:T(8,128)(2,1)}, bf16[32,64,320]{2,1,0:T(8,128)(2,1)}, u32[]{:S(2)}, u32[]{:S(2)}) collective-permute-start(bf16[32,64,320]{2,1,0:T(8,128)(2,1)} %rest_0_.1), channel_id=1, source_target_pairs={{0,1},{1,0},{2,3},{3,2},{4,5},{5,4},{6,7},{7,6},{8,9},{9,8},{10,11... | collective-permute-start | bytes 3932168 | tf_op jit(solution)/shard_map/ppermute | solution.py:225
  9.8 0.1 pad_add_fusion.at_ref
  9.9 0.0 copy-done
  9.9 0.1 dynamic-slice_bitcast_fusion.near_ref
  9.9 1.3 %shard_map.56 = s32[48,128]{1,0:T(8,128)S(1)} custom-call(s32[3]{0:T(128)S(1)} %pad_add_fusion.at_ref, s32[20,64]{1,0:T(8,128)S(1)} %dynamic-slice_bitcast_fusion.near_ref, s32[8,30]{1,0:T(8,128)S(1)} %copy-done.2, s32[8,24]{1,0:T(8,128)S(1)} %copy-done.3), custom_call_target="tpu_custom_call" | custom-call | flops 268435456 | bytes 8388608 | tf_op jit(solution)/shard_map/pallas_call | solution.py:193
  11.2 9.3 %collective-permute-done.rest_0_ = bf16[40,64,128]{2,1,0:T(8,128)(2,1)} collective-permute-done((bf16[40,64,128]{2,1,0:T(8,128)(2,1)}, bf16[40,64,128]{2,1,0:T(8,128)(2,1)}, u32[]{:S(2)}, u32[]{:S(2)}) %collective-permute-start) | collective-permute-done | bytes 655392 | tf_op jit(solution)/shard_map/ppermute | solution.py:222
  20.5 9.6 %collective-permute-done.2.rest_1_ = bf16[40,64,128]{2,1,0:T(8,128)(2,1)S(1)} collective-permute-done((bf16[40,64,128]{2,1,0:T(8,128)(2,1)}, bf16[40,64,128]{2,1,0:T(8,128)(2,1)S(1)}, u32[]{:S(2)}, u32[]{:S(2)}) %collective-permute-start.2) | collective-permute-done | bytes 655392 | tf_op jit(solution)/shard_map/ppermute | solution.py:219
  30.1 1.6 %collective-permute-start.4 = (bf16[40,64,128]{2,1,0:T(8,128)(2,1)S(1)}, bf16[40,64,128]{2,1,0:T(8,128)(2,1)S(1)}, u32[]{:S(2)}, u32[]{:S(2)}) collective-permute-start(bf16[40,64,128]{2,1,0:T(8,128)(2,1)S(1)} %collective-permute-done.2.rest_1_), channel_id=1, source_target_pairs={{0,1},{1,0},{2,3},{3,2},{4,5},{5,4},{6,7},{7,6},{8,9},{9,8},{10,11... | collective-permute-start | bytes 1966088 | tf_op jit(solution)/shard_map/ppermute | solution.py:233
  31.7 6.0 %collective-permute-start.7 = (bf16[40,64,128]{2,1,0:T(8,128)(2,1)}, bf16[40,64,128]{2,1,0:T(8,128)(2,1)}, u32[]{:S(2)}, u32[]{:S(2)}) collective-permute-start(bf16[40,64,128]{2,1,0:T(8,128)(2,1)} %get-tuple-element.31), channel_id=1, source_target_pairs={{126,128},{127,129},{128,126},{129,127}} | collective-permute-start | bytes 1966088 | tf_op jit(solution)/shard_map/ppermute | solution.py:219
  37.7 0.1 collective-permute-start.5
  37.8 2.1 %collective-permute-start.6 = (bf16[40,64,128]{2,1,0:T(8,128)(2,1)}, bf16[40,64,128]{2,1,0:T(8,128)(2,1)}, u32[]{:S(2)}, u32[]{:S(2)}) collective-permute-start(bf16[40,64,128]{2,1,0:T(8,128)(2,1)} %collective-permute-done.rest_0_), channel_id=1, source_target_pairs={{0,4},{1,5},{4,8},{5,9},{8,12},{9,13},{12,16},{13,17},{16,20},{17,... | collective-permute-start | bytes 1966088 | tf_op jit(solution)/shard_map/ppermute | solution.py:219
  40.0 7.2 %shard_map.57.rest_2_ = bf16[8,64,1536]{2,1,0:T(8,128)(2,1)} custom-call(s32[6144]{0:T(1024)S(1)} %bitcast.10, s32[1]{0:T(128)} %bitcast.7.part_ref, bf16[8,64,1920]{2,1,0:T(8,128)(2,1)S(1)} %copy-done.1, bf16[32,64,320]{2,1,0:T(8,128)(2,1)} %rest_0_.1, bf16[40,64,128]{2,1,0:T(8,128)(2,1)S(1)} %collective-permute-done.2.rest_1_), custom_call_target="tpu_custom_call" | custom-call | flops 755000000 | bytes 20971520 | tf_op jit(solution)/shard_map/pallas_call | solution.py:116
  47.2 0.0 collective-permute-done.3.rest_0_
  47.2 0.4 collective-permute-start.1
  47.5 0.0 collective-permute-done.4.rest_1_
  47.5 7.2 %shard_map.58.rest_3_ = bf16[8,64,1536]{2,1,0:T(8,128)(2,1)} custom-call(s32[6144]{0:T(1024)S(1)} %bitcast.11, s32[1]{0:T(128)} %bitcast.6.part_ref, bf16[8,64,1920]{2,1,0:T(8,128)(2,1)S(1)} %copy-done.1, bf16[32,64,320]{2,1,0:T(8,128)(2,1)} %collective-permute-done.3.rest_0_, ...), custom_call_target="tpu_custom_call", output_to_operand_aliasing={{}: (5, {})} | custom-call | flops 755000000 | bytes 20971520 | tf_op jit(solution)/shard_map/pallas_call | solution.py:116
  54.7 8.8 %collective-permute-done.7 = bf16[40,64,128]{2,1,0:T(8,128)(2,1)} collective-permute-done((bf16[40,64,128]{2,1,0:T(8,128)(2,1)}, bf16[40,64,128]{2,1,0:T(8,128)(2,1)}, u32[]{:S(2)}, u32[]{:S(2)}) %collective-permute-start.7) | collective-permute-done | bytes 655392 | tf_op jit(solution)/shard_map/ppermute | solution.py:219
  63.5 0.0 collective-permute-done.5.rest_1_
  63.5 0.0 collective-permute-done.6
  63.5 1.2 %broadcast_select_fusion.rest_2_ = bf16[40,64,128]{2,1,0:T(8,128)(2,1)S(1)} fusion(bf16[40,64,128]{2,1,0:T(8,128)(2,1)} %collective-permute-done.7, bf16[40,64,128]{2,1,0:T(8,128)(2,1)} %collective-permute-done.6, pred[]{:T(512)S(6)} %or.3), kind=kLoop, calls=%fused_computation | loop fusion | flops 327680 | bytes 1966081 | tf_op jit(solution)/shard_map/jit(_where)/select_n | solution.py:240
  64.6 1.4 %collective-permute-start.9 = (bf16[40,64,128]{2,1,0:T(8,128)(2,1)S(1)}, bf16[40,64,128]{2,1,0:T(8,128)(2,1)S(1)}, u32[]{:S(2)}, u32[]{:S(2)}) collective-permute-start(bf16[40,64,128]{2,1,0:T(8,128)(2,1)S(1)} %broadcast_select_fusion.rest_2_), channel_id=1, source_target_pairs={{0,1},{1,0},{2,3},{3,2},{4,5},{5,4},{6,7},{7,6},{8,9},{9,8},{10,11... | collective-permute-start | bytes 1966088 | tf_op jit(solution)/shard_map/ppermute | solution.py:241
  66.1 0.3 collective-permute-start.8
  66.4 7.1 %shard_map.59.rest_3_ = bf16[8,64,1536]{2,1,0:T(8,128)(2,1)} custom-call(s32[6144]{0:T(1024)S(1)} %bitcast.12, s32[1]{0:T(128)} %bitcast.8.part_ref, bf16[8,64,1920]{2,1,0:T(8,128)(2,1)S(1)} %copy-done.1, bf16[40,64,128]{2,1,0:T(8,128)(2,1)} %collective-permute-done.rest_0_, ...), custom_call_target="tpu_custom_call", output_to_operand_aliasing={{}: (6, {})} | custom-call | flops 755000000 | bytes 20971520 | tf_op jit(solution)/shard_map/pallas_call | solution.py:116
  73.5 0.0 collective-permute-done.1.rest_0_
  73.5 0.0 collective-permute-done.9.rest_2_
  73.5 0.0 collective-permute-done.8.rest_1_
  73.5 7.1 %shard_map.60 = bf16[8,64,1536]{2,1,0:T(8,128)(2,1)} custom-call(s32[6144]{0:T(1024)S(1)} %bitcast.13, s32[1]{0:T(128)} %bitcast.5.part_ref, bf16[8,64,1920]{2,1,0:T(8,128)(2,1)S(1)} %copy-done.1, bf16[40,64,128]{2,1,0:T(8,128)(2,1)} %collective-permute-done.1.rest_0_, ...), custom_call_target="tpu_custom_call", output_to_operand_aliasing={{}: (6, {})} | custom-call | flops 755000000 | bytes 20971520 | tf_op jit(solution)/shard_map/pallas_call | solution.py:116
  (5 shorter events, 0.0 us)
Async XLA Ops:
  0.0 9.9 %copy-start = (s32[2048,20]{0,1:T(8,128)S(1)}, s32[2048,20]{0,1:T(8,128)}, u32[]{:S(2)}) copy-start(s32[2048,20]{0,1:T(8,128)} %param.8) | copy-start | bytes 491524
  0.0 9.9 %copy-start.2 = (s32[8,30]{1,0:T(8,128)S(1)}, s32[8,30]{1,0:T(8,128)}, u32[]{:S(2)}) copy-start(s32[8,30]{1,0:T(8,128)} %l_ref.5) | copy-start | bytes 2884
  0.0 9.9 %copy-start.3 = (s32[8,24]{1,0:T(8,128)S(1)}, s32[8,24]{1,0:T(8,128)}, u32[]{:S(2)}) copy-start(s32[8,24]{1,0:T(8,128)} %c_ref.1) | copy-start | bytes 2308
  0.0 40.0 %copy-start.1 = (bf16[8,64,1920]{2,1,0:T(8,128)(2,1)S(1)}, bf16[8,64,1920]{2,1,0:T(8,128)(2,1)}, u32[]{:S(2)}) copy-start(bf16[8,64,1920]{2,1,0:T(8,128)(2,1)} %l_ref.9) | copy-start | bytes 5898244
  3.1 17.4 %collective-permute-start = (bf16[40,64,128]{2,1,0:T(8,128)(2,1)}, bf16[40,64,128]{2,1,0:T(8,128)(2,1)}, u32[]{:S(2)}, u32[]{:S(2)}) collective-permute-start(bf16[40,64,128]{2,1,0:T(8,128)(2,1)} %get-tuple-element.31), channel_id=1, source_target_pairs={{0,2},{1,3},{2,0},{3,1},{4,6},{5,7},{6,4},{7,5},{8,10},{9,11},{10,... | collective-permute-start | bytes 1966088 | tf_op jit(solution)/shard_map/ppermute | solution.py:222
  4.9 25.2 %collective-permute-start.2 = (bf16[40,64,128]{2,1,0:T(8,128)(2,1)}, bf16[40,64,128]{2,1,0:T(8,128)(2,1)S(1)}, u32[]{:S(2)}, u32[]{:S(2)}) collective-permute-start(bf16[40,64,128]{2,1,0:T(8,128)(2,1)} %get-tuple-element.30), channel_id=1, source_target_pairs={{0,4},{1,5},{4,8},{5,9},{8,12},{9,13},{12,16},{13,17},{16,20},{17,... | collective-permute-start | bytes 1966088 | tf_op jit(solution)/shard_map/ppermute | solution.py:219
  8.5 38.7 %collective-permute-start.3 = (bf16[32,64,320]{2,1,0:T(8,128)(2,1)}, bf16[32,64,320]{2,1,0:T(8,128)(2,1)}, u32[]{:S(2)}, u32[]{:S(2)}) collective-permute-start(bf16[32,64,320]{2,1,0:T(8,128)(2,1)} %rest_0_.1), channel_id=1, source_target_pairs={{0,1},{1,0},{2,3},{3,2},{4,5},{5,4},{6,7},{7,6},{8,9},{9,8},{10,11... | collective-permute-start | bytes 3932168 | tf_op jit(solution)/shard_map/ppermute | solution.py:225
  30.1 17.4 %collective-permute-start.4 = (bf16[40,64,128]{2,1,0:T(8,128)(2,1)S(1)}, bf16[40,64,128]{2,1,0:T(8,128)(2,1)S(1)}, u32[]{:S(2)}, u32[]{:S(2)}) collective-permute-start(bf16[40,64,128]{2,1,0:T(8,128)(2,1)S(1)} %collective-permute-done.2.rest_1_), channel_id=1, source_target_pairs={{0,1},{1,0},{2,3},{3,2},{4,5},{5,4},{6,7},{7,6},{8,9},{9,8},{10,11... | collective-permute-start | bytes 1966088 | tf_op jit(solution)/shard_map/ppermute | solution.py:233
  31.7 31.8 %collective-permute-start.7 = (bf16[40,64,128]{2,1,0:T(8,128)(2,1)}, bf16[40,64,128]{2,1,0:T(8,128)(2,1)}, u32[]{:S(2)}, u32[]{:S(2)}) collective-permute-start(bf16[40,64,128]{2,1,0:T(8,128)(2,1)} %get-tuple-element.31), channel_id=1, source_target_pairs={{126,128},{127,129},{128,126},{129,127}} | collective-permute-start | bytes 1966088 | tf_op jit(solution)/shard_map/ppermute | solution.py:219
  37.7 25.7 %collective-permute-start.5 = (bf16[40,64,128]{2,1,0:T(8,128)(2,1)}, bf16[40,64,128]{2,1,0:T(8,128)(2,1)}, u32[]{:S(2)}, u32[]{:S(2)}) collective-permute-start(bf16[40,64,128]{2,1,0:T(8,128)(2,1)} %get-tuple-element.30), channel_id=1, source_target_pairs={{0,2},{1,3},{2,0},{3,1},{4,6},{5,7},{6,4},{7,5},{8,10},{9,11},{10,... | collective-permute-start | bytes 1966088 | tf_op jit(solution)/shard_map/ppermute | solution.py:228
  37.8 25.6 %collective-permute-start.6 = (bf16[40,64,128]{2,1,0:T(8,128)(2,1)}, bf16[40,64,128]{2,1,0:T(8,128)(2,1)}, u32[]{:S(2)}, u32[]{:S(2)}) collective-permute-start(bf16[40,64,128]{2,1,0:T(8,128)(2,1)} %collective-permute-done.rest_0_), channel_id=1, source_target_pairs={{0,4},{1,5},{4,8},{5,9},{8,12},{9,13},{12,16},{13,17},{16,20},{17,... | collective-permute-start | bytes 1966088 | tf_op jit(solution)/shard_map/ppermute | solution.py:219
  47.2 26.3 %collective-permute-start.1 = (bf16[40,64,128]{2,1,0:T(8,128)(2,1)}, bf16[40,64,128]{2,1,0:T(8,128)(2,1)}, u32[]{:S(2)}, u32[]{:S(2)}) collective-permute-start(bf16[40,64,128]{2,1,0:T(8,128)(2,1)} %collective-permute-done.rest_0_), channel_id=1, source_target_pairs={{0,1},{1,0},{2,3},{3,2},{4,5},{5,4},{6,7},{7,6},{8,9},{9,8},{10,11... | collective-permute-start | bytes 1966088 | tf_op jit(solution)/shard_map/ppermute | solution.py:230
  64.6 8.9 %collective-permute-start.9 = (bf16[40,64,128]{2,1,0:T(8,128)(2,1)S(1)}, bf16[40,64,128]{2,1,0:T(8,128)(2,1)S(1)}, u32[]{:S(2)}, u32[]{:S(2)}) collective-permute-start(bf16[40,64,128]{2,1,0:T(8,128)(2,1)S(1)} %broadcast_select_fusion.rest_2_), channel_id=1, source_target_pairs={{0,1},{1,0},{2,3},{3,2},{4,5},{5,4},{6,7},{7,6},{8,9},{9,8},{10,11... | collective-permute-start | bytes 1966088 | tf_op jit(solution)/shard_map/ppermute | solution.py:241
  66.1 7.4 %collective-permute-start.8 = (bf16[40,64,128]{2,1,0:T(8,128)(2,1)}, bf16[40,64,128]{2,1,0:T(8,128)(2,1)}, u32[]{:S(2)}, u32[]{:S(2)}) collective-permute-start(bf16[40,64,128]{2,1,0:T(8,128)(2,1)} %collective-permute-done.5.rest_1_), channel_id=1, source_target_pairs={{0,1},{1,0},{2,3},{3,2},{4,5},{5,4},{6,7},{7,6},{8,9},{9,8},{10,11... | collective-permute-start | bytes 1966088 | tf_op jit(solution)/shard_map/ppermute | solution.py:239

commit v10 on v4

--- a/solution.py
+++ b/solution.py
@@ -231,11 +231,11 @@
     far_halo = send(far_first, plain)
     cross_first = beside(far_first)
     mate_halo = beside(halo)
-    tab, far_first, seam_halo = lax.optimization_barrier((tab, far_first, seam_halo))
+    tab, far_first = lax.optimization_barrier((tab, far_first))
     parts = [(c ^ flip).reshape(1) for flip in range(4)]
     out = product(tab, parts[0], l_blocks, (s_blocks, halo), None)
     out = product(tab, parts[1], l_blocks, (mate, mate_halo), out)
-    out, far_second, far_halo = lax.optimization_barrier((out, far_second, far_halo))
+    out, far_second, far_halo, seam_halo = lax.optimization_barrier((out, far_second, far_halo, seam_halo))
     cross_second = beside(far_second)
     far_halo = jnp.where(takes, seam_halo, far_halo)
     cross_halo = beside(far_halo)

time: 80.4 us -> 79.3 us (0.986)
  waiting for transfers between devices: 18.7 us -> 17.6 us
    ppermute x3, starting transfers between devices: 7.59 us -> 14.2 us  [send(): return lax.ppermute(x, ('rows', 'cols'), perm)]
    ppermute x1, starting transfers between devices: 4.89 us -> 0.09 us  [shards(): far_second = across(second)]
    ppermute x1, starting transfers between devices: 2.02 us -> 0.37 us  [shards(): cross_first = beside(far_first)]
    ppermute x3, waiting for transfers between devices: 18.7 us -> 17.6 us  [send(): return lax.ppermute(x, ('rows', 'cols'), perm)]
    ppermute x1, starting transfers between devices: 0.09 us -> 1.1 us  [shards(): cross_halo = beside(far_halo)]
    ppermute x1, starting transfers between devices: 2.21 us -> 1.29 us  [shards(): mate_halo = beside(halo)]
  transfers between devices with their start and end apart: 10 -> 10, of which waited for: 2 -> 2; matrix products, arithmetic and copies ran while one was open for 2% -> 2% of each run, Pallas kernels for 28% -> 29%
where the time goes in v10:
time: 79.3 us; the launch traced here: 79 us
  Pallas kernels  32.9 us (41%)
  starting transfers between devices  26.9 us (34%)
  waiting for transfers between devices  17.6 us (22%)
  other arithmetic  1.24 us (2%)
    pallas_call x4, Pallas kernels, product(): pl.pallas_call(functools.partial(product_body, len(pieces)), out_shape=ja...  28.6 us
    ppermute x3, waiting for transfers between devices, send(): return lax.ppermute(x, ('rows', 'cols'), perm)  17.6 us
    ppermute x3, starting transfers between devices, send(): return lax.ppermute(x, ('rows', 'cols'), perm)  14.2 us
    ppermute x1, starting transfers between devices, shards(): far_first = across(first)  8.52 us
    pallas_call x1, Pallas kernels, pack(): pl.pallas_call(pack_body, out_shape=(piece, piece), in_specs=[pl.BlockSpe...  3.04 us
  transfers between devices with their start and end apart: 10, of which 2 were waited for; matrix products, arithmetic and copies ran while one was open for 2% of the time, Pallas kernels for 29%

profile of v10, /device:TPU:3, one launch (start us, length us, event | category | flops | bytes accessed | tf_op | source)
XLA Modules:
  0.0 79.0 jit_solution(2355714076706491316)
XLA Ops:
  0.0 0.0 copy-start
  0.0 0.0 copy-start.1
  0.0 3.0 %shard_map.55 = (bf16[40,64,128]{2,1,0:T(8,128)(2,1)}, bf16[40,64,128]{2,1,0:T(8,128)(2,1)}) custom-call(s32[1]{0:T(128)} %bitcast.start_ref, bf16[32,64,320]{2,1,0:T(8,128)(2,1)} %rest_0_.1), custom_call_target="tpu_custom_call" | custom-call | bytes 3145728 | tf_op jit(solution)/shard_map/pallas_call | solution.py:38
  3.1 3.5 %collective-permute-start = (bf16[40,64,128]{2,1,0:T(8,128)(2,1)}, bf16[40,64,128]{2,1,0:T(8,128)(2,1)S(1)}, u32[]{:S(2)}, u32[]{:S(2)}) collective-permute-start(bf16[40,64,128]{2,1,0:T(8,128)(2,1)} %get-tuple-element.23), channel_id=1, source_target_pairs={{0,4},{1,5},{4,8},{5,9},{8,12},{9,13},{12,16},{13,17},{16,20},{17,... | collective-permute-start | bytes 1966088 | tf_op jit(solution)/shard_map/ppermute | solution.py:219
  6.6 1.0 %collective-permute-start.3 = (bf16[32,64,320]{2,1,0:T(8,128)(2,1)}, bf16[32,64,320]{2,1,0:T(8,128)(2,1)}, u32[]{:S(2)}, u32[]{:S(2)}) collective-permute-start(bf16[32,64,320]{2,1,0:T(8,128)(2,1)} %rest_0_.1), channel_id=1, source_target_pairs={{0,1},{1,0},{2,3},{3,2},{4,5},{5,4},{6,7},{7,6},{8,9},{9,8},{10,11... | collective-permute-start | bytes 3932168 | tf_op jit(solution)/shard_map/ppermute | solution.py:226
  7.7 8.5 %collective-permute-start.1 = (bf16[40,64,128]{2,1,0:T(8,128)(2,1)}, bf16[40,64,128]{2,1,0:T(8,128)(2,1)}, u32[]{:S(2)}, u32[]{:S(2)}) collective-permute-start(bf16[40,64,128]{2,1,0:T(8,128)(2,1)} %get-tuple-element.19), channel_id=1, source_target_pairs={{0,2},{1,3},{2,0},{3,1},{4,6},{5,7},{6,4},{7,5},{8,10},{9,11},{10,... | collective-permute-start | bytes 1966088 | tf_op jit(solution)/shard_map/ppermute | solution.py:222
  16.2 0.1 pad_add_fusion.at_ref
  16.3 0.1 dynamic-slice_bitcast_fusion.near_ref
  16.3 0.0 copy-done.2
  16.3 1.3 %shard_map.56 = s32[48,128]{1,0:T(8,128)S(1)} custom-call(s32[3]{0:T(128)S(1)} %pad_add_fusion.at_ref, s32[20,64]{1,0:T(8,128)S(1)} %dynamic-slice_bitcast_fusion.near_ref, s32[8,30]{1,0:T(8,128)S(1)} %copy-done.2, s32[8,24]{1,0:T(8,128)S(1)} %copy-done.3), custom_call_target="tpu_custom_call" | custom-call | flops 268435456 | bytes 8388608 | tf_op jit(solution)/shard_map/pallas_call | solution.py:193
  17.6 10.0 %collective-permute-done.rest_1_ = bf16[40,64,128]{2,1,0:T(8,128)(2,1)S(1)} collective-permute-done((bf16[40,64,128]{2,1,0:T(8,128)(2,1)}, bf16[40,64,128]{2,1,0:T(8,128)(2,1)S(1)}, u32[]{:S(2)}, u32[]{:S(2)}) %collective-permute-start) | collective-permute-done | bytes 655392 | tf_op jit(solution)/shard_map/ppermute | solution.py:219
  27.7 1.3 %collective-permute-start.4 = (bf16[40,64,128]{2,1,0:T(8,128)(2,1)S(1)}, bf16[40,64,128]{2,1,0:T(8,128)(2,1)S(1)}, u32[]{:S(2)}, u32[]{:S(2)}) collective-permute-start(bf16[40,64,128]{2,1,0:T(8,128)(2,1)S(1)} %collective-permute-done.rest_1_), channel_id=1, source_target_pairs={{0,1},{1,0},{2,3},{3,2},{4,5},{5,4},{6,7},{7,6},{8,9},{9,8},{10,11... | collective-permute-start | bytes 1966088 | tf_op jit(solution)/shard_map/ppermute | solution.py:233
  29.0 8.5 %collective-permute-start.7 = (bf16[40,64,128]{2,1,0:T(8,128)(2,1)}, bf16[40,64,128]{2,1,0:T(8,128)(2,1)}, u32[]{:S(2)}, u32[]{:S(2)}) collective-permute-start(bf16[40,64,128]{2,1,0:T(8,128)(2,1)} %get-tuple-element.19), channel_id=1, source_target_pairs={{126,128},{127,129},{128,126},{129,127}} | collective-permute-start | bytes 1966088 | tf_op jit(solution)/shard_map/ppermute | solution.py:219
  37.5 0.1 collective-permute-start.5
  37.6 0.0 collective-permute-done.1.rest_0_
  37.6 2.1 %collective-permute-start.6 = (bf16[40,64,128]{2,1,0:T(8,128)(2,1)}, bf16[40,64,128]{2,1,0:T(8,128)(2,1)}, u32[]{:S(2)}, u32[]{:S(2)}) collective-permute-start(bf16[40,64,128]{2,1,0:T(8,128)(2,1)} %collective-permute-done.1.rest_0_), channel_id=1, source_target_pairs={{0,4},{1,5},{4,8},{5,9},{8,12},{9,13},{12,16},{13,17},{16,20},{17,... | collective-permute-start | bytes 1966088 | tf_op jit(solution)/shard_map/ppermute | solution.py:219
  39.8 7.2 %shard_map.57.rest_2_ = bf16[8,64,1536]{2,1,0:T(8,128)(2,1)} custom-call(s32[6144]{0:T(1024)S(1)} %bitcast.10, s32[1]{0:T(128)} %bitcast.7.part_ref, bf16[8,64,1920]{2,1,0:T(8,128)(2,1)S(1)} %copy-done.1, bf16[32,64,320]{2,1,0:T(8,128)(2,1)} %rest_0_.1, bf16[40,64,128]{2,1,0:T(8,128)(2,1)S(1)} %collective-permute-done.rest_1_), custom_call_target="tpu_custom_call" | custom-call | flops 755000000 | bytes 20971520 | tf_op jit(solution)/shard_map/pallas_call | solution.py:116
  46.9 0.0 collective-permute-done.3.rest_0_
  46.9 0.4 collective-permute-start.2
  47.3 0.0 collective-permute-done.4.rest_1_
  47.3 7.2 %shard_map.58.rest_3_ = bf16[8,64,1536]{2,1,0:T(8,128)(2,1)} custom-call(s32[6144]{0:T(1024)S(1)} %bitcast.11, s32[1]{0:T(128)} %bitcast.6.part_ref, bf16[8,64,1920]{2,1,0:T(8,128)(2,1)S(1)} %copy-done.1, bf16[32,64,320]{2,1,0:T(8,128)(2,1)} %collective-permute-done.3.rest_0_, ...), custom_call_target="tpu_custom_call", output_to_operand_aliasing={{}: (5, {})} | custom-call | flops 755000000 | bytes 20971520 | tf_op jit(solution)/shard_map/pallas_call | solution.py:116
  54.5 7.5 %collective-permute-done.7 = bf16[40,64,128]{2,1,0:T(8,128)(2,1)} collective-permute-done((bf16[40,64,128]{2,1,0:T(8,128)(2,1)}, bf16[40,64,128]{2,1,0:T(8,128)(2,1)}, u32[]{:S(2)}, u32[]{:S(2)}) %collective-permute-start.7) | collective-permute-done | bytes 655392 | tf_op jit(solution)/shard_map/ppermute | solution.py:219
  62.0 0.0 collective-permute-done.5.rest_1_
  62.0 0.0 collective-permute-done.6
  62.0 1.2 %broadcast_select_fusion.rest_2_ = bf16[40,64,128]{2,1,0:T(8,128)(2,1)S(1)} fusion(bf16[40,64,128]{2,1,0:T(8,128)(2,1)} %collective-permute-done.7, bf16[40,64,128]{2,1,0:T(8,128)(2,1)} %collective-permute-done.6, pred[]{:T(512)S(6)} %or.3), kind=kLoop, calls=%fused_computation | loop fusion | flops 327680 | bytes 1966081 | tf_op jit(solution)/shard_map/jit(_where)/select_n | solution.py:240
  63.2 1.1 %collective-permute-start.9 = (bf16[40,64,128]{2,1,0:T(8,128)(2,1)S(1)}, bf16[40,64,128]{2,1,0:T(8,128)(2,1)S(1)}, u32[]{:S(2)}, u32[]{:S(2)}) collective-permute-start(bf16[40,64,128]{2,1,0:T(8,128)(2,1)S(1)} %broadcast_select_fusion.rest_2_), channel_id=1, source_target_pairs={{0,1},{1,0},{2,3},{3,2},{4,5},{5,4},{6,7},{7,6},{8,9},{9,8},{10,11... | collective-permute-start | bytes 1966088 | tf_op jit(solution)/shard_map/ppermute | solution.py:241
  64.3 0.3 collective-permute-start.8
  64.6 7.1 %shard_map.59.rest_3_ = bf16[8,64,1536]{2,1,0:T(8,128)(2,1)} custom-call(s32[6144]{0:T(1024)S(1)} %bitcast.12, s32[1]{0:T(128)} %bitcast.8.part_ref, bf16[8,64,1920]{2,1,0:T(8,128)(2,1)S(1)} %copy-done.1, bf16[40,64,128]{2,1,0:T(8,128)(2,1)} %collective-permute-done.1.rest_0_, ...), custom_call_target="tpu_custom_call", output_to_operand_aliasing={{}: (6, {})} | custom-call | flops 755000000 | bytes 20971520 | tf_op jit(solution)/shard_map/pallas_call | solution.py:116
  71.7 0.0 collective-permute-done.2.rest_0_
  71.7 0.0 collective-permute-done.9.rest_2_
  71.7 0.0 collective-permute-done.8.rest_1_
  71.7 7.1 %shard_map.60 = bf16[8,64,1536]{2,1,0:T(8,128)(2,1)} custom-call(s32[6144]{0:T(1024)S(1)} %bitcast.13, s32[1]{0:T(128)} %bitcast.5.part_ref, bf16[8,64,1920]{2,1,0:T(8,128)(2,1)S(1)} %copy-done.1, bf16[40,64,128]{2,1,0:T(8,128)(2,1)} %collective-permute-done.2.rest_0_, ...), custom_call_target="tpu_custom_call", output_to_operand_aliasing={{}: (6, {})} | custom-call | flops 755000000 | bytes 20971520 | tf_op jit(solution)/shard_map/pallas_call | solution.py:116
  (5 shorter events, 0.0 us)
Async XLA Ops:
  0.0 16.3 %copy-start = (s32[2048,20]{0,1:T(8,128)S(1)}, s32[2048,20]{0,1:T(8,128)}, u32[]{:S(2)}) copy-start(s32[2048,20]{0,1:T(8,128)} %param.8) | copy-start | bytes 491524
  0.0 16.3 %copy-start.2 = (s32[8,30]{1,0:T(8,128)S(1)}, s32[8,30]{1,0:T(8,128)}, u32[]{:S(2)}) copy-start(s32[8,30]{1,0:T(8,128)} %l_ref.5) | copy-start | bytes 2884
  0.0 16.3 %copy-start.3 = (s32[8,24]{1,0:T(8,128)S(1)}, s32[8,24]{1,0:T(8,128)}, u32[]{:S(2)}) copy-start(s32[8,24]{1,0:T(8,128)} %c_ref.1) | copy-start | bytes 2308
  0.0 39.7 %copy-start.1 = (bf16[8,64,1920]{2,1,0:T(8,128)(2,1)S(1)}, bf16[8,64,1920]{2,1,0:T(8,128)(2,1)}, u32[]{:S(2)}) copy-start(bf16[8,64,1920]{2,1,0:T(8,128)(2,1)} %l_ref.9) | copy-start | bytes 5898244
  3.1 24.6 %collective-permute-start = (bf16[40,64,128]{2,1,0:T(8,128)(2,1)}, bf16[40,64,128]{2,1,0:T(8,128)(2,1)S(1)}, u32[]{:S(2)}, u32[]{:S(2)}) collective-permute-start(bf16[40,64,128]{2,1,0:T(8,128)(2,1)} %get-tuple-element.23), channel_id=1, source_target_pairs={{0,4},{1,5},{4,8},{5,9},{8,12},{9,13},{12,16},{13,17},{16,20},{17,... | collective-permute-start | bytes 1966088 | tf_op jit(solution)/shard_map/ppermute | solution.py:219
  6.6 40.3 %collective-permute-start.3 = (bf16[32,64,320]{2,1,0:T(8,128)(2,1)}, bf16[32,64,320]{2,1,0:T(8,128)(2,1)}, u32[]{:S(2)}, u32[]{:S(2)}) collective-permute-start(bf16[32,64,320]{2,1,0:T(8,128)(2,1)} %rest_0_.1), channel_id=1, source_target_pairs={{0,1},{1,0},{2,3},{3,2},{4,5},{5,4},{6,7},{7,6},{8,9},{9,8},{10,11... | collective-permute-start | bytes 3932168 | tf_op jit(solution)/shard_map/ppermute | solution.py:226
  7.7 29.9 %collective-permute-start.1 = (bf16[40,64,128]{2,1,0:T(8,128)(2,1)}, bf16[40,64,128]{2,1,0:T(8,128)(2,1)}, u32[]{:S(2)}, u32[]{:S(2)}) collective-permute-start(bf16[40,64,128]{2,1,0:T(8,128)(2,1)} %get-tuple-element.19), channel_id=1, source_target_pairs={{0,2},{1,3},{2,0},{3,1},{4,6},{5,7},{6,4},{7,5},{8,10},{9,11},{10,... | collective-permute-start | bytes 1966088 | tf_op jit(solution)/shard_map/ppermute | solution.py:222
  27.7 19.6 %collective-permute-start.4 = (bf16[40,64,128]{2,1,0:T(8,128)(2,1)S(1)}, bf16[40,64,128]{2,1,0:T(8,128)(2,1)S(1)}, u32[]{:S(2)}, u32[]{:S(2)}) collective-permute-start(bf16[40,64,128]{2,1,0:T(8,128)(2,1)S(1)} %collective-permute-done.rest_1_), channel_id=1, source_target_pairs={{0,1},{1,0},{2,3},{3,2},{4,5},{5,4},{6,7},{7,6},{8,9},{9,8},{10,11... | collective-permute-start | bytes 1966088 | tf_op jit(solution)/shard_map/ppermute | solution.py:233
  29.0 33.1 %collective-permute-start.7 = (bf16[40,64,128]{2,1,0:T(8,128)(2,1)}, bf16[40,64,128]{2,1,0:T(8,128)(2,1)}, u32[]{:S(2)}, u32[]{:S(2)}) collective-permute-start(bf16[40,64,128]{2,1,0:T(8,128)(2,1)} %get-tuple-element.19), channel_id=1, source_target_pairs={{126,128},{127,129},{128,126},{129,127}} | collective-permute-start | bytes 1966088 | tf_op jit(solution)/shard_map/ppermute | solution.py:219
  37.5 24.5 %collective-permute-start.5 = (bf16[40,64,128]{2,1,0:T(8,128)(2,1)}, bf16[40,64,128]{2,1,0:T(8,128)(2,1)}, u32[]{:S(2)}, u32[]{:S(2)}) collective-permute-start(bf16[40,64,128]{2,1,0:T(8,128)(2,1)} %get-tuple-element.23), channel_id=1, source_target_pairs={{0,2},{1,3},{2,0},{3,1},{4,6},{5,7},{6,4},{7,5},{8,10},{9,11},{10,... | collective-permute-start | bytes 1966088 | tf_op jit(solution)/shard_map/ppermute | solution.py:229
  37.6 24.4 %collective-permute-start.6 = (bf16[40,64,128]{2,1,0:T(8,128)(2,1)}, bf16[40,64,128]{2,1,0:T(8,128)(2,1)}, u32[]{:S(2)}, u32[]{:S(2)}) collective-permute-start(bf16[40,64,128]{2,1,0:T(8,128)(2,1)} %collective-permute-done.1.rest_0_), channel_id=1, source_target_pairs={{0,4},{1,5},{4,8},{5,9},{8,12},{9,13},{12,16},{13,17},{16,20},{17,... | collective-permute-start | bytes 1966088 | tf_op jit(solution)/shard_map/ppermute | solution.py:219
  46.9 24.7 %collective-permute-start.2 = (bf16[40,64,128]{2,1,0:T(8,128)(2,1)}, bf16[40,64,128]{2,1,0:T(8,128)(2,1)}, u32[]{:S(2)}, u32[]{:S(2)}) collective-permute-start(bf16[40,64,128]{2,1,0:T(8,128)(2,1)} %collective-permute-done.1.rest_0_), channel_id=1, source_target_pairs={{0,1},{1,0},{2,3},{3,2},{4,5},{5,4},{6,7},{7,6},{8,9},{9,8},{10,11... | collective-permute-start | bytes 1966088 | tf_op jit(solution)/shard_map/ppermute | solution.py:232
  63.2 8.5 %collective-permute-start.9 = (bf16[40,64,128]{2,1,0:T(8,128)(2,1)S(1)}, bf16[40,64,128]{2,1,0:T(8,128)(2,1)S(1)}, u32[]{:S(2)}, u32[]{:S(2)}) collective-permute-start(bf16[40,64,128]{2,1,0:T(8,128)(2,1)S(1)} %broadcast_select_fusion.rest_2_), channel_id=1, source_target_pairs={{0,1},{1,0},{2,3},{3,2},{4,5},{5,4},{6,7},{7,6},{8,9},{9,8},{10,11... | collective-permute-start | bytes 1966088 | tf_op jit(solution)/shard_map/ppermute | solution.py:241
  64.3 7.4 %collective-permute-start.8 = (bf16[40,64,128]{2,1,0:T(8,128)(2,1)}, bf16[40,64,128]{2,1,0:T(8,128)(2,1)}, u32[]{:S(2)}, u32[]{:S(2)}) collective-permute-start(bf16[40,64,128]{2,1,0:T(8,128)(2,1)} %collective-permute-done.5.rest_1_), channel_id=1, source_target_pairs={{0,1},{1,0},{2,3},{3,2},{4,5},{5,4},{6,7},{7,6},{8,9},{9,8},{10,11... | collective-permute-start | bytes 1966088 | tf_op jit(solution)/shard_map/ppermute | solution.py:239
